TPU v7x, 32 devices: a whole 2x2x4 slice. The times are simulated.
32 devices in a mesh: grp: 2 (over x), seq: 16 (over z, y, core).
Axes of the slice: x: 2, y: 2, z: 4, core: 2. Of those that a mesh axis runs over, the one named last changes fastest.
Arguments:
- fast_state: bfloat16 [32, 3, 1024, 512], P(('grp', 'seq')), parts along dimension 0, may hold values from -0.25 to 0.25
- initial_fast: bfloat16 [3, 1024, 512], P(None, 'seq'), may hold values from -0.25 to 0.25
- queries: bfloat16 [32, 4, 384, 512], P(('grp', 'seq')), parts along dimension 0, may hold values from -6 to 6
- token_keys: bfloat16 [32, 4, 384, 512], P(('grp', 'seq')), parts along dimension 0, may hold values from -6 to 6
- token_values: bfloat16 [32, 4, 384, 512], P(('grp', 'seq')), parts along dimension 0, may hold values from -6 to 6
- step_sizes: bfloat16 [32, 4, 384], P(('grp', 'seq')), parts along dimension 0, may hold values from 0.0019989014 to 0.019897461
Outputs:
- layer_output: bfloat16 [32, 4, 384, 512], P(('grp', 'seq')), parts along dimension 0
There are 2 independent parts, one for each index of `grp`. A program takes and returns all parts, laid end to end along the dimension named above; an argument that names none is the same for every part. Nothing has to cross between parts.
All inputs are finite; a program needn't handle non-finite values.
Results may differ from a plain program's by a relative error of at most 0.012.
The roundings to bfloat16 on the way count: a program that leaves them out, or rounds other values in their place, can miss the bound.
Values may be sent and summed in bfloat16 or wider, within the bound.
No kernel may reach another device: no remote copies, remote signals or barrier semaphores. Data moves between devices by JAX's collectives and lax.ppermute only.
A program may use at most 64 MiB of HBM per device.

v0:
```python
import jax
import jax.numpy as jnp
from jax import lax
from jax.sharding import PartitionSpec as P

TICKS = 4


epsilon = 1e-06


def shifted(value, axis, steps):
    count = lax.axis_size(axis)
    pairs = [(source, (source + steps) % count) for source in range(count)]
    return lax.ppermute(value, axis, pairs)


def contract_last(left_side, right_side):
    return lax.dot_general(
        left_side, right_side, (((1,), (1,)), ((), ())), preferred_element_type=jnp.float32
    )


def contract_first(left_side, right_side):
    return lax.dot_general(
        left_side, right_side, (((0,), (0,)), ((), ())), preferred_element_type=jnp.float32
    )


def rescale(updated, previous):
    old_norm = jnp.sqrt(jnp.sum(previous * previous, axis=-1, keepdims=True) + epsilon)
    new_norm = jnp.sqrt(jnp.sum(updated * updated, axis=-1, keepdims=True) + epsilon)
    return updated * (old_norm / new_norm)


def advance(fast, token_keys, token_values, step_sizes):
    gate_pre = contract_last(token_keys, fast[0])
    up_pre = contract_last(token_keys, fast[1])
    gate_sig = jax.nn.sigmoid(gate_pre)
    hidden = (gate_pre * gate_sig * up_pre).astype(jnp.bfloat16)
    target = (step_sizes.astype(jnp.float32)[:, None] * token_values.astype(jnp.float32)).astype(
        jnp.bfloat16
    )
    back_grad = contract_last(target, fast[2])
    grad_gate = (back_grad * up_pre * gate_sig * (1.0 + gate_pre * (1.0 - gate_sig))).astype(
        jnp.bfloat16
    )
    grad_up = (back_grad * gate_pre * gate_sig).astype(jnp.bfloat16)
    delta_gate = contract_first(grad_gate, token_keys)
    delta_up = contract_first(grad_up, token_keys)
    delta_down = contract_first(hidden, target)
    previous = fast.astype(jnp.float32)
    updated = previous + jnp.stack([delta_gate, delta_up, delta_down])
    return rescale(updated, previous).astype(jnp.bfloat16)


def serve_queries(fast, queries):
    gate_pre = contract_last(queries, fast[0])
    up_pre = contract_last(queries, fast[1])
    hidden = (gate_pre * jax.nn.sigmoid(gate_pre) * up_pre).astype(jnp.bfloat16)
    return jnp.dot(hidden, fast[2], preferred_element_type=jnp.float32).astype(jnp.bfloat16)


def body(fast_state, initial_fast, queries, token_keys, token_values, step_sizes):
    carried = fast_state[0]
    whole_initial = lax.all_gather(initial_fast, "seq", axis=1, tiled=True)
    position = lax.axis_index("seq")
    results = []
    section_count = lax.axis_size("seq")
    advanced = carried
    for step_index in range(TICKS):
        if step_index == 0:
            tick_queries = queries[0, 0]
            tick_keys = token_keys[0, 0]
            tick_values = token_values[0, 0]
            tick_steps = step_sizes[0, 0]
        else:
            tick_queries, tick_keys, tick_values, tick_steps = shifted(
                (
                    queries[0, step_index],
                    token_keys[0, step_index],
                    token_values[0, step_index],
                    step_sizes[0, step_index],
                ),
                "seq",
                -step_index,
            )
            restart = position + step_index == section_count
            carried = jnp.where(restart, whole_initial, advanced)
        advanced = advance(carried, tick_keys, tick_values, tick_steps)
        answer = serve_queries(advanced, tick_queries)
        if step_index == 0:
            results.append(answer)
        else:
            results.append(shifted(answer, "seq", step_index))
    return jnp.stack(results, axis=0)[None]


def solution(mesh):
    return jax.shard_map(
        body,
        mesh=mesh,
        in_specs=(
            P(("grp", "seq"), None, None, None),
            P(None, "seq", None),
            P(("grp", "seq"), None, None, None),
            P(("grp", "seq"), None, None, None),
            P(("grp", "seq"), None, None, None),
            P(("grp", "seq"), None, None),
        ),
        out_specs=P(("grp", "seq"), None, None, None),
        check_vma=False,
    )
```

profile of v0, /device:TPU:1, one launch (start us, length us, event | category | flops | bytes accessed | tf_op | source)
XLA Modules:
  0.0 195.9 jit_solution(10988839707194773126)
XLA Ops:
  6.5 0.7 all-gather.2.cloned.1.call-update
  7.3 0.8 slice_reduce_fusion
  8.1 5.7 %collective-permute-start.10 = (bf16[384]{0:T(512)(128)(2,1)S(1)}, bf16[384]{0:T(512)(128)(2,1)S(1)}, u32[]{:S(2)}, u32[]{:S(2)}) collective-permute-start(bf16[384]{0:T(512)(128)(2,1)S(1)} %get-tuple-element.13), channel_id=1, source_target_pairs={{0,13},{1,14},{2,15},{3,0},{4,1},{5,2},{6,3},{7,4},{8,5},{9,6},{10... | collective-permute-start | bytes 2312 | tf_op jit(solution)/shard_map/ppermute | solution.py:15
  14.0 2.3 %slice_bitcast_fusion.53 = (bf16[384,512]{1,0:T(8,128)(2,1)}, bf16[384,512]{1,0:T(8,128)(2,1)}, bf16[384,512]{1,0:T(8,128)(2,1)}) fusion(bf16[1,4,384,512]{3,2,1,0:T(8,128)(2,1)} %param.8), kind=kLoop, calls=%fused_computation.197 | loop fusion | bytes 2359296 | tf_op jit(solution)/shard_map/squeeze | solution.py:80
  16.3 1.8 collective-permute-start.3
  18.2 3.2 %copy.19 = bf16[1,3,1024,512]{2,3,1,0:T(8,128)(2,1)S(1)} copy(bf16[1,3,1024,512]{3,2,1,0:T(8,128)(2,1)} %param.6) | data formatting | bytes 6291456 | tf_op args[0]
  21.5 3.4 %slice_bitcast_fusion.49 = (bf16[384,512]{1,0:T(8,128)(2,1)}, bf16[384,512]{1,0:T(8,128)(2,1)}, bf16[384,512]{1,0:T(8,128)(2,1)}) fusion(bf16[1,4,384,512]{3,2,1,0:T(8,128)(2,1)} %param.10), kind=kLoop, calls=%fused_computation.193 | loop fusion | bytes 2359296 | tf_op jit(solution)/shard_map/squeeze | solution.py:82
  24.9 1.1 slice_bitcast_fusion.48
  25.9 0.6 fusion.67
  26.5 0.6 fusion.69
  27.2 0.8 copy-done.12
  28.0 0.6 fusion.71
  28.6 0.9 convolution_bitcast_fusion.10
  29.5 1.0 convolution_bitcast_fusion.9
  30.5 1.1 convolution_bitcast_fusion.11
  31.8 1.5 fusion.3
  33.3 1.1 collective-permute-start.8
  34.5 0.6 convert_element_type.178
  35.0 0.9 collective-permute-start.11
  35.9 0.6 convert_element_type.158
  36.5 0.6 copy-done.20
  37.1 1.3 convert_element_type.168
  38.4 47.0 %all-gather.2.cloned.1.call-done = bf16[3,1024,512]{2,1,0:T(8,128)(2,1)} async-done(((bf16[3,64,512]{2,1,0:T(8,128)(2,1)}), bf16[3,1024,512]{2,1,0:T(8,128)(2,1)}) %all-gather.2.cloned.1.call-update) | async-done | bytes 3145744 | tf_op jit(solution)/shard_map/all_gather | solution.py:66
  85.3 3.2 %copy.21 = bf16[3,1024,512]{1,2,0:T(8,128)(2,1)S(1)} copy(bf16[3,1024,512]{2,1,0:T(8,128)(2,1)} %all-gather.2.cloned.1.call-done) | data formatting | bytes 6291456 | tf_op jit(solution)/shard_map/all_gather | solution.py:66
  88.5 6.0 %broadcast_select_fusion.2 = (bf16[3,1024,512]{1,2,0:T(8,128)(2,1)S(1)}, bf16[3,1024,512]{1,2,0:T(8,128)(2,1)}) fusion(bf16[3,1024,512]{1,2,0:T(8,128)(2,1)S(1)} %copy.21, pred[]{:T(512)S(6)} %eq.9, f32[3,1024]{1,0:T(4,128)S(1)} %rsqrt_multiply_fusion.3, f32[1,1024,512]{1,2,0:T(8,128)} %copy-done.5, f32[1,1024,512]{1,2,0:T(8,128)} %copy-done.4, ...), kind=kLoop, calls=%fused_computation.22 | loop fusion | flops 11010048 | bytes 18886656 | tf_op jit(solution)/shard_map/jit(_where)/select_n | solution.py:89
  94.8 0.6 fusion.63
  95.4 0.6 fusion.64
  96.0 5.7 %collective-permute-done.1 = bf16[384,512]{1,0:T(8,128)(2,1)S(1)} collective-permute-done((bf16[384,512]{1,0:T(8,128)(2,1)S(1)}, bf16[384,512]{1,0:T(8,128)(2,1)S(1)}, u32[]{:S(2)}, u32[]{:S(2)}) %collective-permute-start.1) | collective-permute-done | bytes 393248 | tf_op jit(solution)/shard_map/ppermute | solution.py:15
  101.8 4.1 %collective-permute-start.6 = (bf16[384,512]{1,0:T(8,128)(2,1)}, bf16[384,512]{1,0:T(8,128)(2,1)}, u32[]{:S(2)}, u32[]{:S(2)}) collective-permute-start(bf16[384,512]{1,0:T(8,128)(2,1)} %get-tuple-element.27), channel_id=1, source_target_pairs={{0,14},{1,15},{2,0},{3,1},{4,2},{5,3},{6,4},{7,5},{8,6},{9,7},{10,... | collective-permute-start | bytes 1179656 | tf_op jit(solution)/shard_map/ppermute | solution.py:15
  105.8 0.6 fusion.65
  106.5 0.9 convolution_bitcast_fusion.6
  107.4 1.0 convolution_bitcast_fusion.8
  108.5 0.9 convolution_bitcast_fusion.7
  109.4 1.4 fusion
  110.9 3.6 %broadcast_select_fusion.1 = (bf16[3,1024,512]{1,2,0:T(8,128)(2,1)}, bf16[3,1024,512]{1,2,0:T(8,128)(2,1)S(1)}) fusion(bf16[3,1024,512]{1,2,0:T(8,128)(2,1)S(1)} %copy.21, pred[]{:T(512)S(6)} %eq.10, f32[3,1024]{1,0:T(4,128)S(1)} %rsqrt_multiply_fusion.2, f32[1,1024,512]{1,2,0:T(8,128)S(1)} %convolution_bitcast_fusion.6, ...), kind=kLoop, calls=%fused_computation.21 | loop fusion | flops 11010048 | bytes 18886656 | tf_op jit(solution)/shard_map/jit(_where)/select_n | solution.py:89
  114.5 1.7 copy-done.8
  116.2 2.7 %fusion.62 = f32[1024,384]{0,1:T(8,128)} fusion(bf16[384,512]{1,0:T(8,128)(2,1)} %collective-permute-done.3, bf16[3,1024,512]{1,2,0:T(8,128)(2,1)S(1)} %get-tuple-element.19), kind=kOutput, calls=%fused_computation.144 | convolution fusion | flops 402653184 | bytes 3014656 | tf_op jit(solution)/shard_map/dot_general | solution.py:19
  118.9 4.0 %convolution_convert_fusion.2 = bf16[384,512]{1,0:T(8,128)(2,1)} fusion(f32[1024,384]{0,1:T(8,128)} %fusion.62, bf16[384,512]{1,0:T(8,128)(2,1)} %collective-permute-done.3, bf16[3,1024,512]{1,2,0:T(8,128)(2,1)} %copy-done.8), kind=kOutput, calls=%fused_computation.118 | convolution fusion | flops 807862272 | bytes 4456448 | tf_op jit(solution)/shard_map/dot_general | solution.py:61
  123.3 0.7 copy-done.13
  124.0 3.3 %collective-permute-start.12 = (bf16[384,512]{1,0:T(8,128)(2,1)}, bf16[384,512]{1,0:T(8,128)(2,1)S(1)}, u32[]{:S(2)}, u32[]{:S(2)}) collective-permute-start(bf16[384,512]{1,0:T(8,128)(2,1)} %get-tuple-element.28), channel_id=1, source_target_pairs={{0,13},{1,14},{2,15},{3,0},{4,1},{5,2},{6,3},{7,4},{8,5},{9,6},{10... | collective-permute-start | bytes 1179656 | tf_op jit(solution)/shard_map/ppermute | solution.py:15
  127.3 2.1 %fusion.59 = f32[1024,384]{0,1:T(8,128)S(1)} fusion(bf16[384,512]{1,0:T(8,128)(2,1)} %copy-done.13, bf16[3,1024,512]{1,2,0:T(8,128)(2,1)} %get-tuple-element.18), kind=kOutput, calls=%fused_computation.136 | convolution fusion | flops 402653184 | bytes 3014656 | tf_op jit(solution)/shard_map/dot_general | solution.py:19
  129.4 1.8 fusion.60
  131.2 1.4 collective-permute-start.4
  132.6 1.6 fusion.61
  134.3 2.0 convolution_bitcast_fusion.3
  136.2 1.0 convolution_bitcast_fusion.5
  137.3 0.9 convolution_bitcast_fusion.4
  138.1 1.4 fusion.1
  139.6 3.6 %broadcast_select_fusion = (bf16[3,1024,512]{1,2,0:T(8,128)(2,1)}, bf16[3,1024,512]{1,2,0:T(8,128)(2,1)S(1)}) fusion(bf16[3,1024,512]{1,2,0:T(8,128)(2,1)S(1)} %copy.21, pred[]{:T(512)S(6)} %eq.11, f32[3,1024]{1,0:T(4,128)S(1)} %rsqrt_multiply_fusion.1, f32[1,1024,512]{1,2,0:T(8,128)S(1)} %convolution_bitcast_fusion.3, ...), kind=kLoop, calls=%fused_computation.20 | loop fusion | flops 11010048 | bytes 18886656 | tf_op jit(solution)/shard_map/jit(_where)/select_n | solution.py:89
  143.2 1.7 copy-done.9
  144.9 2.7 %fusion.58 = f32[1024,384]{0,1:T(8,128)} fusion(bf16[384,512]{1,0:T(8,128)(2,1)} %collective-permute-done.8, bf16[3,1024,512]{1,2,0:T(8,128)(2,1)S(1)} %get-tuple-element.17), kind=kOutput, calls=%fused_computation.134 | convolution fusion | flops 402653184 | bytes 3014656 | tf_op jit(solution)/shard_map/dot_general | solution.py:19
  147.7 4.1 %convolution_convert_fusion.1 = bf16[384,512]{1,0:T(8,128)(2,1)} fusion(f32[1024,384]{0,1:T(8,128)} %fusion.58, bf16[384,512]{1,0:T(8,128)(2,1)} %collective-permute-done.8, bf16[3,1024,512]{1,2,0:T(8,128)(2,1)} %copy-done.9), kind=kOutput, calls=%fused_computation.117 | convolution fusion | flops 807862272 | bytes 4456448 | tf_op jit(solution)/shard_map/dot_general | solution.py:61
  153.1 1.6 fusion.57
  154.7 2.0 convolution_bitcast_fusion
  156.7 1.0 convolution_bitcast_fusion.2
  157.7 0.9 convolution_bitcast_fusion.1
  158.6 1.5 fusion.2
  160.1 1.4 multiply_convert_fusion
  161.6 4.1 %fusion.66 = f32[1024,384]{0,1:T(8,128)} fusion(bf16[3,1024,512]{1,2,0:T(8,128)(2,1)} %get-tuple-element.21, bf16[1,4,384,512]{3,2,1,0:T(8,128)(2,1)} %param.8), kind=kOutput, calls=%fused_computation.154 | convolution fusion | flops 402653184 | bytes 3014656 | tf_op jit(solution)/shard_map/dot_general | solution.py:19
  165.8 2.7 %fusion.54 = f32[1024,384]{0,1:T(8,128)} fusion(bf16[384,512]{1,0:T(8,128)(2,1)} %collective-permute-done.13, bf16[3,1024,512]{1,2,0:T(8,128)(2,1)S(1)} %multiply_convert_fusion), kind=kOutput, calls=%fused_computation.124 | convolution fusion | flops 402653184 | bytes 3014656 | tf_op jit(solution)/shard_map/dot_general | solution.py:19
  168.5 4.2 %convolution_convert_fusion = bf16[384,512]{1,0:T(8,128)(2,1)} fusion(f32[1024,384]{0,1:T(8,128)} %fusion.54, bf16[384,512]{1,0:T(8,128)(2,1)} %collective-permute-done.13, bf16[3,1024,512]{1,2,0:T(8,128)(2,1)} %copy-done.10), kind=kOutput, calls=%fused_computation.116 | convolution fusion | flops 807862272 | bytes 4456448 | tf_op jit(solution)/shard_map/dot_general | solution.py:61
  172.7 3.5 %fusion.53 = bf16[1,384,512]{2,1,0:T(8,128)(2,1)} fusion(bf16[3,1024,512]{1,2,0:T(8,128)(2,1)S(1)} %copy-done.7, f32[1024,384]{0,1:T(8,128)} %fusion.66, bf16[1,4,384,512]{3,2,1,0:T(8,128)(2,1)} %param.8), kind=kOutput, calls=%fused_computation.120 | convolution fusion | flops 807862272 | bytes 4456448 | tf_op jit(solution)/shard_map/dot_general | solution.py:61
  176.2 10.3 %collective-permute-done.14 = bf16[384,512]{1,0:T(8,128)(2,1)S(1)} collective-permute-done((bf16[384,512]{1,0:T(8,128)(2,1)}, bf16[384,512]{1,0:T(8,128)(2,1)S(1)}, u32[]{:S(2)}, u32[]{:S(2)}) %collective-permute-start.14) | collective-permute-done | bytes 393248 | tf_op jit(solution)/shard_map/ppermute | solution.py:15
  186.4 2.6 %maximum_bitcast_fusion = bf16[1,4,384,512]{3,2,1,0:T(8,128)(2,1)} fusion(bf16[1,384,512]{2,1,0:T(8,128)(2,1)S(1)} %bitcast.391, bf16[1,384,512]{2,1,0:T(8,128)(2,1)} %bitcast.51, bf16[1,384,512]{2,1,0:T(8,128)(2,1)} %bitcast.34, bf16[1,384,512]{2,1,0:T(8,128)(2,1)} %fusion.53), kind=kLoop, calls=%fused_computation.35 | loop fusion | flops 2359296 | bytes 3145728 | tf_op jit(solution)/shard_map/broadcast_in_dim | solution.py:96
  (66 shorter events, 2.7 us)
Async XLA Ops:
  6.5 78.8 %all-gather.2.cloned.1.call-start = ((), (), s32[]{:S(2)}) async-start(), calls=%async_computation | async-start | bytes 3342336 | tf_op jit(solution)/shard_map/all_gather | solution.py:66
  8.1 25.2 %collective-permute-start.10 = (bf16[384]{0:T(512)(128)(2,1)S(1)}, bf16[384]{0:T(512)(128)(2,1)S(1)}, u32[]{:S(2)}, u32[]{:S(2)}) collective-permute-start(bf16[384]{0:T(512)(128)(2,1)S(1)} %get-tuple-element.13), channel_id=1, source_target_pairs={{0,13},{1,14},{2,15},{3,0},{4,1},{5,2},{6,3},{7,4},{8,5},{9,6},{10... | collective-permute-start | bytes 2312 | tf_op jit(solution)/shard_map/ppermute | solution.py:15
  13.8 21.3 %collective-permute-start = (bf16[384]{0:T(512)(128)(2,1)S(1)}, bf16[384]{0:T(512)(128)(2,1)S(1)}, u32[]{:S(2)}, u32[]{:S(2)}) collective-permute-start(bf16[384]{0:T(512)(128)(2,1)S(1)} %get-tuple-element.14), channel_id=1, source_target_pairs={{0,15},{1,0},{2,1},{3,2},{4,3},{5,4},{6,5},{7,6},{8,7},{9,8},{10,9... | collective-permute-start | bytes 2312 | tf_op jit(solution)/shard_map/ppermute | solution.py:15
  13.8 22.7 %collective-permute-start.5 = (bf16[384]{0:T(512)(128)(2,1)S(1)}, bf16[384]{0:T(512)(128)(2,1)S(1)}, u32[]{:S(2)}, u32[]{:S(2)}) collective-permute-start(bf16[384]{0:T(512)(128)(2,1)S(1)} %get-tuple-element.15), channel_id=1, source_target_pairs={{0,14},{1,15},{2,0},{3,1},{4,2},{5,3},{6,4},{7,5},{8,6},{9,7},{10,... | collective-permute-start | bytes 2312 | tf_op jit(solution)/shard_map/ppermute | solution.py:15
  16.3 98.2 %collective-permute-start.3 = (bf16[384,512]{1,0:T(8,128)(2,1)}, bf16[384,512]{1,0:T(8,128)(2,1)}, u32[]{:S(2)}, u32[]{:S(2)}) collective-permute-start(bf16[384,512]{1,0:T(8,128)(2,1)} %get-tuple-element.22), channel_id=1, source_target_pairs={{0,15},{1,0},{2,1},{3,2},{4,3},{5,4},{6,5},{7,6},{8,7},{9,8},{10,9... | collective-permute-start | bytes 1179656 | tf_op jit(solution)/shard_map/ppermute | solution.py:15
  18.1 3.4 %copy-start.16 = (bf16[1,4,384]{2,1,0:T(4,128)(2,1)S(1)}, bf16[1,4,384]{2,1,0:T(4,128)(2,1)}, u32[]{:S(2)}) copy-start(bf16[1,4,384]{2,1,0:T(4,128)(2,1)} %param.11) | copy-start | bytes 9220
  18.1 147.7 %collective-permute-start.13 = (bf16[384,512]{1,0:T(8,128)(2,1)}, bf16[384,512]{1,0:T(8,128)(2,1)}, u32[]{:S(2)}, u32[]{:S(2)}) collective-permute-start(bf16[384,512]{1,0:T(8,128)(2,1)} %get-tuple-element.23), channel_id=1, source_target_pairs={{0,13},{1,14},{2,15},{3,0},{4,1},{5,2},{6,3},{7,4},{8,5},{9,6},{10... | collective-permute-start | bytes 1179656 | tf_op jit(solution)/shard_map/ppermute | solution.py:15
  21.4 10.1 %copy-start.2 = (bf16[1,3,1024,512]{2,3,1,0:T(8,128)(2,1)}, bf16[1,3,1024,512]{2,3,1,0:T(8,128)(2,1)S(1)}, u32[]{:S(2)}) copy-start(bf16[1,3,1024,512]{2,3,1,0:T(8,128)(2,1)S(1)} %copy.19) | copy-start | bytes 9437188
  21.4 3.4 %copy-start.11 = (bf16[1,4,384,512]{3,2,1,0:T(8,128)(2,1)S(1)}, bf16[1,4,384,512]{3,2,1,0:T(8,128)(2,1)}, u32[]{:S(2)}) copy-start(bf16[1,4,384,512]{3,2,1,0:T(8,128)(2,1)} %param.9) | copy-start | bytes 4718596
  21.5 4.4 %copy-start.3 = (bf16[1,3,1024,512]{3,2,1,0:T(8,128)(2,1)S(1)}, bf16[1,3,1024,512]{3,2,1,0:T(8,128)(2,1)}, u32[]{:S(2)}) copy-start(bf16[1,3,1024,512]{3,2,1,0:T(8,128)(2,1)} %param.6) | copy-start | bytes 9437188
  26.5 1.4 copy-start.12
  29.5 2.1 %copy-start.4 = (f32[1,1024,512]{1,2,0:T(8,128)}, f32[1,1024,512]{1,2,0:T(8,128)S(1)}, u32[]{:S(2)}) copy-start(f32[1,1024,512]{1,2,0:T(8,128)S(1)} %convolution_bitcast_fusion.10) | copy-start | bytes 6291460
  30.4 1.3 copy-start.5
  31.8 1.5 copy-start.6
  33.3 109.9 %collective-permute-start.8 = (bf16[384,512]{1,0:T(8,128)(2,1)}, bf16[384,512]{1,0:T(8,128)(2,1)}, u32[]{:S(2)}, u32[]{:S(2)}) collective-permute-start(bf16[384,512]{1,0:T(8,128)(2,1)} %get-tuple-element.24), channel_id=1, source_target_pairs={{0,14},{1,15},{2,0},{3,1},{4,2},{5,3},{6,4},{7,5},{8,6},{9,7},{10,... | collective-permute-start | bytes 1179656 | tf_op jit(solution)/shard_map/ppermute | solution.py:15
  35.0 118.0 %collective-permute-start.11 = (bf16[384,512]{1,0:T(8,128)(2,1)}, bf16[384,512]{1,0:T(8,128)(2,1)}, u32[]{:S(2)}, u32[]{:S(2)}) collective-permute-start(bf16[384,512]{1,0:T(8,128)(2,1)} %get-tuple-element.25), channel_id=1, source_target_pairs={{0,13},{1,14},{2,15},{3,0},{4,1},{5,2},{6,3},{7,4},{8,5},{9,6},{10... | collective-permute-start | bytes 1179656 | tf_op jit(solution)/shard_map/ppermute | solution.py:15
  36.5 0.6 copy-start.20
  37.1 57.4 %collective-permute-start.2 = (bf16[384,512]{1,0:T(8,128)(2,1)}, bf16[384,512]{1,0:T(8,128)(2,1)S(1)}, u32[]{:S(2)}, u32[]{:S(2)}) collective-permute-start(bf16[384,512]{1,0:T(8,128)(2,1)} %get-tuple-element.29), channel_id=1, source_target_pairs={{0,15},{1,0},{2,1},{3,2},{4,3},{5,4},{6,5},{7,6},{8,7},{9,8},{10,9... | collective-permute-start | bytes 1179656 | tf_op jit(solution)/shard_map/ppermute | solution.py:15
  88.5 6.0 %copy-start.15 = (bf16[384,512]{1,0:T(8,128)(2,1)S(1)}, bf16[384,512]{1,0:T(8,128)(2,1)}, u32[]{:S(2)}) copy-start(bf16[384,512]{1,0:T(8,128)(2,1)} %get-tuple-element.26) | copy-start | bytes 1179652
  94.5 7.3 %collective-permute-start.1 = (bf16[384,512]{1,0:T(8,128)(2,1)S(1)}, bf16[384,512]{1,0:T(8,128)(2,1)S(1)}, u32[]{:S(2)}, u32[]{:S(2)}) collective-permute-start(bf16[384,512]{1,0:T(8,128)(2,1)S(1)} %copy-done.15), channel_id=1, source_target_pairs={{0,15},{1,0},{2,1},{3,2},{4,3},{5,4},{6,5},{7,6},{8,7},{9,8},{10,9... | collective-permute-start | bytes 1179656 | tf_op jit(solution)/shard_map/ppermute | solution.py:15
  95.4 10.4 %copy-start.19 = (f32[384]{0:T(512)S(1)}, f32[384]{0:T(512)}, u32[]{:S(2)}) copy-start(f32[384]{0:T(512)} %convert_element_type.158) | copy-start | bytes 4612
  101.8 29.5 %collective-permute-start.6 = (bf16[384,512]{1,0:T(8,128)(2,1)}, bf16[384,512]{1,0:T(8,128)(2,1)}, u32[]{:S(2)}, u32[]{:S(2)}) collective-permute-start(bf16[384,512]{1,0:T(8,128)(2,1)} %get-tuple-element.27), channel_id=1, source_target_pairs={{0,14},{1,15},{2,0},{3,1},{4,2},{5,3},{6,4},{7,5},{8,6},{9,7},{10,... | collective-permute-start | bytes 1179656 | tf_op jit(solution)/shard_map/ppermute | solution.py:15
  114.5 1.7 copy-start.8
  114.5 8.8 %collective-permute-start.7 = (bf16[384,512]{1,0:T(8,128)(2,1)}, bf16[384,512]{1,0:T(8,128)(2,1)S(1)}, u32[]{:S(2)}, u32[]{:S(2)}) collective-permute-start(bf16[384,512]{1,0:T(8,128)(2,1)} %get-tuple-element.30), channel_id=1, source_target_pairs={{0,14},{1,15},{2,0},{3,1},{4,2},{5,3},{6,4},{7,5},{8,6},{9,7},{10,... | collective-permute-start | bytes 1179656 | tf_op jit(solution)/shard_map/ppermute | solution.py:15
  123.2 0.7 copy-start.13
  124.0 5.4 %copy-start.14 = (bf16[384,512]{1,0:T(8,128)(2,1)S(1)}, bf16[384,512]{1,0:T(8,128)(2,1)}, u32[]{:S(2)}) copy-start(bf16[384,512]{1,0:T(8,128)(2,1)} %copy-done.13) | copy-start | bytes 1179652
  124.0 27.8 %collective-permute-start.12 = (bf16[384,512]{1,0:T(8,128)(2,1)}, bf16[384,512]{1,0:T(8,128)(2,1)S(1)}, u32[]{:S(2)}, u32[]{:S(2)}) collective-permute-start(bf16[384,512]{1,0:T(8,128)(2,1)} %get-tuple-element.28), channel_id=1, source_target_pairs={{0,13},{1,14},{2,15},{3,0},{4,1},{5,2},{6,3},{7,4},{8,5},{9,6},{10... | collective-permute-start | bytes 1179656 | tf_op jit(solution)/shard_map/ppermute | solution.py:15
  127.3 5.3 %copy-start = (bf16[3,1024,512]{1,2,0:T(8,128)(2,1)S(1)}, bf16[3,1024,512]{1,2,0:T(8,128)(2,1)}, u32[]{:S(2)}) copy-start(bf16[3,1024,512]{1,2,0:T(8,128)(2,1)} %get-tuple-element.18) | copy-start | bytes 9437188
  129.4 3.2 %copy-start.18 = (f32[384]{0:T(512)S(1)}, f32[384]{0:T(512)}, u32[]{:S(2)}) copy-start(f32[384]{0:T(512)} %convert_element_type.168) | copy-start | bytes 4612
  131.2 45.0 %collective-permute-start.4 = (bf16[384,512]{1,0:T(8,128)(2,1)}, bf16[384,512]{1,0:T(8,128)(2,1)}, u32[]{:S(2)}, u32[]{:S(2)}) collective-permute-start(bf16[384,512]{1,0:T(8,128)(2,1)} %convolution_convert_fusion.2), channel_id=1, source_target_pairs={{0,1},{1,2},{2,3},{3,4},{4,5},{5,6},{6,7},{7,8},{8,9},{9,10},{10,1... | collective-permute-start | bytes 1179656 | tf_op jit(solution)/shard_map/ppermute | solution.py:15
  143.2 1.7 copy-start.9
  147.7 4.2 %copy-start.1 = (bf16[3,1024,512]{1,2,0:T(8,128)(2,1)S(1)}, bf16[3,1024,512]{1,2,0:T(8,128)(2,1)}, u32[]{:S(2)}) copy-start(bf16[3,1024,512]{1,2,0:T(8,128)(2,1)} %get-tuple-element.16) | copy-start | bytes 9437188
  151.8 24.4 %collective-permute-start.9 = (bf16[384,512]{1,0:T(8,128)(2,1)}, bf16[384,512]{1,0:T(8,128)(2,1)}, u32[]{:S(2)}, u32[]{:S(2)}) collective-permute-start(bf16[384,512]{1,0:T(8,128)(2,1)} %convolution_convert_fusion.1), channel_id=1, source_target_pairs={{0,2},{1,3},{2,4},{3,5},{4,6},{5,7},{6,8},{7,9},{8,10},{9,11},{10,... | collective-permute-start | bytes 1179656 | tf_op jit(solution)/shard_map/ppermute | solution.py:15
  152.4 0.7 copy-start.17
  161.6 4.2 %copy-start.10 = (bf16[3,1024,512]{1,2,0:T(8,128)(2,1)}, bf16[3,1024,512]{1,2,0:T(8,128)(2,1)S(1)}, u32[]{:S(2)}) copy-start(bf16[3,1024,512]{1,2,0:T(8,128)(2,1)S(1)} %multiply_convert_fusion) | copy-start | bytes 9437188
  168.5 4.2 %copy-start.7 = (bf16[3,1024,512]{1,2,0:T(8,128)(2,1)S(1)}, bf16[3,1024,512]{1,2,0:T(8,128)(2,1)}, u32[]{:S(2)}) copy-start(bf16[3,1024,512]{1,2,0:T(8,128)(2,1)} %get-tuple-element.21) | copy-start | bytes 9437188
  172.7 13.8 %collective-permute-start.14 = (bf16[384,512]{1,0:T(8,128)(2,1)}, bf16[384,512]{1,0:T(8,128)(2,1)S(1)}, u32[]{:S(2)}, u32[]{:S(2)}) collective-permute-start(bf16[384,512]{1,0:T(8,128)(2,1)} %convolution_convert_fusion), channel_id=1, source_target_pairs={{0,3},{1,4},{2,5},{3,6},{4,7},{5,8},{6,9},{7,10},{8,11},{9,12},{10... | collective-permute-start | bytes 1179656 | tf_op jit(solution)/shard_map/ppermute | solution.py:15
Sparse Core Ops, SparseCore 0:
  9.5 75.7 all-gather.1
where the time goes:
time: 197 us; the launch traced here: 196 us
  waiting for transfers between devices  64 us (32%)
  matrix products  53.6 us (27%)
  other arithmetic  25.6 us (13%)
  local copies, waits for them, and re-layouts  19.8 us (10%)
  starting transfers between devices  19 us (10%)
  between operations  13.9 us (7%)
    all_gather x1, waiting for transfers between devices, body(): whole_initial = lax.all_gather(initial_fast, 'seq', axis=1, tiled=True)  47 us
    dot_general x16, matrix products, contract_last(): lax.dot_general(left_side, right_side, (((1,), (1,)), ((), ())), preferre...  24.2 us
    ppermute x15, starting transfers between devices, shifted(): return lax.ppermute(value, axis, pairs)  19 us
    ppermute x15, waiting for transfers between devices, shifted(): return lax.ppermute(value, axis, pairs)  16.3 us
    dot_general x4, matrix products, serve_queries(): jnp.dot(hidden, fast[2], preferred_element_type=jnp.float32)  15.8 us
    dot_general x12, matrix products, contract_first(): lax.dot_general(left_side, right_side, (((0,), (0,)), ((), ())), preferre...  13.5 us
    select_n x3, other arithmetic, body(): carried = jnp.where(restart, whole_initial, advanced)  13.2 us
    unnamed x43, local copies, waits for them, and re-layouts  9.13 us
  transfers between devices with their start and end apart: 16, of which 4 were waited for; matrix products, arithmetic and copies ran while one was open for 46% of the time, Pallas kernels for 0%

commit v1 on v0

v1 whole, which is shorter than its diff:
```python
import functools
import jax
import jax.numpy as jnp
from jax import lax
from jax.experimental import pallas as pl
from jax.experimental.pallas import tpu as pltpu
from jax.sharding import PartitionSpec as P

epsilon = 1e-06
f32 = jnp.float32
bf16 = jnp.bfloat16


def nt(a, b):
    return lax.dot_general(a, b, (((1,), (1,)), ((), ())), preferred_element_type=f32)


def tn(a, b):
    return lax.dot_general(a, b, (((0,), (0,)), ((), ())), preferred_element_type=f32)


def nn(a, b):
    return lax.dot_general(a, b, (((1,), (0,)), ((), ())), preferred_element_type=f32)


def scaled_values(steps_row, values):
    lanes = 128
    span, width = values.shape
    column = jnp.broadcast_to(steps_row.astype(f32), (lanes, span)).T
    return jnp.concatenate(
        [
            (column * values[:, i : i + lanes].astype(f32)).astype(bf16)
            for i in range(0, width, lanes)
        ],
        axis=1,
    )


def pack_kernel(tick, k_ref, v_ref, q_ref, r_ref, o_ref):
    o_ref[0] = k_ref[...]
    o_ref[1] = scaled_values(r_ref[tick : tick + 1, :], v_ref[...])
    o_ref[2] = q_ref[...]


def pack(tick, keys, values, queries, steps):
    _, ticks, span, width = keys.shape
    one = pl.BlockSpec((None, None, span, width), lambda i: (0, tick, 0, 0))
    return pl.pallas_call(
        functools.partial(pack_kernel, tick),
        grid=(1,),
        in_specs=[one, one, one, pl.BlockSpec((None, ticks, span), lambda i: (0, 0, 0))],
        out_specs=pl.BlockSpec((3, span, width), lambda i: (0, 0, 0)),
        out_shape=jax.ShapeDtypeStruct((3, span, width), bf16),
        name=f"pack{tick}",
    )(keys, values, queries, steps)


def step_rows(old, delta):
    previous = old.astype(f32)
    updated = previous + delta
    old_norm = jnp.sqrt(jnp.sum(previous * previous, axis=-1, keepdims=True) + epsilon)
    new_norm = jnp.sqrt(jnp.sum(updated * updated, axis=-1, keepdims=True) + epsilon)
    return (updated * (old_norm / new_norm)).astype(bf16)


def unit_block(keys, target, queries, gate, up, down):
    gate_pre = nt(keys, gate)
    up_pre = nt(keys, up)
    back_grad = nt(target, down)
    sig = jax.nn.sigmoid(gate_pre)
    silu = gate_pre * sig
    hidden = (silu * up_pre).astype(bf16)
    grad_up = (back_grad * silu).astype(bf16)
    grad_gate = (back_grad * up_pre * sig * (1.0 + gate_pre * (1.0 - sig))).astype(bf16)
    new_gate = step_rows(gate, tn(grad_gate, keys))
    new_up = step_rows(up, tn(grad_up, keys))
    new_down = step_rows(down, tn(hidden, target))
    c = nt(queries, new_gate)
    e = nt(queries, new_up)
    served = (c * jax.nn.sigmoid(c) * e).astype(bf16)
    return new_gate, new_up, new_down, nn(served, new_down)


def unit_kernel(raw, two_tokens, two_states, flags_ref, *refs):
    refs = list(refs)
    take = lambda n: [refs.pop(0) for _ in range(n)]
    if raw:
        k_ref, v_ref, q_ref, r_ref = take(4)
    else:
        packs = take(2 if two_tokens else 1)
    states = take(2 if two_states else 1)
    take(1)
    new_ref, ans_ref, tokens, acc = refs
    step = pl.program_id(0)

    @pl.when(flags_ref[0] != 0)
    def _():
        @pl.when(step == 0)
        def _():
            if raw:
                tokens[0] = k_ref[...]
                tokens[1] = scaled_values(r_ref[0:1, :], v_ref[...])
                tokens[2] = q_ref[...]
            elif two_tokens:
                @pl.when(flags_ref[1] != 0)
                def _():
                    tokens[...] = packs[1][...]

                @pl.when(flags_ref[1] == 0)
                def _():
                    tokens[...] = packs[0][...]

            acc[...] = jnp.zeros_like(acc)

        source = tokens if (raw or two_tokens) else packs[0]
        old = [states[0][i] for i in range(3)]
        if two_states:
            pick = flags_ref[2] != 0
            old = [jnp.where(pick, states[1][i], old[i]) for i in range(3)]
        new_gate, new_up, new_down, part = unit_block(
            source[0], source[1], source[2], *old
        )
        new_ref[0] = new_gate
        new_ref[1] = new_up
        new_ref[2] = new_down
        acc[...] += part

        @pl.when(step == pl.num_programs(0) - 1)
        def _():
            ans_ref[...] = acc[...].astype(bf16)


def unit(name, flags, tokens, states, after, raw=False, ticks=None, block=256):
    width = tokens[0].shape[-1]
    span = tokens[0].shape[-2]
    hid = states[0].shape[-2]
    lead = (None,) * (states[0].ndim - 3)
    zeros = (0,) * (states[0].ndim - 3)
    two_tokens = (not raw) and len(tokens) == 2
    two_states = len(states) == 2
    if raw:
        first = pl.BlockSpec((None, None, span, width), lambda i, f: (0, 0, 0, 0))
        token_specs = [first] * 3 + [
            pl.BlockSpec((None,) + tokens[3].shape[1:], lambda i, f: (0, 0, 0))
        ]
        ans_spec = pl.BlockSpec((None, None, span, width), lambda i, f: (0, 0, 0, 0))
        ans_shape = tokens[0].shape
    else:
        token_specs = [
            pl.BlockSpec((3, span, width), lambda i, f: (0, 0, 0)) for _ in tokens
        ]
        ans_spec = pl.BlockSpec((span, width), lambda i, f: (0, 0))
        ans_shape = (span, width)

    def state_map(second):
        def index(i, f):
            use = f[0] if not two_states else f[0] * (f[2] if second else 1 - f[2])
            return zeros + (0, i * use, 0)
        return index

    state_specs = [
        pl.BlockSpec(lead + (3, block, width), state_map(n == 1))
        for n in range(len(states))
    ]
    return pl.pallas_call(
        functools.partial(unit_kernel, raw, two_tokens, two_states),
        grid_spec=pltpu.PrefetchScalarGridSpec(
            num_scalar_prefetch=1,
            grid=(hid // block,),
            in_specs=token_specs + state_specs + [pl.BlockSpec(memory_space=pl.ANY)],
            out_specs=[
                pl.BlockSpec((3, block, width), lambda i, f: (0, i * f[0], 0)),
                ans_spec,
            ],
            scratch_shapes=[
                pltpu.VMEM((3, span, width) if (raw or two_tokens) else (8, 128), bf16),
                pltpu.VMEM((span, width), f32),
            ],
        ),
        out_shape=[
            jax.ShapeDtypeStruct((3, hid, width), bf16),
            jax.ShapeDtypeStruct(ans_shape, bf16),
        ],
        name=name,
    )(flags, *tokens, *states, after)


def gather_initial(initial, position, count):
    core = 2
    held = initial
    reach = core
    while reach < count:
        pairs = []
        for start in range(0, count, 2 * reach):
            for c in range(core):
                if start + reach + c < count:
                    pairs.append((start + reach + c, start + c))
        held = jnp.concatenate([held, lax.ppermute(held, "seq", pairs)], axis=1)
        reach *= 2
    other = lax.ppermute(held, "seq", [(0, 1), (1, 0)])
    return jnp.concatenate([held, other], axis=1)


def body(fast_state, initial_fast, queries, token_keys, token_values, step_sizes):
    count = lax.axis_size("seq")
    position = lax.axis_index("seq")
    i32 = jnp.int32
    on = jnp.ones((), i32)
    off = jnp.zeros((), i32)
    flags = jnp.stack([on, off, off])
    first = (position == 0).astype(i32)
    second = (position == 1).astype(i32)
    extra = first + second
    flags_e = jnp.stack([extra, second, second])

    def send(value, pairs):
        return lax.ppermute(value, "seq", pairs)

    packs = [None] + [
        pack(t, token_keys, token_values, queries, step_sizes) for t in (1, 2, 3)
    ]
    down = lambda t: [(s, s - t) for s in range(t, count)]
    up = lambda t: [(s, s + t) for s in range(count - t)]
    tokens = [None] + [send(packs[t], down(t)) for t in (1, 2, 3)]
    cross2 = send(packs[2], [(1, 0), (0, 1)])
    cross3 = send(packs[3], [(2, 0), (0, 1)])
    whole = gather_initial(initial_fast, position, count)

    state, out = unit(
        "u0", flags, [token_keys, token_values, queries, step_sizes], [fast_state],
        step_sizes, raw=True,
    )
    s1, a1 = unit("u1", flags, [tokens[1]], [state], out)
    b1 = send(a1, up(1))
    e1, x1 = unit("e1", flags_e, [packs[1], cross2], [whole], a1)
    s2, a2 = unit("u2", flags, [tokens[2]], [s1], x1)
    b2 = send(a2, up(2))
    e2, x2 = unit("e2", flags_e, [cross2, packs[3]], [e1], a2)
    c2 = send(jnp.where(first != 0, x2, x1), [(0, 1), (1, 0)])
    e3, x3 = unit("e3", flags_e, [cross3], [e2, whole], x2)
    c3 = send(x3, [(0, 2), (1, 0)])
    s3, a3 = unit("u3", flags, [tokens[3]], [s2], x3)
    b3 = send(a3, up(3))

    r1 = jnp.where(first != 0, x1, b1)
    r2 = jnp.where(extra != 0, c2, b2)
    early3 = jnp.where(second != 0, x2, c3)
    r3 = jnp.where(position < 3, early3, b3)
    for t, r in ((1, r1), (2, r2), (3, r3)):
        out = lax.dynamic_update_slice(out, r[None, None], (0, t, 0, 0))
    return out


def solution(mesh):
    return jax.shard_map(
        body,
        mesh=mesh,
        in_specs=(
            P(("grp", "seq"), None, None, None),
            P(None, "seq", None),
            P(("grp", "seq"), None, None, None),
            P(("grp", "seq"), None, None, None),
            P(("grp", "seq"), None, None, None),
            P(("grp", "seq"), None, None),
        ),
        out_specs=P(("grp", "seq"), None, None, None),
        check_vma=False,
    )
```

time: 197 us -> 166 us (0.84)
  Pallas kernels: 0 us -> 87.3 us
  matrix products: 53.6 us -> 0 us
  waiting for transfers between devices: 64 us -> 31.4 us
  other arithmetic: 25.6 us -> 7.61 us
  between operations: 13.9 us -> 0.28 us
  local copies, waits for them, and re-layouts: 19.8 us -> 6.47 us
  starting transfers between devices: 19 us -> 31.6 us
    pallas_call x0 -> x10, Pallas kernels: none -> 87.3 us  [the longest x7 79.9 us: unit(): pl.pallas_call(functools.partial(unit_kernel, raw, two_tokens, two_states...]
    dot_general x32 -> x0, matrix products: 53.6 us -> none  [the longest x16 24.2 us: contract_last(): lax.dot_general(left_side, right_side, (((1,), (1,)), ((), ())), preferre...]
    all_gather x1 -> x0, waiting for transfers between devices: 47 us -> none  [body(): whole_initial = lax.all_gather(initial_fast, 'seq', axis=1, tiled=True)]
    ppermute x15 -> x14, waiting for transfers between devices: 16.3 us -> 31.4 us  [the longest x3 29.1 us: gather_initial(): held = jnp.concatenate([held, lax.ppermute(held, 'seq', pairs)], axis=1)]
    select_n x3 -> x1, other arithmetic: 13.2 us -> 0.05 us  [body(): c2 = send(jnp.where(first != 0, x2, x1), [(0, 1), (1, 0)])]
    ppermute x15 -> x14, starting transfers between devices: 19 us -> 31.6 us  [the longest x10 22.7 us: send(): return lax.ppermute(value, 'seq', pairs)]
    squeeze x3 -> x0, local copies, waits for them, and re-layouts: 6.68 us -> none  [the longest x1 3.37 us: body(): token_values[0, step_index]]
    reduce_sum x4 -> x0, other arithmetic: 5.86 us -> none  [rescale(): jnp.sum(previous * previous, axis=-1, keepdims=True) + epsilon]
  transfers between devices with their start and end apart: 16 -> 14, of which waited for: 4 -> 4; matrix products, arithmetic and copies ran while one was open for 46% -> 6% of each run, Pallas kernels for 0% -> 53%
where the time goes in v1:
time: 166 us; the launch traced here: 165 us
  Pallas kernels  87.3 us (53%)
  starting transfers between devices  31.6 us (19%)
  waiting for transfers between devices  31.4 us (19%)
  other arithmetic  7.61 us (5%)
  local copies, waits for them, and re-layouts  6.47 us (4%)
    pallas_call x7, Pallas kernels, unit(): pl.pallas_call(functools.partial(unit_kernel, raw, two_tokens, two_states...  79.9 us
    ppermute x3, waiting for transfers between devices, gather_initial(): held = jnp.concatenate([held, lax.ppermute(held, 'seq', pairs)], axis=1)  29.1 us
    ppermute x10, starting transfers between devices, send(): return lax.ppermute(value, 'seq', pairs)  22.7 us
    pallas_call x3, Pallas kernels, pack(): pl.pallas_call(functools.partial(pack_kernel, tick), grid=(1,), in_specs=...  7.4 us
    unnamed x20, local copies, waits for them, and re-layouts  4.96 us
    ppermute x1, starting transfers between devices, gather_initial(): other = lax.ppermute(held, 'seq', [(0, 1), (1, 0)])  4.89 us
    ppermute x3, starting transfers between devices, gather_initial(): held = jnp.concatenate([held, lax.ppermute(held, 'seq', pairs)], axis=1)  4 us
    dynamic_update_slice x3, other arithmetic, body(): out = lax.dynamic_update_slice(out, r[None, None], (0, t, 0, 0))  3.59 us
  transfers between devices with their start and end apart: 14, of which 4 were waited for; matrix products, arithmetic and copies ran while one was open for 6% of the time, Pallas kernels for 53%

profile of v1, /device:TPU:1, one launch (start us, length us, event | category | flops | bytes accessed | tf_op | source)
XLA Modules:
  0.0 164.6 jit_solution(9565927730362921048)
XLA Ops:
  0.0 1.3 collective-permute-start.1
  1.3 6.9 %collective-permute-done.1 = bf16[3,64,512]{2,1,0:T(8,128)(2,1)S(1)} collective-permute-done((bf16[3,64,512]{2,1,0:T(8,128)(2,1)}, bf16[3,64,512]{2,1,0:T(8,128)(2,1)S(1)}, u32[]{:S(2)}, u32[]{:S(2)}) %collective-permute-start.1) | collective-permute-done | bytes 196640 | tf_op jit(solution)/shard_map/ppermute | solution.py:198
  8.2 0.0 copy-start.4
  8.2 1.0 pad_maximum_fusion.2
  9.2 1.3 collective-permute-start.2
  10.5 10.0 %collective-permute-done.2 = bf16[3,128,512]{2,1,0:T(8,128)(2,1)S(1)} collective-permute-done((bf16[3,128,512]{2,1,0:T(8,128)(2,1)S(1)}, bf16[3,128,512]{2,1,0:T(8,128)(2,1)S(1)}, u32[]{:S(2)}, u32[]{:S(2)}) %collective-permute-start.2) | collective-permute-done | bytes 393248 | tf_op jit(solution)/shard_map/ppermute | solution.py:198
  20.6 1.0 pad_maximum_fusion.1
  21.5 0.0 copy-start.3
  21.6 1.4 collective-permute-start.3
  23.0 2.4 %pack1.1.refs_0_ = bf16[3,384,512]{2,1,0:T(8,128)(2,1)} custom-call(bf16[1,4,384,512]{3,2,1,0:T(8,128)(2,1)} %k_ref.5, bf16[1,4,384,512]{3,2,1,0:T(8,128)(2,1)} %v_ref.5, bf16[1,4,384,512]{3,2,1,0:T(8,128)(2,1)} %q_ref.5, bf16[1,4,384]{2,1,0:T(4,128)(2,1)} %r_ref.5), custom_call_target="tpu_custom_call" | custom-call | tf_op jit(solution)/shard_map/pack1/pallas_call | solution.py:48
  25.4 4.0 %collective-permute-start.5 = (bf16[3,384,512]{2,1,0:T(8,128)(2,1)}, bf16[3,384,512]{2,1,0:T(8,128)(2,1)S(1)}, u32[]{:S(2)}, u32[]{:S(2)}) collective-permute-start(bf16[3,384,512]{2,1,0:T(8,128)(2,1)} %pack1.1.refs_0_), channel_id=1, source_target_pairs={{1,0},{2,1},{3,2},{4,3},{5,4},{6,5},{7,6},{8,7},{9,8},{10,9},{11,1... | collective-permute-start | bytes 3538952 | tf_op jit(solution)/shard_map/ppermute | solution.py:217
  29.4 12.1 %collective-permute-done.3 = bf16[3,256,512]{2,1,0:T(8,128)(2,1)S(1)} collective-permute-done((bf16[3,256,512]{2,1,0:T(8,128)(2,1)S(1)}, bf16[3,256,512]{2,1,0:T(8,128)(2,1)S(1)}, u32[]{:S(2)}, u32[]{:S(2)}) %collective-permute-start.3) | collective-permute-done | bytes 786464 | tf_op jit(solution)/shard_map/ppermute | solution.py:198
  41.5 0.0 copy-done.4
  41.5 0.0 copy-done.3
  41.5 0.0 copy-start.5
  41.5 1.4 pad_maximum_fusion
  42.9 0.1 copy-done.5
  43.0 4.9 %collective-permute-start.4 = (bf16[3,512,512]{2,1,0:T(8,128)(2,1)}, bf16[3,512,512]{2,1,0:T(8,128)(2,1)}, u32[]{:S(2)}, u32[]{:S(2)}) collective-permute-start(bf16[3,512,512]{2,1,0:T(8,128)(2,1)} %pad_maximum_fusion), channel_id=1, source_target_pairs={{0,1},{1,0},{16,17},{17,16}} | collective-permute-start | bytes 4718600 | tf_op jit(solution)/shard_map/ppermute | solution.py:200
  47.9 2.5 %pack2.1 = bf16[3,384,512]{2,1,0:T(8,128)(2,1)} custom-call(bf16[1,4,384,512]{3,2,1,0:T(8,128)(2,1)} %k_ref.5, bf16[1,4,384,512]{3,2,1,0:T(8,128)(2,1)} %v_ref.5, bf16[1,4,384,512]{3,2,1,0:T(8,128)(2,1)} %q_ref.5, bf16[1,4,384]{2,1,0:T(4,128)(2,1)} %r_ref.5), custom_call_target="tpu_custom_call" | custom-call | tf_op jit(solution)/shard_map/pack2/pallas_call | solution.py:48
  50.4 1.9 %collective-permute-start = (bf16[3,384,512]{2,1,0:T(8,128)(2,1)}, bf16[3,384,512]{2,1,0:T(8,128)(2,1)}, u32[]{:S(2)}, u32[]{:S(2)}) collective-permute-start(bf16[3,384,512]{2,1,0:T(8,128)(2,1)} %pack2.1), channel_id=1, source_target_pairs={{1,0},{0,1},{17,16},{16,17}} | collective-permute-start | bytes 3538952 | tf_op jit(solution)/shard_map/ppermute | solution.py:217
  52.4 1.3 collective-permute-start.7
  53.6 2.4 %pack3.1.refs_1_ = bf16[3,384,512]{2,1,0:T(8,128)(2,1)} custom-call(bf16[1,4,384,512]{3,2,1,0:T(8,128)(2,1)} %k_ref.5, bf16[1,4,384,512]{3,2,1,0:T(8,128)(2,1)} %v_ref.5, bf16[1,4,384,512]{3,2,1,0:T(8,128)(2,1)} %q_ref.5, bf16[1,4,384]{2,1,0:T(4,128)(2,1)} %r_ref.5), custom_call_target="tpu_custom_call" | custom-call | tf_op jit(solution)/shard_map/pack3/pallas_call | solution.py:48
  56.1 1.3 collective-permute-start.10
  57.4 0.0 collective-permute-done.5.refs_0_
  57.4 0.0 copy-start.6
  57.4 1.3 collective-permute-start.12
  58.7 11.3 %u0.1 = (bf16[3,1024,512]{2,1,0:T(8,128)(2,1)}, bf16[1,4,384,512]{3,2,1,0:T(8,128)(2,1)}) custom-call(s32[3]{0:T(128)} %constant.6.clone.1.flags_ref, bf16[1,4,384,512]{3,2,1,0:T(8,128)(2,1)} %k_ref.5, bf16[1,4,384,512]{3,2,1,0:T(8,128)(2,1)} %v_ref.5, bf16[1,4,384,512]{3,2,1,0:T(8,128)(2,1)} %q_ref.5, bf16[1,4,384]{2,1,0:T(4,128)(2,1)} %r_ref.5, ...), custom_call_target="tpu_custom_call" | custom-call | tf_op jit(solution)/shard_map/u0/pallas_call | solution.py:165
  70.0 0.0 copy-done.6
  70.0 0.6 pad_add_fusion.flags_ref
  70.6 0.9 constant_dynamic-update-slice_fusion.4
  71.5 0.9 constant_dynamic-update-slice_fusion.3
  72.5 11.1 %u1_.1 = (bf16[3,1024,512]{2,1,0:T(8,128)(2,1)}, bf16[384,512]{1,0:T(8,128)(2,1)}) custom-call(s32[3]{0:T(128)} %constant.6.clone.1.flags_ref, bf16[3,384,512]{2,1,0:T(8,128)(2,1)} %copy-done.6, bf16[3,1024,512]{2,1,0:T(8,128)(2,1)} %get-tuple-element.18.refs_1_, bf16[1,4,384,512]{3,2,1,0:T(8,128)(2,1)} %get-tuple-element.17.refs_2_), custom_call_target="tpu_custom_call" | custom-call | tf_op jit(solution)/shard_map/u1/pallas_call | solution.py:165
  83.7 1.2 constant_dynamic-update-slice_fusion.1
  84.8 0.0 collective-permute-done.4
  84.9 5.8 %collective-permute-start.6 = (bf16[384,512]{1,0:T(8,128)(2,1)}, bf16[384,512]{1,0:T(8,128)(2,1)}, u32[]{:S(2)}, u32[]{:S(2)}) collective-permute-start(bf16[384,512]{1,0:T(8,128)(2,1)} %get-tuple-element.19.refs_3_), channel_id=1, source_target_pairs={{0,1},{1,2},{2,3},{3,4},{4,5},{5,6},{6,7},{7,8},{8,9},{9,10},{10,1... | collective-permute-start | bytes 1179656 | tf_op jit(solution)/shard_map/ppermute | solution.py:217
  90.7 1.5 constant_dynamic-update-slice_fusion.refs_2_
  92.2 0.0 copy-start
  92.2 0.0 collective-permute-done.refs_1_.refs_0_
  92.2 1.7 %copy-done = bf16[3,1024,512]{2,1,0:T(8,128)(2,1)} copy-done((bf16[3,1024,512]{2,1,0:T(8,128)(2,1)}, bf16[3,1024,512]{2,1,0:T(8,128)(2,1)S(1)}, u32[]{:S(2)}) %copy-start) | copy-done | bytes 3145752
  94.0 11.7 %e1.1 = (bf16[3,1024,512]{2,1,0:T(8,128)(2,1)}, bf16[384,512]{1,0:T(8,128)(2,1)}) custom-call(s32[3]{0:T(128)} %pad_add_fusion.flags_ref, bf16[3,384,512]{2,1,0:T(8,128)(2,1)} %pack1.1.refs_0_, bf16[3,384,512]{2,1,0:T(8,128)(2,1)} %collective-permute-done.refs_1_.refs_0_, bf16[3,1024,512]{2,1,0:T(8,128)(2,1)} %copy-done, ...), custom_call_target="tpu_custom_call" | custom-call | tf_op jit(solution)/shard_map/e1/pallas_call | solution.py:165
  105.7 0.0 collective-permute-done.7.refs_0_
  105.7 11.2 %u2_.1 = (bf16[3,1024,512]{2,1,0:T(8,128)(2,1)}, bf16[384,512]{1,0:T(8,128)(2,1)}) custom-call(s32[3]{0:T(128)} %constant.6.clone.1.flags_ref, bf16[3,384,512]{2,1,0:T(8,128)(2,1)} %collective-permute-done.7.refs_0_, bf16[3,1024,512]{2,1,0:T(8,128)(2,1)} %get-tuple-element.22.refs_1_, bf16[384,512]{1,0:T(8,128)(2,1)} %get-tuple-element.20.refs_2_), custom_call_target="tpu_custom_call" | custom-call | tf_op jit(solution)/shard_map/u2/pallas_call | solution.py:165
  116.8 0.0 copy-start.2
  116.8 11.8 %e2.1 = (bf16[3,1024,512]{2,1,0:T(8,128)(2,1)}, bf16[384,512]{1,0:T(8,128)(2,1)}) custom-call(s32[3]{0:T(128)} %pad_add_fusion.flags_ref, bf16[3,384,512]{2,1,0:T(8,128)(2,1)} %collective-permute-done.refs_1_.refs_0_, bf16[3,384,512]{2,1,0:T(8,128)(2,1)} %pack3.1.refs_1_, bf16[3,1024,512]{2,1,0:T(8,128)(2,1)} %get-tuple-element.21.refs_2_, ...), custom_call_target="tpu_custom_call" | custom-call | tf_op jit(solution)/shard_map/e2/pallas_call | solution.py:165
  128.6 0.0 copy-done.2
  128.6 0.1 broadcast_select_fusion
  128.7 1.9 %collective-permute-start.8 = (bf16[384,512]{1,0:T(8,128)(2,1)S(1)}, bf16[384,512]{1,0:T(8,128)(2,1)S(1)}, u32[]{:S(2)}, u32[]{:S(2)}) collective-permute-start(bf16[384,512]{1,0:T(8,128)(2,1)S(1)} %broadcast_select_fusion), channel_id=1, source_target_pairs={{0,1},{1,0},{16,17},{17,16}} | collective-permute-start | bytes 1179656 | tf_op jit(solution)/shard_map/ppermute | solution.py:217
  130.6 0.0 copy-done.7
  130.6 1.3 collective-permute-start.9
  132.0 0.0 collective-permute-done.10.refs_0_
  132.0 11.6 %e3.1 = (bf16[3,1024,512]{2,1,0:T(8,128)(2,1)}, bf16[384,512]{1,0:T(8,128)(2,1)}) custom-call(s32[3]{0:T(128)} %pad_add_fusion.flags_ref, bf16[3,384,512]{2,1,0:T(8,128)(2,1)} %collective-permute-done.10.refs_0_, bf16[3,1024,512]{2,1,0:T(8,128)(2,1)} %get-tuple-element.25.refs_1_, bf16[3,1024,512]{2,1,0:T(8,128)(2,1)} %copy-done, ...), custom_call_target="tpu_custom_call" | custom-call | tf_op jit(solution)/shard_map/e3/pallas_call | solution.py:165
  143.6 2.4 %collective-permute-start.11 = (bf16[384,512]{1,0:T(8,128)(2,1)}, bf16[384,512]{1,0:T(8,128)(2,1)S(1)}, u32[]{:S(2)}, u32[]{:S(2)}) collective-permute-start(bf16[384,512]{1,0:T(8,128)(2,1)} %get-tuple-element.26.refs_2_), channel_id=1, source_target_pairs={{0,2},{1,0},{16,18},{17,16}} | collective-permute-start | bytes 1179656 | tf_op jit(solution)/shard_map/ppermute | solution.py:217
  146.0 0.0 collective-permute-done.12.refs_0_
  146.0 11.2 %u3.1 = (bf16[3,1024,512]{2,1,0:T(8,128)(2,1)}, bf16[384,512]{1,0:T(8,128)(2,1)}) custom-call(s32[3]{0:T(128)} %constant.6.clone.1.flags_ref, bf16[3,384,512]{2,1,0:T(8,128)(2,1)} %collective-permute-done.12.refs_0_, bf16[3,1024,512]{2,1,0:T(8,128)(2,1)} %get-tuple-element.27.refs_1_, bf16[384,512]{1,0:T(8,128)(2,1)} %get-tuple-element.26.refs_2_), custom_call_target="tpu_custom_call" | custom-call | tf_op jit(solution)/shard_map/u3/pallas_call | solution.py:165
  157.2 1.4 collective-permute-start.13
  158.7 0.0 collective-permute-done.6
  158.7 1.8 %bitcast_dynamic-update-slice_fusion.2 = bf16[1,4,384,512]{3,2,1,0:T(8,128)(2,1)} fusion(bf16[1,4,384,512]{3,2,1,0:T(8,128)(2,1)} %get-tuple-element.17.refs_2_, bf16[384,512]{1,0:T(8,128)(2,1)S(1)} %copy-done.2, bf16[384,512]{1,0:T(8,128)(2,1)} %collective-permute-done.6, pred[]{:T(512)S(6)} %ne.10), kind=kLoop, calls=%fused_computation.5 | loop fusion | flops 196608 | bytes 1179649 | tf_op jit(solution)/shard_map/dynamic_update_slice | solution.py:250
  160.5 0.0 collective-permute-done.8
  160.5 0.0 collective-permute-done.9
  160.5 0.8 bitcast_dynamic-update-slice_fusion.1
  161.4 2.3 %collective-permute-done.13 = bf16[384,512]{1,0:T(8,128)(2,1)S(1)} collective-permute-done((bf16[384,512]{1,0:T(8,128)(2,1)}, bf16[384,512]{1,0:T(8,128)(2,1)S(1)}, u32[]{:S(2)}, u32[]{:S(2)}) %collective-permute-start.13) | collective-permute-done | bytes 393248 | tf_op jit(solution)/shard_map/ppermute | solution.py:217
  163.7 0.0 collective-permute-done.11
  163.7 0.0 copy-done.1
  163.7 0.9 bitcast_dynamic-update-slice_fusion
  (3 shorter events, 0.0 us)
Async XLA Ops:
  0.0 8.2 %collective-permute-start.1 = (bf16[3,64,512]{2,1,0:T(8,128)(2,1)}, bf16[3,64,512]{2,1,0:T(8,128)(2,1)S(1)}, u32[]{:S(2)}, u32[]{:S(2)}) collective-permute-start(bf16[3,64,512]{2,1,0:T(8,128)(2,1)} %param.7), channel_id=1, source_target_pairs={{2,0},{3,1},{6,4},{7,5},{10,8},{11,9},{14,12},{15,13},{18,16},{19,... | collective-permute-start | bytes 589832 | tf_op jit(solution)/shard_map/ppermute | solution.py:198
  8.2 33.4 %copy-start.4 = (bf16[3,64,512]{2,1,0:T(8,128)(2,1)}, bf16[3,64,512]{2,1,0:T(8,128)(2,1)S(1)}, u32[]{:S(2)}) copy-start(bf16[3,64,512]{2,1,0:T(8,128)(2,1)S(1)} %collective-permute-done.1) | copy-start | bytes 589828
  9.2 11.3 %collective-permute-start.2 = (bf16[3,128,512]{2,1,0:T(8,128)(2,1)S(1)}, bf16[3,128,512]{2,1,0:T(8,128)(2,1)S(1)}, u32[]{:S(2)}, u32[]{:S(2)}) collective-permute-start(bf16[3,128,512]{2,1,0:T(8,128)(2,1)S(1)} %pad_maximum_fusion.2), channel_id=1, source_target_pairs={{4,0},{5,1},{12,8},{13,9},{20,16},{21,17},{28,24},{29,25}} | collective-permute-start | bytes 1179656 | tf_op jit(solution)/shard_map/ppermute | solution.py:198
  21.5 20.0 %copy-start.3 = (bf16[3,64,512]{2,1,0:T(8,128)(2,1)S(1)}, bf16[3,64,512]{2,1,0:T(8,128)(2,1)}, u32[]{:S(2)}) copy-start(bf16[3,64,512]{2,1,0:T(8,128)(2,1)} %param.7) | copy-start | bytes 589828
  21.6 20.0 %collective-permute-start.3 = (bf16[3,256,512]{2,1,0:T(8,128)(2,1)S(1)}, bf16[3,256,512]{2,1,0:T(8,128)(2,1)S(1)}, u32[]{:S(2)}, u32[]{:S(2)}) collective-permute-start(bf16[3,256,512]{2,1,0:T(8,128)(2,1)S(1)} %pad_maximum_fusion.1), channel_id=1, source_target_pairs={{8,0},{9,1},{24,16},{25,17}} | collective-permute-start | bytes 2359304 | tf_op jit(solution)/shard_map/ppermute | solution.py:198
  25.4 32.0 %collective-permute-start.5 = (bf16[3,384,512]{2,1,0:T(8,128)(2,1)}, bf16[3,384,512]{2,1,0:T(8,128)(2,1)S(1)}, u32[]{:S(2)}, u32[]{:S(2)}) collective-permute-start(bf16[3,384,512]{2,1,0:T(8,128)(2,1)} %pack1.1.refs_0_), channel_id=1, source_target_pairs={{1,0},{2,1},{3,2},{4,3},{5,4},{6,5},{7,6},{8,7},{9,8},{10,9},{11,1... | collective-permute-start | bytes 3538952 | tf_op jit(solution)/shard_map/ppermute | solution.py:217
  41.5 1.5 copy-start.5
  43.0 41.8 %collective-permute-start.4 = (bf16[3,512,512]{2,1,0:T(8,128)(2,1)}, bf16[3,512,512]{2,1,0:T(8,128)(2,1)}, u32[]{:S(2)}, u32[]{:S(2)}) collective-permute-start(bf16[3,512,512]{2,1,0:T(8,128)(2,1)} %pad_maximum_fusion), channel_id=1, source_target_pairs={{0,1},{1,0},{16,17},{17,16}} | collective-permute-start | bytes 4718600 | tf_op jit(solution)/shard_map/ppermute | solution.py:200
  50.4 41.8 %collective-permute-start = (bf16[3,384,512]{2,1,0:T(8,128)(2,1)}, bf16[3,384,512]{2,1,0:T(8,128)(2,1)}, u32[]{:S(2)}, u32[]{:S(2)}) collective-permute-start(bf16[3,384,512]{2,1,0:T(8,128)(2,1)} %pack2.1), channel_id=1, source_target_pairs={{1,0},{0,1},{17,16},{16,17}} | collective-permute-start | bytes 3538952 | tf_op jit(solution)/shard_map/ppermute | solution.py:217
  52.4 53.3 %collective-permute-start.7 = (bf16[3,384,512]{2,1,0:T(8,128)(2,1)}, bf16[3,384,512]{2,1,0:T(8,128)(2,1)}, u32[]{:S(2)}, u32[]{:S(2)}) collective-permute-start(bf16[3,384,512]{2,1,0:T(8,128)(2,1)} %pack2.1), channel_id=1, source_target_pairs={{2,0},{3,1},{4,2},{5,3},{6,4},{7,5},{8,6},{9,7},{10,8},{11,9},{12,... | collective-permute-start | bytes 3538952 | tf_op jit(solution)/shard_map/ppermute | solution.py:217
  56.1 75.9 %collective-permute-start.10 = (bf16[3,384,512]{2,1,0:T(8,128)(2,1)}, bf16[3,384,512]{2,1,0:T(8,128)(2,1)}, u32[]{:S(2)}, u32[]{:S(2)}) collective-permute-start(bf16[3,384,512]{2,1,0:T(8,128)(2,1)} %pack3.1.refs_1_), channel_id=1, source_target_pairs={{2,0},{0,1},{18,16},{16,17}} | collective-permute-start | bytes 3538952 | tf_op jit(solution)/shard_map/ppermute | solution.py:217
  57.4 12.6 %copy-start.6 = (bf16[3,384,512]{2,1,0:T(8,128)(2,1)}, bf16[3,384,512]{2,1,0:T(8,128)(2,1)S(1)}, u32[]{:S(2)}) copy-start(bf16[3,384,512]{2,1,0:T(8,128)(2,1)S(1)} %collective-permute-done.5.refs_0_) | copy-start | bytes 3538948
  57.4 88.6 %collective-permute-start.12 = (bf16[3,384,512]{2,1,0:T(8,128)(2,1)}, bf16[3,384,512]{2,1,0:T(8,128)(2,1)}, u32[]{:S(2)}, u32[]{:S(2)}) collective-permute-start(bf16[3,384,512]{2,1,0:T(8,128)(2,1)} %pack3.1.refs_1_), channel_id=1, source_target_pairs={{3,0},{4,1},{5,2},{6,3},{7,4},{8,5},{9,6},{10,7},{11,8},{12,9},{13... | collective-permute-start | bytes 3538952 | tf_op jit(solution)/shard_map/ppermute | solution.py:217
  84.9 73.8 %collective-permute-start.6 = (bf16[384,512]{1,0:T(8,128)(2,1)}, bf16[384,512]{1,0:T(8,128)(2,1)}, u32[]{:S(2)}, u32[]{:S(2)}) collective-permute-start(bf16[384,512]{1,0:T(8,128)(2,1)} %get-tuple-element.19.refs_3_), channel_id=1, source_target_pairs={{0,1},{1,2},{2,3},{3,4},{4,5},{5,6},{6,7},{7,8},{8,9},{9,10},{10,1... | collective-permute-start | bytes 1179656 | tf_op jit(solution)/shard_map/ppermute | solution.py:217
  92.2 1.7 %copy-start = (bf16[3,1024,512]{2,1,0:T(8,128)(2,1)}, bf16[3,1024,512]{2,1,0:T(8,128)(2,1)S(1)}, u32[]{:S(2)}) copy-start(bf16[3,1024,512]{2,1,0:T(8,128)(2,1)S(1)} %constant_dynamic-update-slice_fusion.refs_2_) | copy-start | bytes 9437188
  116.8 11.8 %copy-start.2 = (bf16[384,512]{1,0:T(8,128)(2,1)S(1)}, bf16[384,512]{1,0:T(8,128)(2,1)}, u32[]{:S(2)}) copy-start(bf16[384,512]{1,0:T(8,128)(2,1)} %get-tuple-element.20.refs_2_) | copy-start | bytes 1179652
  116.8 13.8 %copy-start.7 = (bf16[384,512]{1,0:T(8,128)(2,1)S(1)}, bf16[384,512]{1,0:T(8,128)(2,1)}, u32[]{:S(2)}) copy-start(bf16[384,512]{1,0:T(8,128)(2,1)} %get-tuple-element.23.refs_3_) | copy-start | bytes 1179652
  128.7 31.8 %collective-permute-start.8 = (bf16[384,512]{1,0:T(8,128)(2,1)S(1)}, bf16[384,512]{1,0:T(8,128)(2,1)S(1)}, u32[]{:S(2)}, u32[]{:S(2)}) collective-permute-start(bf16[384,512]{1,0:T(8,128)(2,1)S(1)} %broadcast_select_fusion), channel_id=1, source_target_pairs={{0,1},{1,0},{16,17},{17,16}} | collective-permute-start | bytes 1179656 | tf_op jit(solution)/shard_map/ppermute | solution.py:217
  130.6 29.9 %collective-permute-start.9 = (bf16[384,512]{1,0:T(8,128)(2,1)S(1)}, bf16[384,512]{1,0:T(8,128)(2,1)S(1)}, u32[]{:S(2)}, u32[]{:S(2)}) collective-permute-start(bf16[384,512]{1,0:T(8,128)(2,1)S(1)} %copy-done.7), channel_id=1, source_target_pairs={{0,2},{1,3},{2,4},{3,5},{4,6},{5,7},{6,8},{7,9},{8,10},{9,11},{10,... | collective-permute-start | bytes 1179656 | tf_op jit(solution)/shard_map/ppermute | solution.py:217
  143.6 20.1 %collective-permute-start.11 = (bf16[384,512]{1,0:T(8,128)(2,1)}, bf16[384,512]{1,0:T(8,128)(2,1)S(1)}, u32[]{:S(2)}, u32[]{:S(2)}) collective-permute-start(bf16[384,512]{1,0:T(8,128)(2,1)} %get-tuple-element.26.refs_2_), channel_id=1, source_target_pairs={{0,2},{1,0},{16,18},{17,16}} | collective-permute-start | bytes 1179656 | tf_op jit(solution)/shard_map/ppermute | solution.py:217
  157.2 6.4 %copy-start.1 = (bf16[384,512]{1,0:T(8,128)(2,1)S(1)}, bf16[384,512]{1,0:T(8,128)(2,1)}, u32[]{:S(2)}) copy-start(bf16[384,512]{1,0:T(8,128)(2,1)} %get-tuple-element.24.refs_3_) | copy-start | bytes 1179652
  157.2 6.4 %collective-permute-start.13 = (bf16[384,512]{1,0:T(8,128)(2,1)}, bf16[384,512]{1,0:T(8,128)(2,1)S(1)}, u32[]{:S(2)}, u32[]{:S(2)}) collective-permute-start(bf16[384,512]{1,0:T(8,128)(2,1)} %get-tuple-element.28), channel_id=1, source_target_pairs={{0,3},{1,4},{2,5},{3,6},{4,7},{5,8},{6,9},{7,10},{8,11},{9,12},{10... | collective-permute-start | bytes 1179656 | tf_op jit(solution)/shard_map/ppermute | solution.py:217

commit v2 on v0

v2 whole, which is shorter than its diff:
```python
import functools
import jax
import jax.numpy as jnp
from jax import lax
from jax.experimental import pallas as pl
from jax.experimental.pallas import tpu as pltpu
from jax.sharding import PartitionSpec as P

epsilon = 1e-06
f32 = jnp.float32
bf16 = jnp.bfloat16
HBM = pl.BlockSpec(memory_space=pltpu.HBM)
VMEM = pl.BlockSpec(memory_space=pltpu.VMEM)
SMEM = pl.BlockSpec(memory_space=pltpu.SMEM)
LIMIT = 28 << 20


def in_hbm(*arrays):
    return [pltpu.with_memory_space_constraint(a, pltpu.HBM) for a in arrays]


def nt(a, b):
    return lax.dot_general(a, b, (((1,), (1,)), ((), ())), preferred_element_type=f32)


def nn(a, b):
    return lax.dot_general(a, b, (((1,), (0,)), ((), ())), preferred_element_type=f32)


def sigmoid(x):
    return 0.5 * jnp.tanh(0.5 * x) + 0.5


def scaled_values(steps_row, values):
    lanes = 128
    span, width = values.shape
    column = jnp.broadcast_to(steps_row.astype(f32), (lanes, span)).T
    return jnp.concatenate(
        [
            (column * values[:, i : i + lanes].astype(f32)).astype(bf16)
            for i in range(0, width, lanes)
        ],
        axis=1,
    )


def pack_kernel(tick, k_ref, v_ref, q_ref, r_ref, o_ref, vals, sems):
    copies = [
        pltpu.make_async_copy(v_ref.at[0, tick], vals, sems.at[0]),
        pltpu.make_async_copy(k_ref.at[0, tick], o_ref.at[0], sems.at[1]),
        pltpu.make_async_copy(q_ref.at[0, tick], o_ref.at[2], sems.at[2]),
    ]
    for copy in copies:
        copy.start()
    copies[0].wait()
    vals[...] = scaled_values(r_ref[0, tick : tick + 1, :], vals[...])
    back = pltpu.make_async_copy(vals, o_ref.at[1], sems.at[3])
    back.start()
    copies[1].wait()
    copies[2].wait()
    back.wait()


def pack(tick, keys, values, queries, steps):
    _, _, span, width = keys.shape
    return pl.pallas_call(
        functools.partial(pack_kernel, tick),
        in_specs=[HBM, HBM, HBM, VMEM],
        out_specs=HBM,
        out_shape=jax.ShapeDtypeStruct((3, span, width), bf16),
        scratch_shapes=[pltpu.VMEM((span, width), bf16), pltpu.SemaphoreType.DMA((4,))],
        compiler_params=pltpu.CompilerParams(vmem_limit_bytes=LIMIT),
    )(*in_hbm(keys, values, queries), steps)


def step_rows(old, delta):
    previous = old.astype(f32)
    updated = previous + delta
    old_norm = jnp.sqrt(jnp.sum(previous * previous, axis=-1, keepdims=True) + epsilon)
    new_norm = jnp.sqrt(jnp.sum(updated * updated, axis=-1, keepdims=True) + epsilon)
    return (updated * (old_norm / new_norm)).astype(bf16)


def advance_rows(keys, target, gate, up, down):
    gate_pre = nt(gate, keys)
    up_pre = nt(up, keys)
    back_grad = nt(down, target)
    sig = sigmoid(gate_pre)
    silu = gate_pre * sig
    hidden = (silu * up_pre).astype(bf16)
    grad_up = (back_grad * silu).astype(bf16)
    grad_gate = ((back_grad * up_pre) * (sig * (1.0 + (gate_pre - silu)))).astype(bf16)
    return (
        step_rows(gate, nn(grad_gate, keys)),
        step_rows(up, nn(grad_up, keys)),
        step_rows(down, nn(hidden, target)),
    )


def serve_rows(queries, gate, up, down):
    c = nt(queries, gate)
    e = nt(queries, up)
    return nn((c * sigmoid(c) * e).astype(bf16), down)


def compute(tok, old, new_ref, acc, ans, block, wait_queries):
    count = new_ref.shape[1] // block

    @pl.loop(0, count)
    def _(j):
        rows = pl.ds(pl.multiple_of(j * block, block), block)
        new = advance_rows(tok[0], tok[1], old[0, rows], old[1, rows], old[2, rows])
        for i in range(3):
            new_ref[i, rows] = new[i]

        @pl.when(j == 0)
        def _():
            wait_queries()
            acc[...] = jnp.zeros_like(acc)

        acc[...] += serve_rows(
            tok[2], new_ref[0, rows], new_ref[1, rows], new_ref[2, rows]
        )

    ans[...] = acc[...].astype(bf16)


def unit_kernel(kind, n_tokens, n_states, n_pieces, n_carry, block, flags_ref, *refs):
    refs = list(refs)
    take = lambda n: [refs.pop(0) for _ in range(n)]
    tokens = take(4 if kind == "raw" else n_tokens)
    states = take(n_states)
    pieces = take(n_pieces)
    take(n_carry)
    new_ref, ans_out = take(2)
    take(n_carry)
    tok, acc, ans, sems = take(4)
    if kind == "extra":
        built, made = take(2)
        new_out, new_ref = new_ref, made

    def load(which):
        if kind == "raw":
            k_ref, v_ref, q_ref, _ = tokens
            sources = [k_ref.at[0, 0], v_ref.at[0, 0], q_ref.at[0, 0]]
        else:
            sources = [tokens[which].at[i] for i in range(3)]
        return [
            pltpu.make_async_copy(sources[i], tok.at[i], sems.at[i]) for i in range(3)
        ]

    def run():
        if n_tokens == 2:
            for which in range(2):
                @pl.when(flags_ref[1] == which)
                def _():
                    for copy in load(which):
                        copy.start()
        else:
            for copy in load(0):
                copy.start()
        if kind == "extra":
            def bring(group):
                rows = 0
                copies = []
                for n, piece in enumerate(group):
                    height = piece.shape[1]
                    part = built.at[:, pl.ds(rows, height)]
                    copies.append(pltpu.make_async_copy(piece, part, sems.at[5 + n]))
                    rows += height
                for copy in copies:
                    copy.start()
                for copy in copies:
                    copy.wait()

            if n_states:
                @pl.when(flags_ref[2] != 0)
                def _():
                    bring(pieces)

                @pl.when(flags_ref[2] == 0)
                def _():
                    bring(states)
            else:
                bring(pieces)
            old = built
        else:
            old = states[0]
        if len(old.shape) == 4:
            old = old.at[0]
        waits = load(0)
        waits[0].wait()
        waits[1].wait()
        if kind == "raw":
            tok[1] = scaled_values(tokens[3][0, 0:1, :], tok[1])
        compute(tok, old, new_ref, acc, ans, block, waits[2].wait)
        target = ans_out.at[0, 0] if kind == "raw" else ans_out
        out = pltpu.make_async_copy(ans, target, sems.at[3])
        out.start()
        if kind == "extra":
            keep = pltpu.make_async_copy(made, new_out, sems.at[4])
            keep.start()
            keep.wait()
        out.wait()

    if kind == "extra":
        @pl.when(flags_ref[0] != 0)
        def _():
            run()
    else:
        run()


def unit(kind, flags, tokens, states, pieces, carry, hid, block=512):
    span, width = tokens[0].shape[-2:]
    scratch = [
        pltpu.VMEM((3, span, width), bf16),
        pltpu.VMEM((span, width), f32),
        pltpu.VMEM((span, width), bf16),
        pltpu.SemaphoreType.DMA((5 + len(pieces),)),
    ]
    if kind == "extra":
        scratch += [pltpu.VMEM((3, hid, width), bf16)] * 2
    kept = HBM if kind == "extra" else VMEM
    token_specs = [HBM] * len(tokens)
    if kind == "raw":
        token_specs[3] = VMEM
    n_tokens = 1 if kind == "raw" else len(tokens)
    call = pl.pallas_call(
        functools.partial(
            unit_kernel, kind, n_tokens, len(states), len(pieces), len(carry), block
        ),
        in_specs=[SMEM]
        + token_specs
        + [kept] * len(states)
        + [HBM] * len(pieces)
        + [VMEM] * len(carry),
        out_specs=[kept, HBM] + [VMEM] * len(carry),
        out_shape=[
            jax.ShapeDtypeStruct((3, hid, width), bf16),
            jax.ShapeDtypeStruct(
                tokens[0].shape if kind == "raw" else (span, width), bf16
            ),
        ]
        + [jax.ShapeDtypeStruct(c.shape, c.dtype) for c in carry],
        input_output_aliases={
            1 + len(tokens) + len(states) + len(pieces) + n: 2 + n
            for n in range(len(carry))
        },
        scratch_shapes=scratch,
        compiler_params=pltpu.CompilerParams(vmem_limit_bytes=LIMIT),
    )
    if kind == "raw":
        tokens = in_hbm(*tokens[:3]) + tokens[3:]
    return call(flags, *tokens, *states, *pieces, *carry)


def tied(value, *deps):
    return lax.optimization_barrier((value,) + deps)[0]


def body(fast_state, initial_fast, queries, token_keys, token_values, step_sizes):
    count = lax.axis_size("seq")
    position = lax.axis_index("seq")
    hid = fast_state.shape[2]
    i32 = jnp.int32
    first = (position == 0).astype(i32)
    second = (position == 1).astype(i32)
    extra = first + second
    flags = jnp.stack([extra, second, second])

    def send(value, pairs):
        return lax.ppermute(value, "seq", pairs)

    down = lambda t: [(s, s - t) for s in range(t, count)]
    up = lambda t: [(s, s + t) for s in range(count - t)]

    args = (token_keys, token_values, queries, step_sizes)
    pack1, pack2, pack3 = [pack(t, *args) for t in (1, 2, 3)]
    tokens1 = send(pack1, down(1))
    tokens2 = send(pack2, down(2))
    cross2 = send(pack2, [(1, 0), (0, 1)])
    tokens3 = send(pack3, down(3))
    cross3 = send(pack3, [(2, 0), (0, 1)])

    held = tied(initial_fast, pack3)
    chips = count // 2
    levels = []
    while chips > 1:
        radix = 4 if chips % 4 == 0 else 2
        chips //= radix
        levels.append((2 * chips, radix))

    def gather_level(value, stride, radix):
        return [
            send(value, [(j * stride + i, i) for i in range(stride)])
            for j in range(1, radix)
        ]

    got = gather_level(held, *levels[0])
    state, out = unit("raw", flags, list(args), [fast_state], [], [], hid)
    for level in levels[1:]:
        got = list(tied(tuple(got), out))
        held = jnp.concatenate([held] + got, axis=1)
        got = gather_level(held, *level)

    s1, a1 = unit("next", flags, [tokens1], [state], [], [], hid)
    b1 = send(a1, up(1))
    got = list(tied(tuple(got), a1))
    mine = [held] + got
    pieces = mine + [send(piece, [(0, 1), (1, 0)]) for piece in mine]
    e1, x1, s1 = unit("extra", flags, [pack1, cross2], [], pieces, [s1], hid)
    s2, a2 = unit("next", flags, [tokens2], [s1], [], [], hid)
    b2 = send(a2, up(2))
    e2, x2, s2 = unit("extra", flags, [cross2, pack3], [], [e1], [s2], hid)
    c2 = send(jnp.where(first != 0, x2, x1), [(0, 1), (1, 0)])
    _, x3, s2 = unit("extra", flags, [cross3], [e2], pieces, [s2], hid)
    c3 = send(x3, [(0, 2), (1, 0)])
    _, a3 = unit("next", flags, [tokens3], [s2], [], [], hid)
    b3 = send(a3, up(3))

    r1 = jnp.where(first != 0, x1, b1)
    r2 = jnp.where(extra != 0, c2, b2)
    early3 = jnp.where(second != 0, x2, c3)
    r3 = jnp.where(position < 3, early3, b3)
    for t, r in ((1, r1), (2, r2), (3, r3)):
        out = lax.dynamic_update_slice(out, r[None, None], (0, t, 0, 0))
    return out


def solution(mesh):
    return jax.shard_map(
        body,
        mesh=mesh,
        in_specs=(
            P(("grp", "seq"), None, None, None),
            P(None, "seq", None),
            P(("grp", "seq"), None, None, None),
            P(("grp", "seq"), None, None, None),
            P(("grp", "seq"), None, None, None),
            P(("grp", "seq"), None, None),
        ),
        out_specs=P(("grp", "seq"), None, None, None),
        check_vma=False,
    )
```

time: 197 us -> 181 us (0.919)
  the two profiles are of different devices: /device:TPU:1 before, /device:TPU:6 now
where the time goes in v2:
time: 181 us; the launch traced here: 179 us
  Pallas kernels  92.4 us (51%)
  starting transfers between devices  31.9 us (18%)
  waiting for transfers between devices  30.5 us (17%)
  local copies, waits for them, and re-layouts  18.7 us (10%)
  other arithmetic  5.45 us (3%)
    pallas_call x3, Pallas kernels, pack(): pl.pallas_call(functools.partial(pack_kernel, tick), in_specs=[HBM, HBM,...  51.3 us
    pallas_call x7, Pallas kernels, unit(): return call(flags, *tokens, *states, *pieces, *carry)  41.1 us
    ppermute x16, starting transfers between devices, send(): return lax.ppermute(value, 'seq', pairs)  31.9 us
    ppermute x16, waiting for transfers between devices, send(): return lax.ppermute(value, 'seq', pairs)  30.5 us
    unnamed x43, local copies, waits for them, and re-layouts  18.7 us
    dynamic_update_slice x3, other arithmetic, body(): out = lax.dynamic_update_slice(out, r[None, None], (0, t, 0, 0))  4.58 us
  transfers between devices with their start and end apart: 16, of which 5 were waited for; matrix products, arithmetic and copies ran while one was open for 3% of the time, Pallas kernels for 38%

profile of v2, /device:TPU:6, one launch (start us, length us, event | category | flops | bytes accessed | tf_op | source)
XLA Modules:
  0.0 179.4 jit_solution(10588923900874321948)
XLA Ops:
  0.0 0.7 copy-done.17
  0.7 25.0 %shard_map.67.refs_1_ = bf16[3,384,512]{2,1,0:T(8,128)(2,1)} custom-call(bf16[1,4,384,512]{3,2,1,0:T(8,128)(2,1)} %k_ref.5, bf16[1,4,384,512]{3,2,1,0:T(8,128)(2,1)} %v_ref.5, bf16[1,4,384,512]{3,2,1,0:T(8,128)(2,1)} %q_ref.5, bf16[1,4,384]{2,1,0:T(4,128)(2,1)S(1)} %copy-done.17), custom_call_target="tpu_custom_call" | custom-call | tf_op jit(solution)/shard_map/pallas_call | solution.py:66
  25.7 0.0 copy-start.18
  25.7 1.3 collective-permute-start.1
  27.0 1.3 collective-permute-start.2
  28.3 1.3 collective-permute-start.3
  29.6 1.4 shard_map.65.refs_0_
  31.0 1.9 %collective-permute-start.5 = (bf16[3,384,512]{2,1,0:T(8,128)(2,1)S(1)}, bf16[3,384,512]{2,1,0:T(8,128)(2,1)S(1)}, u32[]{:S(2)}, u32[]{:S(2)}) collective-permute-start(bf16[3,384,512]{2,1,0:T(8,128)(2,1)S(1)} %shard_map.65.refs_0_), channel_id=1, source_target_pairs={{1,0},{2,1},{3,2},{4,3},{5,4},{6,5},{7,6},{8,7},{9,8},{10,9},{11,1... | collective-permute-start | bytes 3538952 | tf_op jit(solution)/shard_map/ppermute | solution.py:273
  32.9 0.1 pad_add_fusion.flags_ref
  33.0 0.0 copy-done.18
  33.0 1.9 %copy-done.7 = bf16[1,3,1024,512]{3,2,1,0:T(8,128)(2,1)S(1)} copy-done((bf16[1,3,1024,512]{3,2,1,0:T(8,128)(2,1)S(1)}, bf16[1,3,1024,512]{3,2,1,0:T(8,128)(2,1)}, u32[]{:S(2)}) %copy-start.7) | copy-done | bytes 3145752
  34.9 9.6 %shard_map.64 = (bf16[3,1024,512]{2,1,0:T(8,128)(2,1)S(1)}, bf16[1,4,384,512]{3,2,1,0:T(8,128)(2,1)}) custom-call(s32[3]{0:T(128)S(1)} %pad_add_fusion.flags_ref, bf16[1,4,384,512]{3,2,1,0:T(8,128)(2,1)} %k_ref.5, bf16[1,4,384,512]{3,2,1,0:T(8,128)(2,1)} %v_ref.5, bf16[1,4,384,512]{3,2,1,0:T(8,128)(2,1)} %q_ref.5, bf16[1,4,384]{2,1,0:T(4,128)(2,1)S(1)} %copy-done.18, ...), custom_call_target="tpu_custom_call" | custom-call | tf_op jit(solution)/shard_map/pallas_call | solution.py:255
  44.6 0.0 collective-permute-done.1
  44.6 0.0 collective-permute-done.2
  44.6 0.0 collective-permute-done.3
  44.7 2.7 %collective-permute-start.4 = (bf16[3,256,512]{2,1,0:T(8,128)(2,1)S(1)}, bf16[3,256,512]{2,1,0:T(8,128)(2,1)}, u32[]{:S(2)}, u32[]{:S(2)}) collective-permute-start(bf16[3,256,512]{2,1,0:T(8,128)(2,1)S(1)} %constant_dynamic-update-slice_fusion.refs_2_), channel_id=1, source_target_pairs={{2,0},{3,1},{18,16},{19,17}} | collective-permute-start | bytes 2359304 | tf_op jit(solution)/shard_map/ppermute | solution.py:273
  47.4 0.7 collective-permute-start.6
  48.1 25.0 %shard_map.66 = bf16[3,384,512]{2,1,0:T(8,128)(2,1)} custom-call(bf16[1,4,384,512]{3,2,1,0:T(8,128)(2,1)} %k_ref.5, bf16[1,4,384,512]{3,2,1,0:T(8,128)(2,1)} %v_ref.5, bf16[1,4,384,512]{3,2,1,0:T(8,128)(2,1)} %q_ref.5, bf16[1,4,384]{2,1,0:T(4,128)(2,1)S(1)} %copy-done.18), custom_call_target="tpu_custom_call" | custom-call | tf_op jit(solution)/shard_map/pallas_call | solution.py:66
  73.0 1.7 collective-permute-start
  74.8 3.0 %collective-permute-start.9 = (bf16[3,384,512]{2,1,0:T(8,128)(2,1)}, bf16[3,384,512]{2,1,0:T(8,128)(2,1)}, u32[]{:S(2)}, u32[]{:S(2)}) collective-permute-start(bf16[3,384,512]{2,1,0:T(8,128)(2,1)} %shard_map.66), channel_id=1, source_target_pairs={{2,0},{3,1},{4,2},{5,3},{6,4},{7,5},{8,6},{9,7},{10,8},{11,9},{12,... | collective-permute-start | bytes 3538952 | tf_op jit(solution)/shard_map/ppermute | solution.py:273
  77.8 0.0 collective-permute-done.5.refs_0_
  77.8 1.0 copy-done.15
  78.8 2.3 %collective-permute-start.12 = (bf16[3,384,512]{2,1,0:T(8,128)(2,1)}, bf16[3,384,512]{2,1,0:T(8,128)(2,1)}, u32[]{:S(2)}, u32[]{:S(2)}) collective-permute-start(bf16[3,384,512]{2,1,0:T(8,128)(2,1)} %shard_map.67.refs_1_), channel_id=1, source_target_pairs={{2,0},{0,1},{18,16},{16,17}} | collective-permute-start | bytes 3538952 | tf_op jit(solution)/shard_map/ppermute | solution.py:273
  81.1 1.3 copy-done.16
  82.4 9.0 %shard_map.68 = (bf16[3,1024,512]{2,1,0:T(8,128)(2,1)S(1)}, bf16[384,512]{1,0:T(8,128)(2,1)}) custom-call(s32[3]{0:T(128)S(1)} %pad_add_fusion.flags_ref, bf16[3,384,512]{2,1,0:T(8,128)(2,1)S(1)} %copy-done.16, bf16[3,1024,512]{2,1,0:T(8,128)(2,1)S(1)} %get-tuple-element.30.refs_1_), custom_call_target="tpu_custom_call" | custom-call | tf_op jit(solution)/shard_map/pallas_call | solution.py:255
  91.4 0.0 collective-permute-done.4.refs_3_
  91.4 1.6 collective-permute-start.7
  93.0 0.0 collective-permute-done.6.refs_4_
  93.0 0.9 copy-done.10
  94.0 1.3 collective-permute-start.14
  95.2 0.0 collective-permute-done.refs_1_.refs_0_
  95.3 2.4 %collective-permute-start.8 = (bf16[384,512]{1,0:T(8,128)(2,1)}, bf16[384,512]{1,0:T(8,128)(2,1)}, u32[]{:S(2)}, u32[]{:S(2)}) collective-permute-start(bf16[384,512]{1,0:T(8,128)(2,1)} %get-tuple-element.31), channel_id=1, source_target_pairs={{0,1},{1,2},{2,3},{3,4},{4,5},{5,6},{6,7},{7,8},{8,9},{9,10},{10,1... | collective-permute-start | bytes 1179656 | tf_op jit(solution)/shard_map/ppermute | solution.py:273
  97.7 0.0 collective-permute-done.7.refs_5_
  97.7 1.3 copy-done.3
  99.0 1.1 copy-done.5
  100.1 1.1 copy-done.11
  101.3 0.8 shard_map.69
  102.1 0.0 copy-start
  102.1 1.6 copy-done
  103.8 3.0 %collective-permute-done.9.refs_0_ = bf16[3,384,512]{2,1,0:T(8,128)(2,1)} collective-permute-done((bf16[3,384,512]{2,1,0:T(8,128)(2,1)}, bf16[3,384,512]{2,1,0:T(8,128)(2,1)}, u32[]{:S(2)}, u32[]{:S(2)}) %collective-permute-start.9) | collective-permute-done | bytes 1179680 | tf_op jit(solution)/shard_map/ppermute | solution.py:273
  106.8 1.9 %copy-done.1 = bf16[3,1024,512]{2,1,0:T(8,128)(2,1)S(1)} copy-done((bf16[3,1024,512]{2,1,0:T(8,128)(2,1)S(1)}, bf16[3,1024,512]{2,1,0:T(8,128)(2,1)}, u32[]{:S(2)}) %copy-start.1) | copy-done | bytes 3145752
  108.7 9.6 %shard_map.70 = (bf16[3,1024,512]{2,1,0:T(8,128)(2,1)S(1)}, bf16[384,512]{1,0:T(8,128)(2,1)}) custom-call(s32[3]{0:T(128)S(1)} %pad_add_fusion.flags_ref, bf16[3,384,512]{2,1,0:T(8,128)(2,1)} %collective-permute-done.9.refs_0_, bf16[3,1024,512]{2,1,0:T(8,128)(2,1)S(1)} %copy-done.1), custom_call_target="tpu_custom_call" | custom-call | tf_op jit(solution)/shard_map/pallas_call | solution.py:255
  118.3 0.6 shard_map.71
  118.9 1.6 copy-done.8
  120.5 0.8 broadcast_select_fusion
  121.3 1.4 collective-permute-start.10
  122.7 6.4 %collective-permute-start.11 = (bf16[384,512]{1,0:T(8,128)(2,1)}, bf16[384,512]{1,0:T(8,128)(2,1)}, u32[]{:S(2)}, u32[]{:S(2)}) collective-permute-start(bf16[384,512]{1,0:T(8,128)(2,1)} %get-tuple-element.39), channel_id=1, source_target_pairs={{0,2},{1,3},{2,4},{3,5},{4,6},{5,7},{6,8},{7,9},{8,10},{9,11},{10,... | collective-permute-start | bytes 1179656 | tf_op jit(solution)/shard_map/ppermute | solution.py:273
  129.1 0.1 collective-permute-done.12.refs_0_
  129.2 1.1 copy-done.6
  130.4 1.9 %copy-done.9 = bf16[3,1024,512]{2,1,0:T(8,128)(2,1)S(1)} copy-done((bf16[3,1024,512]{2,1,0:T(8,128)(2,1)S(1)}, bf16[3,1024,512]{2,1,0:T(8,128)(2,1)}, u32[]{:S(2)}) %copy-start.9) | copy-done | bytes 3145752
  132.2 1.1 copy-done.12
  133.4 0.9 shard_map.72
  134.3 0.0 collective-permute-done.14.refs_0_
  134.3 10.5 %shard_map.73 = (bf16[3,1024,512]{2,1,0:T(8,128)(2,1)}, bf16[384,512]{1,0:T(8,128)(2,1)S(1)}) custom-call(s32[3]{0:T(128)S(1)} %pad_add_fusion.flags_ref, bf16[3,384,512]{2,1,0:T(8,128)(2,1)} %collective-permute-done.14.refs_0_, bf16[3,1024,512]{2,1,0:T(8,128)(2,1)S(1)} %get-tuple-element.43.refs_1_), custom_call_target="tpu_custom_call" | custom-call | tf_op jit(solution)/shard_map/pallas_call | solution.py:255
  144.8 1.3 collective-permute-start.15
  146.2 1.3 collective-permute-start.13
  147.5 0.0 collective-permute-done.8
  147.5 1.8 %bitcast_dynamic-update-slice_fusion.2 = bf16[1,4,384,512]{3,2,1,0:T(8,128)(2,1)} fusion(bf16[1,4,384,512]{3,2,1,0:T(8,128)(2,1)} %get-tuple-element.25, bf16[384,512]{1,0:T(8,128)(2,1)S(1)} %copy-done.14, bf16[384,512]{1,0:T(8,128)(2,1)} %collective-permute-done.8, pred[]{:T(512)S(6)} %ne.10), kind=kLoop, calls=%fused_computation.2 | loop fusion | flops 196608 | bytes 1179649 | tf_op jit(solution)/shard_map/dynamic_update_slice | solution.py:327
  149.3 0.0 collective-permute-done.10
  149.3 1.4 collective-permute-done.11
  150.8 1.8 %bitcast_dynamic-update-slice_fusion.1 = bf16[1,4,384,512]{3,2,1,0:T(8,128)(2,1)} fusion(bf16[1,4,384,512]{3,2,1,0:T(8,128)(2,1)} %bitcast_dynamic-update-slice_fusion.2, bf16[384,512]{1,0:T(8,128)(2,1)} %collective-permute-done.10, bf16[384,512]{1,0:T(8,128)(2,1)} %collective-permute-done.11, pred[]{:T(512)S(6)} %ne.11), kind=kLoop, calls=%fused_computation.1 | loop fusion | flops 196608 | bytes 1179649 | tf_op jit(solution)/shard_map/dynamic_update_slice | solution.py:327
  152.6 1.9 %collective-permute-done.15 = bf16[384,512]{1,0:T(8,128)(2,1)S(1)} collective-permute-done((bf16[384,512]{1,0:T(8,128)(2,1)S(1)}, bf16[384,512]{1,0:T(8,128)(2,1)S(1)}, u32[]{:S(2)}, u32[]{:S(2)}) %collective-permute-start.15) | collective-permute-done | bytes 393248 | tf_op jit(solution)/shard_map/ppermute | solution.py:273
  154.5 24.0 %collective-permute-done.13 = bf16[384,512]{1,0:T(8,128)(2,1)S(1)} collective-permute-done((bf16[384,512]{1,0:T(8,128)(2,1)S(1)}, bf16[384,512]{1,0:T(8,128)(2,1)S(1)}, u32[]{:S(2)}, u32[]{:S(2)}) %collective-permute-start.13) | collective-permute-done | bytes 393248 | tf_op jit(solution)/shard_map/ppermute | solution.py:273
  178.5 0.9 bitcast_dynamic-update-slice_fusion
  (27 shorter events, 0.1 us)
Async XLA Ops:
  0.0 0.7 copy-start.17
  0.7 25.0 %copy-start.19 = (bf16[3,64,512]{2,1,0:T(8,128)(2,1)S(1)}, bf16[3,64,512]{2,1,0:T(8,128)(2,1)}, u32[]{:S(2)}) copy-start(bf16[3,64,512]{2,1,0:T(8,128)(2,1)} %param.7) | copy-start | bytes 589828
  25.7 7.3 %copy-start.18 = (bf16[1,4,384]{2,1,0:T(4,128)(2,1)S(1)}, bf16[1,4,384]{2,1,0:T(4,128)(2,1)}, u32[]{:S(2)}) copy-start(bf16[1,4,384]{2,1,0:T(4,128)(2,1)} %r_ref.5) | copy-start | bytes 9220
  25.7 18.9 %collective-permute-start.1 = (bf16[3,64,512]{2,1,0:T(8,128)(2,1)S(1)}, bf16[3,64,512]{2,1,0:T(8,128)(2,1)S(1)}, u32[]{:S(2)}, u32[]{:S(2)}) collective-permute-start(bf16[3,64,512]{2,1,0:T(8,128)(2,1)S(1)} %copy-done.19), channel_id=1, source_target_pairs={{4,0},{5,1},{6,2},{7,3},{20,16},{21,17},{22,18},{23,19}} | collective-permute-start | bytes 589832 | tf_op jit(solution)/shard_map/ppermute | solution.py:273
  27.0 17.6 %collective-permute-start.2 = (bf16[3,64,512]{2,1,0:T(8,128)(2,1)S(1)}, bf16[3,64,512]{2,1,0:T(8,128)(2,1)S(1)}, u32[]{:S(2)}, u32[]{:S(2)}) collective-permute-start(bf16[3,64,512]{2,1,0:T(8,128)(2,1)S(1)} %copy-done.19), channel_id=1, source_target_pairs={{8,0},{9,1},{10,2},{11,3},{24,16},{25,17},{26,18},{27,19}} | collective-permute-start | bytes 589832 | tf_op jit(solution)/shard_map/ppermute | solution.py:273
  28.3 16.3 %collective-permute-start.3 = (bf16[3,64,512]{2,1,0:T(8,128)(2,1)S(1)}, bf16[3,64,512]{2,1,0:T(8,128)(2,1)S(1)}, u32[]{:S(2)}, u32[]{:S(2)}) collective-permute-start(bf16[3,64,512]{2,1,0:T(8,128)(2,1)S(1)} %copy-done.19), channel_id=1, source_target_pairs={{12,0},{13,1},{14,2},{15,3},{28,16},{29,17},{30,18},{31,19}} | collective-permute-start | bytes 589832 | tf_op jit(solution)/shard_map/ppermute | solution.py:273
  30.9 13.6 %copy-start.2 = (bf16[3,384,512]{2,1,0:T(8,128)(2,1)}, bf16[3,384,512]{2,1,0:T(8,128)(2,1)S(1)}, u32[]{:S(2)}) copy-start(bf16[3,384,512]{2,1,0:T(8,128)(2,1)S(1)} %shard_map.65.refs_0_) | copy-start | bytes 3538948
  31.0 46.8 %collective-permute-start.5 = (bf16[3,384,512]{2,1,0:T(8,128)(2,1)S(1)}, bf16[3,384,512]{2,1,0:T(8,128)(2,1)S(1)}, u32[]{:S(2)}, u32[]{:S(2)}) collective-permute-start(bf16[3,384,512]{2,1,0:T(8,128)(2,1)S(1)} %shard_map.65.refs_0_), channel_id=1, source_target_pairs={{1,0},{2,1},{3,2},{4,3},{5,4},{6,5},{7,6},{8,7},{9,8},{10,9},{11,1... | collective-permute-start | bytes 3538952 | tf_op jit(solution)/shard_map/ppermute | solution.py:273
  33.0 1.9 %copy-start.7 = (bf16[1,3,1024,512]{3,2,1,0:T(8,128)(2,1)S(1)}, bf16[1,3,1024,512]{3,2,1,0:T(8,128)(2,1)}, u32[]{:S(2)}) copy-start(bf16[1,3,1024,512]{3,2,1,0:T(8,128)(2,1)} %refs_4_.1) | copy-start | bytes 9437188
  44.7 28.4 %copy-start.4 = (bf16[3,256,512]{2,1,0:T(8,128)(2,1)}, bf16[3,256,512]{2,1,0:T(8,128)(2,1)S(1)}, u32[]{:S(2)}) copy-start(bf16[3,256,512]{2,1,0:T(8,128)(2,1)S(1)} %constant_dynamic-update-slice_fusion.refs_2_) | copy-start | bytes 2359300
  44.7 46.8 %collective-permute-start.4 = (bf16[3,256,512]{2,1,0:T(8,128)(2,1)S(1)}, bf16[3,256,512]{2,1,0:T(8,128)(2,1)}, u32[]{:S(2)}, u32[]{:S(2)}) collective-permute-start(bf16[3,256,512]{2,1,0:T(8,128)(2,1)S(1)} %constant_dynamic-update-slice_fusion.refs_2_), channel_id=1, source_target_pairs={{2,0},{3,1},{18,16},{19,17}} | collective-permute-start | bytes 2359304 | tf_op jit(solution)/shard_map/ppermute | solution.py:273
  47.4 45.7 %collective-permute-start.6 = (bf16[3,256,512]{2,1,0:T(8,128)(2,1)S(1)}, bf16[3,256,512]{2,1,0:T(8,128)(2,1)S(1)}, u32[]{:S(2)}, u32[]{:S(2)}) collective-permute-start(bf16[3,256,512]{2,1,0:T(8,128)(2,1)S(1)} %constant_dynamic-update-slice_fusion.refs_2_), channel_id=1, source_target_pairs={{0,1},{1,0},{16,17},{17,16}} | collective-permute-start | bytes 2359304 | tf_op jit(solution)/shard_map/ppermute | solution.py:273
  73.0 22.2 %collective-permute-start = (bf16[3,384,512]{2,1,0:T(8,128)(2,1)}, bf16[3,384,512]{2,1,0:T(8,128)(2,1)}, u32[]{:S(2)}, u32[]{:S(2)}) collective-permute-start(bf16[3,384,512]{2,1,0:T(8,128)(2,1)} %shard_map.66), channel_id=1, source_target_pairs={{1,0},{0,1},{17,16},{16,17}} | collective-permute-start | bytes 3538952 | tf_op jit(solution)/shard_map/ppermute | solution.py:273
  74.8 32.0 %collective-permute-start.9 = (bf16[3,384,512]{2,1,0:T(8,128)(2,1)}, bf16[3,384,512]{2,1,0:T(8,128)(2,1)}, u32[]{:S(2)}, u32[]{:S(2)}) collective-permute-start(bf16[3,384,512]{2,1,0:T(8,128)(2,1)} %shard_map.66), channel_id=1, source_target_pairs={{2,0},{3,1},{4,2},{5,3},{6,4},{7,5},{8,6},{9,7},{10,8},{11,9},{12,... | collective-permute-start | bytes 3538952 | tf_op jit(solution)/shard_map/ppermute | solution.py:273
  77.8 1.0 copy-start.15
  78.8 50.4 %collective-permute-start.12 = (bf16[3,384,512]{2,1,0:T(8,128)(2,1)}, bf16[3,384,512]{2,1,0:T(8,128)(2,1)}, u32[]{:S(2)}, u32[]{:S(2)}) collective-permute-start(bf16[3,384,512]{2,1,0:T(8,128)(2,1)} %shard_map.67.refs_1_), channel_id=1, source_target_pairs={{2,0},{0,1},{18,16},{16,17}} | collective-permute-start | bytes 3538952 | tf_op jit(solution)/shard_map/ppermute | solution.py:273
  81.1 1.3 copy-start.16
  91.4 6.3 %collective-permute-start.7 = (bf16[3,256,512]{2,1,0:T(8,128)(2,1)}, bf16[3,256,512]{2,1,0:T(8,128)(2,1)}, u32[]{:S(2)}, u32[]{:S(2)}) collective-permute-start(bf16[3,256,512]{2,1,0:T(8,128)(2,1)} %collective-permute-done.4.refs_3_), channel_id=1, source_target_pairs={{0,1},{1,0},{16,17},{17,16}} | collective-permute-start | bytes 2359304 | tf_op jit(solution)/shard_map/ppermute | solution.py:273
  93.0 0.9 copy-start.10
  94.0 40.3 %collective-permute-start.14 = (bf16[3,384,512]{2,1,0:T(8,128)(2,1)}, bf16[3,384,512]{2,1,0:T(8,128)(2,1)}, u32[]{:S(2)}, u32[]{:S(2)}) collective-permute-start(bf16[3,384,512]{2,1,0:T(8,128)(2,1)} %shard_map.67.refs_1_), channel_id=1, source_target_pairs={{3,0},{4,1},{5,2},{6,3},{7,4},{8,5},{9,6},{10,7},{11,8},{12,9},{13... | collective-permute-start | bytes 3538952 | tf_op jit(solution)/shard_map/ppermute | solution.py:273
  95.3 52.2 %collective-permute-start.8 = (bf16[384,512]{1,0:T(8,128)(2,1)}, bf16[384,512]{1,0:T(8,128)(2,1)}, u32[]{:S(2)}, u32[]{:S(2)}) collective-permute-start(bf16[384,512]{1,0:T(8,128)(2,1)} %get-tuple-element.31), channel_id=1, source_target_pairs={{0,1},{1,2},{2,3},{3,4},{4,5},{5,6},{6,7},{7,8},{8,9},{9,10},{10,1... | collective-permute-start | bytes 1179656 | tf_op jit(solution)/shard_map/ppermute | solution.py:273
  97.7 1.3 copy-start.3
  99.0 1.1 copy-start.5
  100.1 1.1 copy-start.11
  102.1 1.6 copy-start
  103.8 16.8 %copy-start.13 = (bf16[384,512]{1,0:T(8,128)(2,1)}, bf16[384,512]{1,0:T(8,128)(2,1)S(1)}, u32[]{:S(2)}) copy-start(bf16[384,512]{1,0:T(8,128)(2,1)S(1)} %get-tuple-element.34) | copy-start | bytes 1179652
  106.8 1.9 %copy-start.1 = (bf16[3,1024,512]{2,1,0:T(8,128)(2,1)S(1)}, bf16[3,1024,512]{2,1,0:T(8,128)(2,1)}, u32[]{:S(2)}) copy-start(bf16[3,1024,512]{2,1,0:T(8,128)(2,1)} %copy-done) | copy-start | bytes 9437188
  118.9 1.6 copy-start.8
  121.3 28.0 %collective-permute-start.10 = (bf16[384,512]{1,0:T(8,128)(2,1)}, bf16[384,512]{1,0:T(8,128)(2,1)}, u32[]{:S(2)}, u32[]{:S(2)}) collective-permute-start(bf16[384,512]{1,0:T(8,128)(2,1)} %broadcast_select_fusion), channel_id=1, source_target_pairs={{0,1},{1,0},{16,17},{17,16}} | collective-permute-start | bytes 1179656 | tf_op jit(solution)/shard_map/ppermute | solution.py:273
  122.7 28.0 %collective-permute-start.11 = (bf16[384,512]{1,0:T(8,128)(2,1)}, bf16[384,512]{1,0:T(8,128)(2,1)}, u32[]{:S(2)}, u32[]{:S(2)}) collective-permute-start(bf16[384,512]{1,0:T(8,128)(2,1)} %get-tuple-element.39), channel_id=1, source_target_pairs={{0,2},{1,3},{2,4},{3,5},{4,6},{5,7},{6,8},{7,9},{8,10},{9,11},{10,... | collective-permute-start | bytes 1179656 | tf_op jit(solution)/shard_map/ppermute | solution.py:273
  129.2 1.1 copy-start.6
  130.4 1.9 %copy-start.9 = (bf16[3,1024,512]{2,1,0:T(8,128)(2,1)S(1)}, bf16[3,1024,512]{2,1,0:T(8,128)(2,1)}, u32[]{:S(2)}) copy-start(bf16[3,1024,512]{2,1,0:T(8,128)(2,1)} %copy-done.8) | copy-start | bytes 9437188
  132.2 1.1 copy-start.12
  134.3 13.2 %copy-start.14 = (bf16[384,512]{1,0:T(8,128)(2,1)S(1)}, bf16[384,512]{1,0:T(8,128)(2,1)}, u32[]{:S(2)}) copy-start(bf16[384,512]{1,0:T(8,128)(2,1)} %copy-done.13) | copy-start | bytes 1179652
  144.8 9.7 %collective-permute-start.15 = (bf16[384,512]{1,0:T(8,128)(2,1)S(1)}, bf16[384,512]{1,0:T(8,128)(2,1)S(1)}, u32[]{:S(2)}, u32[]{:S(2)}) collective-permute-start(bf16[384,512]{1,0:T(8,128)(2,1)S(1)} %get-tuple-element.44), channel_id=1, source_target_pairs={{0,3},{1,4},{2,5},{3,6},{4,7},{5,8},{6,9},{7,10},{8,11},{9,12},{10... | collective-permute-start | bytes 1179656 | tf_op jit(solution)/shard_map/ppermute | solution.py:273
  146.2 32.4 %collective-permute-start.13 = (bf16[384,512]{1,0:T(8,128)(2,1)S(1)}, bf16[384,512]{1,0:T(8,128)(2,1)S(1)}, u32[]{:S(2)}, u32[]{:S(2)}) collective-permute-start(bf16[384,512]{1,0:T(8,128)(2,1)S(1)} %get-tuple-element.42), channel_id=1, source_target_pairs={{0,2},{1,0},{16,18},{17,16}} | collective-permute-start | bytes 1179656 | tf_op jit(solution)/shard_map/ppermute | solution.py:273

commit v3 on v0

v3 whole, which is shorter than its diff:
```python
import functools
import jax
import jax.numpy as jnp
from jax import lax
from jax.experimental import pallas as pl
from jax.experimental.pallas import tpu as pltpu
from jax.sharding import PartitionSpec as P

epsilon = 1e-06
f32 = jnp.float32
bf16 = jnp.bfloat16
HBM = pl.BlockSpec(memory_space=pltpu.HBM)
VMEM = pl.BlockSpec(memory_space=pltpu.VMEM)
SMEM = pl.BlockSpec(memory_space=pltpu.SMEM)
LIMIT = 28 << 20


def in_hbm(*arrays):
    return [pltpu.with_memory_space_constraint(a, pltpu.HBM) for a in arrays]


def nt(a, b):
    return lax.dot_general(a, b, (((1,), (1,)), ((), ())), preferred_element_type=f32)


def nn(a, b):
    return lax.dot_general(a, b, (((1,), (0,)), ((), ())), preferred_element_type=f32)


def sigmoid(x):
    return 0.5 * jnp.tanh(0.5 * x) + 0.5


def scaled_values(steps_row, values):
    lanes = 128
    span, width = values.shape
    column = jnp.broadcast_to(steps_row.astype(f32), (lanes, span)).T
    return jnp.concatenate(
        [
            (column * values[:, i : i + lanes].astype(f32)).astype(bf16)
            for i in range(0, width, lanes)
        ],
        axis=1,
    )


def pack_kernel(tick, k_ref, v_ref, q_ref, r_ref, o_ref, tok, sems):
    sources = (k_ref, v_ref, q_ref)
    loads = [
        pltpu.make_async_copy(sources[i].at[0, tick], tok.at[i], sems.at[i])
        for i in range(3)
    ]
    stores = [pltpu.make_async_copy(tok.at[i], o_ref.at[i], sems.at[3 + i]) for i in range(3)]
    for i in (1, 0, 2):
        loads[i].start()
    loads[1].wait()
    tok[1] = scaled_values(r_ref[0, tick : tick + 1, :], tok[1])
    stores[1].start()
    for i in (0, 2):
        loads[i].wait()
        stores[i].start()
    for store in stores:
        store.wait()


def pack(tick, keys, values, queries, steps):
    _, _, span, width = keys.shape
    return pl.pallas_call(
        functools.partial(pack_kernel, tick),
        in_specs=[HBM, HBM, HBM, VMEM],
        out_specs=HBM,
        out_shape=jax.ShapeDtypeStruct((3, span, width), bf16),
        scratch_shapes=[pltpu.VMEM((3, span, width), bf16), pltpu.SemaphoreType.DMA((6,))],
        compiler_params=pltpu.CompilerParams(vmem_limit_bytes=LIMIT),
    )(*in_hbm(keys, values, queries), steps)


def join_kernel(*refs):
    out = refs[-1]
    rows = 0
    for ref in refs[:-1]:
        height = ref.shape[1]
        out[:, rows : rows + height] = ref[...]
        rows += height


def join(parts):
    planes, _, width = parts[0].shape
    rows = sum(part.shape[1] for part in parts)
    return pl.pallas_call(
        join_kernel,
        in_specs=[VMEM] * len(parts),
        out_specs=VMEM,
        out_shape=jax.ShapeDtypeStruct((planes, rows, width), bf16),
        compiler_params=pltpu.CompilerParams(vmem_limit_bytes=LIMIT),
        name="join",
    )(*parts)


def step_rows(old, delta):
    previous = old.astype(f32)
    updated = previous + delta
    old_norm = jnp.sqrt(jnp.sum(previous * previous, axis=-1, keepdims=True) + epsilon)
    new_norm = jnp.sqrt(jnp.sum(updated * updated, axis=-1, keepdims=True) + epsilon)
    return (updated * (old_norm / new_norm)).astype(bf16)


def advance_rows(keys, target, gate, up, down):
    gate_pre = nt(gate, keys)
    up_pre = nt(up, keys)
    back_grad = nt(down, target)
    sig = sigmoid(gate_pre)
    silu = gate_pre * sig
    hidden = (silu * up_pre).astype(bf16)
    grad_up = (back_grad * silu).astype(bf16)
    grad_gate = ((back_grad * up_pre) * (sig * (1.0 + (gate_pre - silu)))).astype(bf16)
    return (
        step_rows(gate, nn(grad_gate, keys)),
        step_rows(up, nn(grad_up, keys)),
        step_rows(down, nn(hidden, target)),
    )


def serve_rows(queries, gate, up, down):
    c = nt(queries, gate)
    e = nt(queries, up)
    return nn((c * sigmoid(c) * e).astype(bf16), down)


def unit_kernel(tick, n_pieces, block, flags_ref, *refs):
    refs = list(refs)
    take = lambda n: [refs.pop(0) for _ in range(n)]
    tokens = take(4 if tick == 0 else 1)
    pieces = take(n_pieces)
    state, new_ref, ans_out, tok, acc, ans, sems = refs
    if tick == 0:
        sources = [tokens[i].at[0, 0] for i in range(3)]
        state = state.at[0]
    else:
        sources = [tokens[0].at[i] for i in range(3)]
        state = new_ref
    loads = [pltpu.make_async_copy(sources[i], tok.at[i], sems.at[i]) for i in range(3)]
    for load in loads:
        load.start()
    if n_pieces:
        @pl.when(flags_ref[tick] != 0)
        def _():
            rows = 0
            copies = []
            for n, piece in enumerate(pieces):
                height = piece.shape[1]
                part = new_ref.at[:, pl.ds(rows, height)]
                copies.append(pltpu.make_async_copy(piece, part, sems.at[4 + n]))
                rows += height
            for copy in copies:
                copy.start()
            for copy in copies:
                copy.wait()

    loads[0].wait()
    loads[1].wait()
    if tick == 0:
        tok[1] = scaled_values(tokens[3][0, 0:1, :], tok[1])
    count = new_ref.shape[1] // block
    for j in range(count):
        rows = pl.ds(j * block, block)
        new = advance_rows(tok[0], tok[1], state[0, rows], state[1, rows], state[2, rows])
        for i in range(3):
            new_ref[i, rows] = new[i]
        if j == 0:
            loads[2].wait()
        part = serve_rows(tok[2], new_ref[0, rows], new_ref[1, rows], new_ref[2, rows])
        total = part if j == 0 else acc[...] + part
        if j == count - 1:
            ans[...] = total.astype(bf16)
        else:
            acc[...] = total
    out = pltpu.make_async_copy(ans, ans_out.at[0, 0] if tick == 0 else ans_out, sems.at[3])
    out.start()
    out.wait()


def unit(tick, flags, tokens, state, pieces, block=512):
    span, width = tokens[0].shape[-2:]
    hid = state.shape[-2]
    token_specs = [HBM] * len(tokens)
    if tick == 0:
        token_specs[3] = VMEM
        tokens = in_hbm(*tokens[:3]) + tokens[3:]
    return pl.pallas_call(
        functools.partial(unit_kernel, tick, len(pieces), block),
        in_specs=[SMEM] + token_specs + [HBM] * len(pieces) + [VMEM],
        out_specs=[VMEM, HBM],
        out_shape=[
            jax.ShapeDtypeStruct((3, hid, width), bf16),
            jax.ShapeDtypeStruct(tokens[0].shape if tick == 0 else (span, width), bf16),
        ],
        input_output_aliases={} if tick == 0 else {1 + len(tokens) + len(pieces): 0},
        scratch_shapes=[
            pltpu.VMEM((3, span, width), bf16),
            pltpu.VMEM((span, width), f32),
            pltpu.VMEM((span, width), bf16),
            pltpu.SemaphoreType.DMA((4 + len(pieces),)),
        ],
        compiler_params=pltpu.CompilerParams(vmem_limit_bytes=LIMIT),
    )(flags, *tokens, *pieces, state)


def body(fast_state, initial_fast, queries, token_keys, token_values, step_sizes):
    count = lax.axis_size("seq")
    position = lax.axis_index("seq")
    ticks = token_keys.shape[1]
    flags = jnp.stack([(position + t == count).astype(jnp.int32) for t in range(ticks)])

    def send(value, pairs):
        return lax.ppermute(value, "seq", pairs)

    def shift(value, steps):
        return send(value, [(s, (s + steps) % count) for s in range(count)])

    args = [token_keys, token_values, queries, step_sizes]
    packs = [pack(t, *args) for t in range(1, ticks)]
    tokens = [shift(packs[t - 1], -t) for t in range(1, ticks)]

    last = 4
    width = count
    held = initial_fast
    while width > last:
        radix = 4 if width % (4 * last) == 0 else 2
        width //= radix
        base = count - width
        got = [
            send(held, [(base - j * width + i, base + i) for i in range(width)])
            for j in range(1, radix)
        ]
        held = join([held] + got)
    base = count - last
    swap = lambda value, bit: send(
        value, [(base + i, base + (i ^ bit)) for i in range(last)]
    )
    pieces = [held, swap(held, 2)]
    pieces += [swap(piece, 1) for piece in pieces]

    state, out = unit(0, flags, args, fast_state, [])
    answers = []
    for t in range(1, ticks):
        state, answer = unit(t, flags, [tokens[t - 1]], state, pieces)
        answers.append(shift(answer, t))
    for t in range(1, ticks):
        out = lax.dynamic_update_slice(out, answers[t - 1][None, None], (0, t, 0, 0))
    return out


def solution(mesh):
    return jax.shard_map(
        body,
        mesh=mesh,
        in_specs=(
            P(("grp", "seq"), None, None, None),
            P(None, "seq", None),
            P(("grp", "seq"), None, None, None),
            P(("grp", "seq"), None, None, None),
            P(("grp", "seq"), None, None, None),
            P(("grp", "seq"), None, None),
        ),
        out_specs=P(("grp", "seq"), None, None, None),
        check_vma=False,
    )
```

time: 197 us -> 144 us (0.73)
  matrix products: 53.6 us -> 0 us
  Pallas kernels: 0 us -> 41.4 us
  other arithmetic: 25.6 us -> 0.08 us
  local copies, waits for them, and re-layouts: 19.8 us -> 5.14 us
  between operations: 13.9 us -> 0.18 us
  starting transfers between devices: 19 us -> 29 us
  waiting for transfers between devices: 64 us -> 68 us
    dot_general x32 -> x0, matrix products: 53.6 us -> none  [the longest x16 24.2 us: contract_last(): lax.dot_general(left_side, right_side, (((1,), (1,)), ((), ())), preferre...]
    ppermute x15 -> x12, waiting for transfers between devices: 16.3 us -> 68 us  [send(): return lax.ppermute(value, 'seq', pairs)]
    all_gather x1 -> x0, waiting for transfers between devices: 47 us -> none  [body(): whole_initial = lax.all_gather(initial_fast, 'seq', axis=1, tiled=True)]
    pallas_call x0 -> x8, Pallas kernels: none -> 41.4 us  [the longest x4 34.7 us: unit(): pl.pallas_call(functools.partial(unit_kernel, tick, len(pieces), block),...]
    select_n x3 -> x0, other arithmetic: 13.2 us -> none  [body(): carried = jnp.where(restart, whole_initial, advanced)]
    ppermute x15 -> x12, starting transfers between devices: 19 us -> 29 us  [send(): return lax.ppermute(value, 'seq', pairs)]
    squeeze x3 -> x0, local copies, waits for them, and re-layouts: 6.68 us -> none  [the longest x1 3.37 us: body(): token_values[0, step_index]]
    unnamed x43 -> x6, local copies, waits for them, and re-layouts: 9.13 us -> 2.82 us
  transfers between devices with their start and end apart: 16 -> 12, of which waited for: 4 -> 5; matrix products, arithmetic and copies ran while one was open for 46% -> 1% of each run, Pallas kernels for 0% -> 29%
where the time goes in v3:
time: 144 us
  waiting for transfers between devices  68 us (47%)
  Pallas kernels  41.4 us (29%)
  starting transfers between devices  29 us (20%)
  local copies, waits for them, and re-layouts  5.14 us (4%)
    ppermute x12, waiting for transfers between devices, send(): return lax.ppermute(value, 'seq', pairs)  68 us
    pallas_call x4, Pallas kernels, unit(): pl.pallas_call(functools.partial(unit_kernel, tick, len(pieces), block),...  34.7 us
    ppermute x12, starting transfers between devices, send(): return lax.ppermute(value, 'seq', pairs)  29 us
    pallas_call x3, Pallas kernels, pack(): pl.pallas_call(functools.partial(pack_kernel, tick), in_specs=[HBM, HBM,...  6.69 us
  transfers between devices with their start and end apart: 12, of which 5 were waited for; matrix products, arithmetic and copies ran while one was open for 1% of the time, Pallas kernels for 29%

profile of v3, /device:TPU:1, one launch (start us, length us, event | category | flops | bytes accessed | tf_op | source)
XLA Modules:
  0.0 143.8 jit_solution(2877908226253233465)
XLA Ops:
  0.0 0.7 collective-permute-start.1
  0.7 0.7 collective-permute-start.2
  1.4 7.3 %collective-permute-start.3 = (bf16[3,64,512]{2,1,0:T(8,128)(2,1)}, bf16[3,64,512]{2,1,0:T(8,128)(2,1)S(1)}, u32[]{:S(2)}, u32[]{:S(2)}) collective-permute-start(bf16[3,64,512]{2,1,0:T(8,128)(2,1)} %refs_0_.3), channel_id=1, source_target_pairs={{0,12},{1,13},{2,14},{3,15},{16,28},{17,29},{18,30},{19,31}} | collective-permute-start | bytes 589832 | tf_op jit(solution)/shard_map/ppermute | solution.py:216
  8.7 0.0 collective-permute-done.1.refs_1_
  8.7 0.0 collective-permute-done.2.refs_2_
  8.7 3.9 %collective-permute-done.3.refs_3_ = bf16[3,64,512]{2,1,0:T(8,128)(2,1)S(1)} collective-permute-done((bf16[3,64,512]{2,1,0:T(8,128)(2,1)}, bf16[3,64,512]{2,1,0:T(8,128)(2,1)S(1)}, u32[]{:S(2)}, u32[]{:S(2)}) %collective-permute-start.3) | collective-permute-done | bytes 196640 | tf_op jit(solution)/shard_map/ppermute | solution.py:216
  12.6 0.0 copy-start.1
  12.6 0.9 copy-done.1
  13.5 0.0 copy-start.2
  13.5 0.1 join.1.refs_1_
  13.6 0.7 collective-permute-start.4
  14.3 0.0 copy-done.2
  14.3 2.2 %shard_map.65 = bf16[3,384,512]{2,1,0:T(8,128)(2,1)} custom-call(bf16[1,4,384,512]{3,2,1,0:T(8,128)(2,1)} %k_ref.5, bf16[1,4,384,512]{3,2,1,0:T(8,128)(2,1)} %v_ref.5, bf16[1,4,384,512]{3,2,1,0:T(8,128)(2,1)} %q_ref.5, bf16[1,4,384]{2,1,0:T(4,128)(2,1)S(1)} %copy-done.2), custom_call_target="tpu_custom_call" | custom-call | tf_op jit(solution)/shard_map/pallas_call | solution.py:68
  16.6 1.5 %collective-permute-start = (bf16[3,384,512]{2,1,0:T(8,128)(2,1)}, bf16[3,384,512]{2,1,0:T(8,128)(2,1)}, u32[]{:S(2)}, u32[]{:S(2)}) collective-permute-start(bf16[3,384,512]{2,1,0:T(8,128)(2,1)} %shard_map.65), channel_id=1, source_target_pairs={{0,15},{1,0},{2,1},{3,2},{4,3},{5,4},{6,5},{7,6},{8,7},{9,8},{10,9... | collective-permute-start | bytes 3538952 | tf_op jit(solution)/shard_map/ppermute | solution.py:216
  18.1 2.2 %shard_map.67 = bf16[3,384,512]{2,1,0:T(8,128)(2,1)} custom-call(bf16[1,4,384,512]{3,2,1,0:T(8,128)(2,1)} %k_ref.5, bf16[1,4,384,512]{3,2,1,0:T(8,128)(2,1)} %v_ref.5, bf16[1,4,384,512]{3,2,1,0:T(8,128)(2,1)} %q_ref.5, bf16[1,4,384]{2,1,0:T(4,128)(2,1)S(1)} %copy-done.2), custom_call_target="tpu_custom_call" | custom-call | tf_op jit(solution)/shard_map/pallas_call | solution.py:68
  20.3 10.6 %collective-permute-start.8 = (bf16[3,384,512]{2,1,0:T(8,128)(2,1)}, bf16[3,384,512]{2,1,0:T(8,128)(2,1)}, u32[]{:S(2)}, u32[]{:S(2)}) collective-permute-start(bf16[3,384,512]{2,1,0:T(8,128)(2,1)} %shard_map.67), channel_id=1, source_target_pairs={{0,14},{1,15},{2,0},{3,1},{4,2},{5,3},{6,4},{7,5},{8,6},{9,7},{10,... | collective-permute-start | bytes 3538952 | tf_op jit(solution)/shard_map/ppermute | solution.py:216
  30.9 2.2 %shard_map.69 = bf16[3,384,512]{2,1,0:T(8,128)(2,1)} custom-call(bf16[1,4,384,512]{3,2,1,0:T(8,128)(2,1)} %k_ref.5, bf16[1,4,384,512]{3,2,1,0:T(8,128)(2,1)} %v_ref.5, bf16[1,4,384,512]{3,2,1,0:T(8,128)(2,1)} %q_ref.5, bf16[1,4,384]{2,1,0:T(4,128)(2,1)S(1)} %copy-done.2), custom_call_target="tpu_custom_call" | custom-call | tf_op jit(solution)/shard_map/pallas_call | solution.py:68
  33.2 1.5 %collective-permute-start.10 = (bf16[3,384,512]{2,1,0:T(8,128)(2,1)}, bf16[3,384,512]{2,1,0:T(8,128)(2,1)}, u32[]{:S(2)}, u32[]{:S(2)}) collective-permute-start(bf16[3,384,512]{2,1,0:T(8,128)(2,1)} %shard_map.69), channel_id=1, source_target_pairs={{0,13},{1,14},{2,15},{3,0},{4,1},{5,2},{6,3},{7,4},{8,5},{9,6},{10... | collective-permute-start | bytes 3538952 | tf_op jit(solution)/shard_map/ppermute | solution.py:216
  34.7 0.7 collective-permute-start.5
  35.4 0.0 collective-permute-done.4.refs_2_
  35.4 0.7 collective-permute-start.6
  36.1 0.1 add_convert_fusion.flags_ref
  36.2 0.0 copy-start
  36.2 1.9 %copy-done = bf16[1,3,1024,512]{3,2,1,0:T(8,128)(2,1)S(1)} copy-done((bf16[1,3,1024,512]{3,2,1,0:T(8,128)(2,1)S(1)}, bf16[1,3,1024,512]{3,2,1,0:T(8,128)(2,1)}, u32[]{:S(2)}) %copy-start) | copy-done | bytes 3145752
  38.1 9.0 %shard_map.64 = (bf16[3,1024,512]{2,1,0:T(8,128)(2,1)S(1)}, bf16[1,4,384,512]{3,2,1,0:T(8,128)(2,1)}) custom-call(s32[4]{0:T(128)S(1)} %add_convert_fusion.flags_ref, bf16[1,4,384,512]{3,2,1,0:T(8,128)(2,1)} %k_ref.5, bf16[1,4,384,512]{3,2,1,0:T(8,128)(2,1)} %v_ref.5, bf16[1,4,384,512]{3,2,1,0:T(8,128)(2,1)} %q_ref.5, bf16[1,4,384]{2,1,0:T(4,128)(2,1)S(1)} %copy-done.2, ...), custom_call_target="tpu_custom_call" | custom-call | tf_op jit(solution)/shard_map/pallas_call | solution.py:190
  47.1 0.0 collective-permute-done.5.refs_3_
  47.1 0.0 collective-permute-done.refs_0_
  47.1 0.0 collective-permute-done.6.refs_4_
  47.1 8.6 %shard_map.66 = (bf16[3,1024,512]{2,1,0:T(8,128)(2,1)S(1)}, bf16[384,512]{1,0:T(8,128)(2,1)S(1)}) custom-call(s32[4]{0:T(128)S(1)} %add_convert_fusion.flags_ref, bf16[3,384,512]{2,1,0:T(8,128)(2,1)} %collective-permute-done.refs_0_, bf16[3,256,512]{2,1,0:T(8,128)(2,1)S(1)} %join.1.refs_1_, ...), custom_call_target="tpu_custom_call", output_to_operand_aliasing={{0}: (6, {})} | custom-call | tf_op jit(solution)/shard_map/pallas_call | solution.py:190
  55.7 0.4 collective-permute-start.7
  56.1 0.9 collective-permute-done.8.refs_0_
  57.0 8.6 %shard_map.68 = (bf16[3,1024,512]{2,1,0:T(8,128)(2,1)S(1)}, bf16[384,512]{1,0:T(8,128)(2,1)S(1)}) custom-call(s32[4]{0:T(128)S(1)} %add_convert_fusion.flags_ref, bf16[3,384,512]{2,1,0:T(8,128)(2,1)} %collective-permute-done.8.refs_0_, bf16[3,256,512]{2,1,0:T(8,128)(2,1)S(1)} %join.1.refs_1_, ...), custom_call_target="tpu_custom_call", output_to_operand_aliasing={{0}: (6, {})} | custom-call | tf_op jit(solution)/shard_map/pallas_call | solution.py:190
  65.6 0.2 collective-permute-start.9
  65.9 20.1 %collective-permute-done.10.refs_0_ = bf16[3,384,512]{2,1,0:T(8,128)(2,1)} collective-permute-done((bf16[3,384,512]{2,1,0:T(8,128)(2,1)}, bf16[3,384,512]{2,1,0:T(8,128)(2,1)}, u32[]{:S(2)}, u32[]{:S(2)}) %collective-permute-start.10) | collective-permute-done | bytes 1179680 | tf_op jit(solution)/shard_map/ppermute | solution.py:216
  86.0 8.6 %shard_map.70 = (bf16[3,1024,512]{2,1,0:T(8,128)(2,1)S(1)}, bf16[384,512]{1,0:T(8,128)(2,1)S(1)}) custom-call(s32[4]{0:T(128)S(1)} %add_convert_fusion.flags_ref, bf16[3,384,512]{2,1,0:T(8,128)(2,1)} %collective-permute-done.10.refs_0_, bf16[3,256,512]{2,1,0:T(8,128)(2,1)S(1)} %join.1.refs_1_, ...), custom_call_target="tpu_custom_call", output_to_operand_aliasing={{0}: (6, {})} | custom-call | tf_op jit(solution)/shard_map/pallas_call | solution.py:190
  94.6 3.9 %collective-permute-start.11 = (bf16[384,512]{1,0:T(8,128)(2,1)S(1)}, bf16[384,512]{1,0:T(8,128)(2,1)S(1)}, u32[]{:S(2)}, u32[]{:S(2)}) collective-permute-start(bf16[384,512]{1,0:T(8,128)(2,1)S(1)} %get-tuple-element.18), channel_id=1, source_target_pairs={{0,3},{1,4},{2,5},{3,6},{4,7},{5,8},{6,9},{7,10},{8,11},{9,12},{10... | collective-permute-start | bytes 1179656 | tf_op jit(solution)/shard_map/ppermute | solution.py:216
  98.5 0.0 collective-permute-done.7
  98.5 0.8 bitcast_dynamic-update-slice_fusion.2
  99.3 34.7 %collective-permute-done.9 = bf16[384,512]{1,0:T(8,128)(2,1)S(1)} collective-permute-done((bf16[384,512]{1,0:T(8,128)(2,1)S(1)}, bf16[384,512]{1,0:T(8,128)(2,1)S(1)}, u32[]{:S(2)}, u32[]{:S(2)}) %collective-permute-start.9) | collective-permute-done | bytes 393248 | tf_op jit(solution)/shard_map/ppermute | solution.py:216
  134.0 0.8 bitcast_dynamic-update-slice_fusion.1
  134.8 8.3 %collective-permute-done.11 = bf16[384,512]{1,0:T(8,128)(2,1)S(1)} collective-permute-done((bf16[384,512]{1,0:T(8,128)(2,1)S(1)}, bf16[384,512]{1,0:T(8,128)(2,1)S(1)}, u32[]{:S(2)}, u32[]{:S(2)}) %collective-permute-start.11) | collective-permute-done | bytes 393248 | tf_op jit(solution)/shard_map/ppermute | solution.py:216
  143.0 0.8 bitcast_dynamic-update-slice_fusion
Async XLA Ops:
  0.0 8.7 %collective-permute-start.1 = (bf16[3,64,512]{2,1,0:T(8,128)(2,1)}, bf16[3,64,512]{2,1,0:T(8,128)(2,1)S(1)}, u32[]{:S(2)}, u32[]{:S(2)}) collective-permute-start(bf16[3,64,512]{2,1,0:T(8,128)(2,1)} %refs_0_.3), channel_id=1, source_target_pairs={{8,12},{9,13},{10,14},{11,15},{24,28},{25,29},{26,30},{27,31}} | collective-permute-start | bytes 589832 | tf_op jit(solution)/shard_map/ppermute | solution.py:216
  0.7 8.0 %collective-permute-start.2 = (bf16[3,64,512]{2,1,0:T(8,128)(2,1)}, bf16[3,64,512]{2,1,0:T(8,128)(2,1)S(1)}, u32[]{:S(2)}, u32[]{:S(2)}) collective-permute-start(bf16[3,64,512]{2,1,0:T(8,128)(2,1)} %refs_0_.3), channel_id=1, source_target_pairs={{4,12},{5,13},{6,14},{7,15},{20,28},{21,29},{22,30},{23,31}} | collective-permute-start | bytes 589832 | tf_op jit(solution)/shard_map/ppermute | solution.py:216
  1.4 11.3 %collective-permute-start.3 = (bf16[3,64,512]{2,1,0:T(8,128)(2,1)}, bf16[3,64,512]{2,1,0:T(8,128)(2,1)S(1)}, u32[]{:S(2)}, u32[]{:S(2)}) collective-permute-start(bf16[3,64,512]{2,1,0:T(8,128)(2,1)} %refs_0_.3), channel_id=1, source_target_pairs={{0,12},{1,13},{2,14},{3,15},{16,28},{17,29},{18,30},{19,31}} | collective-permute-start | bytes 589832 | tf_op jit(solution)/shard_map/ppermute | solution.py:216
  12.6 0.9 copy-start.1
  13.5 0.8 copy-start.2
  13.6 21.8 %collective-permute-start.4 = (bf16[3,256,512]{2,1,0:T(8,128)(2,1)S(1)}, bf16[3,256,512]{2,1,0:T(8,128)(2,1)S(1)}, u32[]{:S(2)}, u32[]{:S(2)}) collective-permute-start(bf16[3,256,512]{2,1,0:T(8,128)(2,1)S(1)} %join.1.refs_1_), channel_id=1, source_target_pairs={{12,14},{13,15},{14,12},{15,13},{28,30},{29,31},{30,28},{31,29}} | collective-permute-start | bytes 2359304 | tf_op jit(solution)/shard_map/ppermute | solution.py:216
  16.6 30.5 %collective-permute-start = (bf16[3,384,512]{2,1,0:T(8,128)(2,1)}, bf16[3,384,512]{2,1,0:T(8,128)(2,1)}, u32[]{:S(2)}, u32[]{:S(2)}) collective-permute-start(bf16[3,384,512]{2,1,0:T(8,128)(2,1)} %shard_map.65), channel_id=1, source_target_pairs={{0,15},{1,0},{2,1},{3,2},{4,3},{5,4},{6,5},{7,6},{8,7},{9,8},{10,9... | collective-permute-start | bytes 3538952 | tf_op jit(solution)/shard_map/ppermute | solution.py:216
  20.3 36.7 %collective-permute-start.8 = (bf16[3,384,512]{2,1,0:T(8,128)(2,1)}, bf16[3,384,512]{2,1,0:T(8,128)(2,1)}, u32[]{:S(2)}, u32[]{:S(2)}) collective-permute-start(bf16[3,384,512]{2,1,0:T(8,128)(2,1)} %shard_map.67), channel_id=1, source_target_pairs={{0,14},{1,15},{2,0},{3,1},{4,2},{5,3},{6,4},{7,5},{8,6},{9,7},{10,... | collective-permute-start | bytes 3538952 | tf_op jit(solution)/shard_map/ppermute | solution.py:216
  33.2 52.8 %collective-permute-start.10 = (bf16[3,384,512]{2,1,0:T(8,128)(2,1)}, bf16[3,384,512]{2,1,0:T(8,128)(2,1)}, u32[]{:S(2)}, u32[]{:S(2)}) collective-permute-start(bf16[3,384,512]{2,1,0:T(8,128)(2,1)} %shard_map.69), channel_id=1, source_target_pairs={{0,13},{1,14},{2,15},{3,0},{4,1},{5,2},{6,3},{7,4},{8,5},{9,6},{10... | collective-permute-start | bytes 3538952 | tf_op jit(solution)/shard_map/ppermute | solution.py:216
  34.7 12.4 %collective-permute-start.5 = (bf16[3,256,512]{2,1,0:T(8,128)(2,1)S(1)}, bf16[3,256,512]{2,1,0:T(8,128)(2,1)S(1)}, u32[]{:S(2)}, u32[]{:S(2)}) collective-permute-start(bf16[3,256,512]{2,1,0:T(8,128)(2,1)S(1)} %join.1.refs_1_), channel_id=1, source_target_pairs={{12,13},{13,12},{14,15},{15,14},{28,29},{29,28},{30,31},{31,30}} | collective-permute-start | bytes 2359304 | tf_op jit(solution)/shard_map/ppermute | solution.py:216
  35.4 11.7 %collective-permute-start.6 = (bf16[3,256,512]{2,1,0:T(8,128)(2,1)S(1)}, bf16[3,256,512]{2,1,0:T(8,128)(2,1)S(1)}, u32[]{:S(2)}, u32[]{:S(2)}) collective-permute-start(bf16[3,256,512]{2,1,0:T(8,128)(2,1)S(1)} %collective-permute-done.4.refs_2_), channel_id=1, source_target_pairs={{12,13},{13,12},{14,15},{15,14},{28,29},{29,28},{30,31},{31,30}} | collective-permute-start | bytes 2359304 | tf_op jit(solution)/shard_map/ppermute | solution.py:216
  36.2 1.9 %copy-start = (bf16[1,3,1024,512]{3,2,1,0:T(8,128)(2,1)S(1)}, bf16[1,3,1024,512]{3,2,1,0:T(8,128)(2,1)}, u32[]{:S(2)}) copy-start(bf16[1,3,1024,512]{3,2,1,0:T(8,128)(2,1)} %refs_4_.1) | copy-start | bytes 9437188
  55.7 42.8 %collective-permute-start.7 = (bf16[384,512]{1,0:T(8,128)(2,1)S(1)}, bf16[384,512]{1,0:T(8,128)(2,1)S(1)}, u32[]{:S(2)}, u32[]{:S(2)}) collective-permute-start(bf16[384,512]{1,0:T(8,128)(2,1)S(1)} %get-tuple-element.14), channel_id=1, source_target_pairs={{0,1},{1,2},{2,3},{3,4},{4,5},{5,6},{6,7},{7,8},{8,9},{9,10},{10,1... | collective-permute-start | bytes 1179656 | tf_op jit(solution)/shard_map/ppermute | solution.py:216
  65.6 68.4 %collective-permute-start.9 = (bf16[384,512]{1,0:T(8,128)(2,1)S(1)}, bf16[384,512]{1,0:T(8,128)(2,1)S(1)}, u32[]{:S(2)}, u32[]{:S(2)}) collective-permute-start(bf16[384,512]{1,0:T(8,128)(2,1)S(1)} %get-tuple-element.16), channel_id=1, source_target_pairs={{0,2},{1,3},{2,4},{3,5},{4,6},{5,7},{6,8},{7,9},{8,10},{9,11},{10,... | collective-permute-start | bytes 1179656 | tf_op jit(solution)/shard_map/ppermute | solution.py:216
  94.6 48.5 %collective-permute-start.11 = (bf16[384,512]{1,0:T(8,128)(2,1)S(1)}, bf16[384,512]{1,0:T(8,128)(2,1)S(1)}, u32[]{:S(2)}, u32[]{:S(2)}) collective-permute-start(bf16[384,512]{1,0:T(8,128)(2,1)S(1)} %get-tuple-element.18), channel_id=1, source_target_pairs={{0,3},{1,4},{2,5},{3,6},{4,7},{5,8},{6,9},{7,10},{8,11},{9,12},{10... | collective-permute-start | bytes 1179656 | tf_op jit(solution)/shard_map/ppermute | solution.py:216

commit v4 on v3

--- a/solution.py
+++ b/solution.py
@@ -13,6 +13,7 @@
 VMEM = pl.BlockSpec(memory_space=pltpu.VMEM)
 SMEM = pl.BlockSpec(memory_space=pltpu.SMEM)
 LIMIT = 28 << 20
+EXTRA = -1
 
 
 def in_hbm(*arrays):
@@ -72,6 +73,7 @@
         out_shape=jax.ShapeDtypeStruct((3, span, width), bf16),
         scratch_shapes=[pltpu.VMEM((3, span, width), bf16), pltpu.SemaphoreType.DMA((6,))],
         compiler_params=pltpu.CompilerParams(vmem_limit_bytes=LIMIT),
+        cost_estimate=pl.CostEstimate(flops=0, bytes_accessed=0, transcendentals=0),
     )(*in_hbm(keys, values, queries), steps)
 
 
@@ -93,6 +95,7 @@
         out_specs=VMEM,
         out_shape=jax.ShapeDtypeStruct((planes, rows, width), bf16),
         compiler_params=pltpu.CompilerParams(vmem_limit_bytes=LIMIT),
+        cost_estimate=pl.CostEstimate(flops=0, bytes_accessed=0, transcendentals=0),
         name="join",
     )(*parts)
 
@@ -132,7 +135,22 @@
     take = lambda n: [refs.pop(0) for _ in range(n)]
     tokens = take(4 if tick == 0 else 1)
     pieces = take(n_pieces)
-    state, new_ref, ans_out, tok, acc, ans, sems = refs
+    if tick == EXTRA:
+        ans_out, new_ref, tok, acc, ans, sems = refs
+
+        @pl.when(flags_ref[0] != 0)
+        def _():
+            unit_steps(
+                tick, block, flags_ref, tokens, pieces, new_ref, new_ref, ans_out, tok,
+                acc, ans, sems,
+            )
+    else:
+        unit_steps(tick, block, flags_ref, tokens, pieces, *refs)
+
+
+def unit_steps(
+    tick, block, flags_ref, tokens, pieces, state, new_ref, ans_out, tok, acc, ans, sems
+):
     if tick == 0:
         sources = [tokens[i].at[0, 0] for i in range(3)]
         state = state.at[0]
@@ -142,8 +160,8 @@
     loads = [pltpu.make_async_copy(sources[i], tok.at[i], sems.at[i]) for i in range(3)]
     for load in loads:
         load.start()
-    if n_pieces:
-        @pl.when(flags_ref[tick] != 0)
+    if pieces:
+        @pl.when(flags_ref[max(tick, 0)] != 0)
         def _():
             rows = 0
             copies = []
@@ -162,19 +180,32 @@
     if tick == 0:
         tok[1] = scaled_values(tokens[3][0, 0:1, :], tok[1])
     count = new_ref.shape[1] // block
-    for j in range(count):
-        rows = pl.ds(j * block, block)
+
+    def one(rows, first, last):
         new = advance_rows(tok[0], tok[1], state[0, rows], state[1, rows], state[2, rows])
         for i in range(3):
             new_ref[i, rows] = new[i]
-        if j == 0:
+        if first:
             loads[2].wait()
         part = serve_rows(tok[2], new_ref[0, rows], new_ref[1, rows], new_ref[2, rows])
-        total = part if j == 0 else acc[...] + part
-        if j == count - 1:
+        total = part if first else acc[...] + part
+        if last:
             ans[...] = total.astype(bf16)
         else:
             acc[...] = total
+
+    if tick == EXTRA:
+        loads[2].wait()
+        acc[...] = jnp.zeros_like(acc)
+
+        @pl.loop(0, count)
+        def _(j):
+            one(pl.ds(pl.multiple_of(j * block, block), block), False, False)
+
+        ans[...] = acc[...].astype(bf16)
+    else:
+        for j in range(count):
+            one(pl.ds(j * block, block), j == 0, j == count - 1)
     out = pltpu.make_async_copy(ans, ans_out.at[0, 0] if tick == 0 else ans_out, sems.at[3])
     out.start()
     out.wait()
@@ -182,72 +213,100 @@
 
 def unit(tick, flags, tokens, state, pieces, block=512):
     span, width = tokens[0].shape[-2:]
-    hid = state.shape[-2]
+    if tick == EXTRA:
+        hid = sum(piece.shape[1] for piece in pieces)
+        states, state_shapes = [], []
+        aliases = {}
+    else:
+        hid = state.shape[-2]
+        states = [state]
+        state_shapes = [jax.ShapeDtypeStruct((3, hid, width), bf16)]
+        aliases = {} if tick == 0 else {1 + len(tokens) + len(pieces): 0}
+    rows = [pltpu.VMEM((3, hid, width), bf16)] if tick == EXTRA else []
     token_specs = [HBM] * len(tokens)
     if tick == 0:
         token_specs[3] = VMEM
         tokens = in_hbm(*tokens[:3]) + tokens[3:]
     return pl.pallas_call(
         functools.partial(unit_kernel, tick, len(pieces), block),
-        in_specs=[SMEM] + token_specs + [HBM] * len(pieces) + [VMEM],
-        out_specs=[VMEM, HBM],
-        out_shape=[
-            jax.ShapeDtypeStruct((3, hid, width), bf16),
-            jax.ShapeDtypeStruct(tokens[0].shape if tick == 0 else (span, width), bf16),
-        ],
-        input_output_aliases={} if tick == 0 else {1 + len(tokens) + len(pieces): 0},
-        scratch_shapes=[
+        in_specs=[SMEM] + token_specs + [HBM] * len(pieces) + [VMEM] * len(states),
+        out_specs=[VMEM] * len(states) + [HBM],
+        out_shape=state_shapes
+        + [jax.ShapeDtypeStruct(tokens[0].shape if tick == 0 else (span, width), bf16)],
+        input_output_aliases=aliases,
+        scratch_shapes=rows
+        + [
             pltpu.VMEM((3, span, width), bf16),
             pltpu.VMEM((span, width), f32),
             pltpu.VMEM((span, width), bf16),
             pltpu.SemaphoreType.DMA((4 + len(pieces),)),
         ],
         compiler_params=pltpu.CompilerParams(vmem_limit_bytes=LIMIT),
-    )(flags, *tokens, *pieces, state)
+        cost_estimate=pl.CostEstimate(flops=0, bytes_accessed=0, transcendentals=0),
+    )(flags, *tokens, *pieces, *states)
 
 
 def body(fast_state, initial_fast, queries, token_keys, token_values, step_sizes):
     count = lax.axis_size("seq")
     position = lax.axis_index("seq")
     ticks = token_keys.shape[1]
-    flags = jnp.stack([(position + t == count).astype(jnp.int32) for t in range(ticks)])
+    flags = jnp.stack(
+        [(position == count - 1).astype(jnp.int32)]
+        + [
+            ((position + t == count) & (t < ticks - 1)).astype(jnp.int32)
+            for t in range(1, ticks)
+        ]
+    )
 
     def send(value, pairs):
         return lax.ppermute(value, "seq", pairs)
 
     def shift(value, steps):
-        return send(value, [(s, (s + steps) % count) for s in range(count)])
-
+        pairs = [(s, (s + steps) % count) for s in range(count)]
+        if abs(steps) == ticks - 1:
+            pairs = [p for p in pairs if set(p) != {0, count - steps if steps > 0 else count + steps}]
+        return send(value, pairs)
+
+    quads = count // 4
+    cross = [(4 * q + c, 4 * q + c + 2) for q in range(quads) for c in (0, 1)]
+    got = [send(initial_fast, cross)]
+    held = initial_fast
     args = [token_keys, token_values, queries, step_sizes]
     packs = [pack(t, *args) for t in range(1, ticks)]
     tokens = [shift(packs[t - 1], -t) for t in range(1, ticks)]
-
-    last = 4
-    width = count
-    held = initial_fast
-    while width > last:
-        radix = 4 if width % (4 * last) == 0 else 2
+    tokens_x = send(packs[-1], [(0, count - 1)])
+    width = quads
+    while width > 1:
+        held = join([held] + got)
+        radix = 4 if width % 4 == 0 else 2
         width //= radix
-        base = count - width
+        base = quads - width
         got = [
-            send(held, [(base - j * width + i, base + i) for i in range(width)])
+            send(
+                held,
+                [
+                    (4 * (base - j * width + i) + c, 4 * (base + i) + c)
+                    for i in range(width)
+                    for c in (2, 3)
+                ],
+            )
             for j in range(1, radix)
         ]
-        held = join([held] + got)
-    base = count - last
-    swap = lambda value, bit: send(
-        value, [(base + i, base + (i ^ bit)) for i in range(last)]
-    )
-    pieces = [held, swap(held, 2)]
-    pieces += [swap(piece, 1) for piece in pieces]
+    held = join([held] + got)
+    swapped = send(held, [(count - 2, count - 1), (count - 1, count - 2)])
+    pieces = [held, swapped]
 
     state, out = unit(0, flags, args, fast_state, [])
-    answers = []
+    state, answer1 = unit(1, flags, tokens[:1], state, pieces)
+    (answer_x,) = unit(EXTRA, flags, [tokens_x], None, pieces)
+    back = [shift(answer1, 1)]
+    for t in range(2, ticks):
+        state, answer = unit(t, flags, tokens[t - 1 : t], state, pieces)
+        back.append(shift(answer, t))
+    back_x = send(answer_x, [(count - 1, 0)])
+    back[-1] = jnp.where(position == 0, back_x, back[-1])
     for t in range(1, ticks):
-        state, answer = unit(t, flags, [tokens[t - 1]], state, pieces)
-        answers.append(shift(answer, t))
-    for t in range(1, ticks):
-        out = lax.dynamic_update_slice(out, answers[t - 1][None, None], (0, t, 0, 0))
+        out = lax.dynamic_update_slice(out, back[t - 1][None, None], (0, t, 0, 0))
     return out
 
 

time: 144 us -> 143 us (level)
  the two profiles are of different devices: /device:TPU:1 before, /device:TPU:4 now
where the time goes in v4:
time: 143 us; the launch traced here: 142 us
  starting transfers between devices  52.1 us (36%)
  Pallas kernels  42.5 us (30%)
  waiting for transfers between devices  38.1 us (27%)
  local copies, waits for them, and re-layouts  8.44 us (6%)
    ppermute x13, starting transfers between devices, send(): return lax.ppermute(value, 'seq', pairs)  52.1 us
    ppermute x13, waiting for transfers between devices, send(): return lax.ppermute(value, 'seq', pairs)  38.1 us
    pallas_call x5, Pallas kernels, unit(): pl.pallas_call(functools.partial(unit_kernel, tick, len(pieces), block),...  35.8 us
    pallas_call x3, Pallas kernels, pack(): pl.pallas_call(functools.partial(pack_kernel, tick), in_specs=[HBM, HBM,...  6.64 us
    unnamed x10, local copies, waits for them, and re-layouts  4.91 us
    dynamic_update_slice x2, local copies, waits for them, and re-layouts, body(): out = lax.dynamic_update_slice(out, back[t - 1][None, None], (0, t, 0, 0))  3.54 us
  transfers between devices with their start and end apart: 13, of which 4 were waited for; matrix products, arithmetic and copies ran while one was open for 3% of the time, Pallas kernels for 30%

profile of v4, /device:TPU:4, one launch (start us, length us, event | category | flops | bytes accessed | tf_op | source)
XLA Modules:
  0.0 142.3 jit_solution(3087154836843178987)
XLA Ops:
  0.0 1.3 collective-permute-start.1
  1.3 7.4 %collective-permute-done.1.refs_1_ = bf16[3,64,512]{2,1,0:T(8,128)(2,1)S(1)} collective-permute-done((bf16[3,64,512]{2,1,0:T(8,128)(2,1)}, bf16[3,64,512]{2,1,0:T(8,128)(2,1)S(1)}, u32[]{:S(2)}, u32[]{:S(2)}) %collective-permute-start.1) | collective-permute-done | bytes 196640 | tf_op jit(solution)/shard_map/ppermute | solution.py:262
  8.7 0.0 copy-start.3
  8.7 0.9 copy-done.3
  9.7 0.0 copy-start.4
  9.7 0.7 collective-permute-start.2
  10.4 0.7 collective-permute-start.3
  11.1 6.7 %collective-permute-start.4 = (bf16[3,128,512]{2,1,0:T(8,128)(2,1)S(1)}, bf16[3,128,512]{2,1,0:T(8,128)(2,1)S(1)}, u32[]{:S(2)}, u32[]{:S(2)}) collective-permute-start(bf16[3,128,512]{2,1,0:T(8,128)(2,1)S(1)} %join.2.refs_0_), channel_id=1, source_target_pairs={{2,14},{3,15},{18,30},{19,31}} | collective-permute-start | bytes 1179656 | tf_op jit(solution)/shard_map/ppermute | solution.py:262
  17.8 0.0 collective-permute-done.2.refs_1_
  17.9 0.0 collective-permute-done.3.refs_2_
  17.9 7.5 %collective-permute-done.4.refs_3_ = bf16[3,128,512]{2,1,0:T(8,128)(2,1)S(1)} collective-permute-done((bf16[3,128,512]{2,1,0:T(8,128)(2,1)S(1)}, bf16[3,128,512]{2,1,0:T(8,128)(2,1)S(1)}, u32[]{:S(2)}, u32[]{:S(2)}) %collective-permute-start.4) | collective-permute-done | bytes 393248 | tf_op jit(solution)/shard_map/ppermute | solution.py:262
  25.4 0.1 join.3.refs_1_
  25.5 0.8 collective-permute-start.5
  26.2 0.0 copy-done.4
  26.2 2.2 %shard_map.65 = bf16[3,384,512]{2,1,0:T(8,128)(2,1)} custom-call(bf16[1,4,384,512]{3,2,1,0:T(8,128)(2,1)} %k_ref.5, bf16[1,4,384,512]{3,2,1,0:T(8,128)(2,1)} %v_ref.5, bf16[1,4,384,512]{3,2,1,0:T(8,128)(2,1)} %q_ref.5, bf16[1,4,384]{2,1,0:T(4,128)(2,1)S(1)} %copy-done.4), custom_call_target="tpu_custom_call" | custom-call | tf_op jit(solution)/shard_map/pallas_call | solution.py:69
  28.5 0.1 collective-permute-start
  28.5 2.2 %shard_map.67 = bf16[3,384,512]{2,1,0:T(8,128)(2,1)} custom-call(bf16[1,4,384,512]{3,2,1,0:T(8,128)(2,1)} %k_ref.5, bf16[1,4,384,512]{3,2,1,0:T(8,128)(2,1)} %v_ref.5, bf16[1,4,384,512]{3,2,1,0:T(8,128)(2,1)} %q_ref.5, bf16[1,4,384]{2,1,0:T(4,128)(2,1)S(1)} %copy-done.4), custom_call_target="tpu_custom_call" | custom-call | tf_op jit(solution)/shard_map/pallas_call | solution.py:69
  30.7 19.5 %collective-permute-start.7 = (bf16[3,384,512]{2,1,0:T(8,128)(2,1)}, bf16[3,384,512]{2,1,0:T(8,128)(2,1)}, u32[]{:S(2)}, u32[]{:S(2)}) collective-permute-start(bf16[3,384,512]{2,1,0:T(8,128)(2,1)} %shard_map.67), channel_id=1, source_target_pairs={{0,14},{1,15},{2,0},{3,1},{4,2},{5,3},{6,4},{7,5},{8,6},{9,7},{10,... | collective-permute-start | bytes 3538952 | tf_op jit(solution)/shard_map/ppermute | solution.py:262
  50.2 2.2 %shard_map.69 = bf16[3,384,512]{2,1,0:T(8,128)(2,1)} custom-call(bf16[1,4,384,512]{3,2,1,0:T(8,128)(2,1)} %k_ref.5, bf16[1,4,384,512]{3,2,1,0:T(8,128)(2,1)} %v_ref.5, bf16[1,4,384,512]{3,2,1,0:T(8,128)(2,1)} %q_ref.5, bf16[1,4,384]{2,1,0:T(4,128)(2,1)S(1)} %copy-done.4), custom_call_target="tpu_custom_call" | custom-call | tf_op jit(solution)/shard_map/pallas_call | solution.py:69
  52.4 1.7 %collective-permute-start.9 = (bf16[3,384,512]{2,1,0:T(8,128)(2,1)}, bf16[3,384,512]{2,1,0:T(8,128)(2,1)}, u32[]{:S(2)}, u32[]{:S(2)}) collective-permute-start(bf16[3,384,512]{2,1,0:T(8,128)(2,1)} %shard_map.69), channel_id=1, source_target_pairs={{0,15},{16,31}} | collective-permute-start | bytes 3538952 | tf_op jit(solution)/shard_map/ppermute | solution.py:262
  54.1 1.9 %collective-permute-start.11 = (bf16[3,384,512]{2,1,0:T(8,128)(2,1)}, bf16[3,384,512]{2,1,0:T(8,128)(2,1)}, u32[]{:S(2)}, u32[]{:S(2)}) collective-permute-start(bf16[3,384,512]{2,1,0:T(8,128)(2,1)} %shard_map.69), channel_id=1, source_target_pairs={{1,14},{2,15},{3,0},{4,1},{5,2},{6,3},{7,4},{8,5},{9,6},{10,7},{11... | collective-permute-start | bytes 3538952 | tf_op jit(solution)/shard_map/ppermute | solution.py:262
  56.1 0.1 add_convert_fusion.flags_ref
  56.1 0.0 copy-start.2
  56.2 1.9 %copy-done.2 = bf16[1,3,1024,512]{3,2,1,0:T(8,128)(2,1)S(1)} copy-done((bf16[1,3,1024,512]{3,2,1,0:T(8,128)(2,1)S(1)}, bf16[1,3,1024,512]{3,2,1,0:T(8,128)(2,1)}, u32[]{:S(2)}) %copy-start.2) | copy-done | bytes 3145752
  58.0 9.0 %shard_map.64 = (bf16[3,1024,512]{2,1,0:T(8,128)(2,1)S(1)}, bf16[1,4,384,512]{3,2,1,0:T(8,128)(2,1)}) custom-call(s32[4]{0:T(128)S(1)} %add_convert_fusion.flags_ref, bf16[1,4,384,512]{3,2,1,0:T(8,128)(2,1)} %k_ref.5, bf16[1,4,384,512]{3,2,1,0:T(8,128)(2,1)} %v_ref.5, bf16[1,4,384,512]{3,2,1,0:T(8,128)(2,1)} %q_ref.5, bf16[1,4,384]{2,1,0:T(4,128)(2,1)S(1)} %copy-done.4, ...), custom_call_target="tpu_custom_call" | custom-call | tf_op jit(solution)/shard_map/pallas_call | solution.py:230
  67.0 0.0 collective-permute-done.refs_0_
  67.0 0.0 collective-permute-done.5.refs_2_
  67.0 8.5 %shard_map.66 = (bf16[3,1024,512]{2,1,0:T(8,128)(2,1)S(1)}, bf16[384,512]{1,0:T(8,128)(2,1)S(1)}) custom-call(s32[4]{0:T(128)S(1)} %add_convert_fusion.flags_ref, bf16[3,384,512]{2,1,0:T(8,128)(2,1)} %collective-permute-done.refs_0_, bf16[3,512,512]{2,1,0:T(8,128)(2,1)S(1)} %join.3.refs_1_, ...), custom_call_target="tpu_custom_call", output_to_operand_aliasing={{0}: (4, {})} | custom-call | tf_op jit(solution)/shard_map/pallas_call | solution.py:230
  75.6 1.4 %collective-permute-start.6 = (bf16[384,512]{1,0:T(8,128)(2,1)S(1)}, bf16[384,512]{1,0:T(8,128)(2,1)}, u32[]{:S(2)}, u32[]{:S(2)}) collective-permute-start(bf16[384,512]{1,0:T(8,128)(2,1)S(1)} %get-tuple-element.14), channel_id=1, source_target_pairs={{0,1},{1,2},{2,3},{3,4},{4,5},{5,6},{6,7},{7,8},{8,9},{9,10},{10,1... | collective-permute-start | bytes 1179656 | tf_op jit(solution)/shard_map/ppermute | solution.py:262
  77.0 0.6 collective-permute-done.7.refs_0_
  77.6 9.1 %shard_map.68 = (bf16[3,1024,512]{2,1,0:T(8,128)(2,1)S(1)}, bf16[384,512]{1,0:T(8,128)(2,1)}) custom-call(s32[4]{0:T(128)S(1)} %add_convert_fusion.flags_ref, bf16[3,384,512]{2,1,0:T(8,128)(2,1)} %collective-permute-done.7.refs_0_, bf16[3,512,512]{2,1,0:T(8,128)(2,1)S(1)} %join.3.refs_1_, ...), custom_call_target="tpu_custom_call", output_to_operand_aliasing={{0}: (4, {})} | custom-call | tf_op jit(solution)/shard_map/pallas_call | solution.py:230
  86.7 0.0 copy-start
  86.7 1.6 %copy-done = bf16[3,1024,512]{2,1,0:T(8,128)(2,1)} copy-done((bf16[3,1024,512]{2,1,0:T(8,128)(2,1)}, bf16[3,1024,512]{2,1,0:T(8,128)(2,1)S(1)}, u32[]{:S(2)}) %copy-start) | copy-done | bytes 3145752
  88.4 14.6 %collective-permute-start.8 = (bf16[384,512]{1,0:T(8,128)(2,1)}, bf16[384,512]{1,0:T(8,128)(2,1)}, u32[]{:S(2)}, u32[]{:S(2)}) collective-permute-start(bf16[384,512]{1,0:T(8,128)(2,1)} %get-tuple-element.16), channel_id=1, source_target_pairs={{0,2},{1,3},{2,4},{3,5},{4,6},{5,7},{6,8},{7,9},{8,10},{9,11},{10,... | collective-permute-start | bytes 1179656 | tf_op jit(solution)/shard_map/ppermute | solution.py:262
  103.0 0.0 copy-start.1
  103.0 0.0 collective-permute-done.9.refs_0_
  103.0 0.6 shard_map.70
  103.6 0.8 collective-permute-start.10
  104.4 0.0 collective-permute-done.11.refs_0_
  104.4 0.4 copy-done.1
  104.9 8.5 %shard_map.71 = (bf16[3,1024,512]{2,1,0:T(8,128)(2,1)S(1)}, bf16[384,512]{1,0:T(8,128)(2,1)S(1)}) custom-call(s32[4]{0:T(128)S(1)} %add_convert_fusion.flags_ref, bf16[3,384,512]{2,1,0:T(8,128)(2,1)} %collective-permute-done.11.refs_0_, bf16[3,512,512]{2,1,0:T(8,128)(2,1)S(1)} %join.3.refs_1_, ...), custom_call_target="tpu_custom_call", output_to_operand_aliasing={{0}: (4, {})} | custom-call | tf_op jit(solution)/shard_map/pallas_call | solution.py:230
  113.4 1.9 %collective-permute-start.12 = (bf16[384,512]{1,0:T(8,128)(2,1)S(1)}, bf16[384,512]{1,0:T(8,128)(2,1)S(1)}, u32[]{:S(2)}, u32[]{:S(2)}) collective-permute-start(bf16[384,512]{1,0:T(8,128)(2,1)S(1)} %get-tuple-element.18), channel_id=1, source_target_pairs={{0,3},{1,4},{2,5},{3,6},{4,7},{5,8},{6,9},{7,10},{8,11},{9,12},{10... | collective-permute-start | bytes 1179656 | tf_op jit(solution)/shard_map/ppermute | solution.py:262
  115.4 0.0 collective-permute-done.6
  115.4 1.8 %bitcast_dynamic-update-slice_fusion.2 = bf16[1,4,384,512]{3,2,1,0:T(8,128)(2,1)} fusion(bf16[1,4,384,512]{3,2,1,0:T(8,128)(2,1)} %get-tuple-element.12, bf16[384,512]{1,0:T(8,128)(2,1)} %collective-permute-done.6), kind=kLoop, calls=%fused_computation.2 | loop fusion | bytes 786432 | tf_op jit(solution)/shard_map/dynamic_update_slice | solution.py:309
  117.1 0.0 collective-permute-done.8
  117.1 1.8 %bitcast_dynamic-update-slice_fusion.1 = bf16[1,4,384,512]{3,2,1,0:T(8,128)(2,1)} fusion(bf16[1,4,384,512]{3,2,1,0:T(8,128)(2,1)} %bitcast_dynamic-update-slice_fusion.2, bf16[384,512]{1,0:T(8,128)(2,1)} %collective-permute-done.8), kind=kLoop, calls=%fused_computation.1 | loop fusion | bytes 786432 | tf_op jit(solution)/shard_map/dynamic_update_slice | solution.py:309
  118.9 0.0 collective-permute-done.10
  118.9 22.6 %collective-permute-done.12 = bf16[384,512]{1,0:T(8,128)(2,1)S(1)} collective-permute-done((bf16[384,512]{1,0:T(8,128)(2,1)S(1)}, bf16[384,512]{1,0:T(8,128)(2,1)S(1)}, u32[]{:S(2)}, u32[]{:S(2)}) %collective-permute-start.12) | collective-permute-done | bytes 393248 | tf_op jit(solution)/shard_map/ppermute | solution.py:262
  141.5 0.8 bitcast_dynamic-update-slice_fusion
  (1 shorter events, 0.0 us)
Async XLA Ops:
  0.0 8.7 %collective-permute-start.1 = (bf16[3,64,512]{2,1,0:T(8,128)(2,1)}, bf16[3,64,512]{2,1,0:T(8,128)(2,1)S(1)}, u32[]{:S(2)}, u32[]{:S(2)}) collective-permute-start(bf16[3,64,512]{2,1,0:T(8,128)(2,1)} %refs_0_.3), channel_id=1, source_target_pairs={{0,2},{1,3},{4,6},{5,7},{8,10},{9,11},{12,14},{13,15},{16,18},{17,... | collective-permute-start | bytes 589832 | tf_op jit(solution)/shard_map/ppermute | solution.py:262
  8.7 0.9 copy-start.3
  9.7 16.5 %copy-start.4 = (bf16[1,4,384]{2,1,0:T(4,128)(2,1)S(1)}, bf16[1,4,384]{2,1,0:T(4,128)(2,1)}, u32[]{:S(2)}) copy-start(bf16[1,4,384]{2,1,0:T(4,128)(2,1)} %r_ref.5) | copy-start | bytes 9220
  9.7 8.1 %collective-permute-start.2 = (bf16[3,128,512]{2,1,0:T(8,128)(2,1)S(1)}, bf16[3,128,512]{2,1,0:T(8,128)(2,1)S(1)}, u32[]{:S(2)}, u32[]{:S(2)}) collective-permute-start(bf16[3,128,512]{2,1,0:T(8,128)(2,1)S(1)} %join.2.refs_0_), channel_id=1, source_target_pairs={{10,14},{11,15},{26,30},{27,31}} | collective-permute-start | bytes 1179656 | tf_op jit(solution)/shard_map/ppermute | solution.py:262
  10.4 7.5 %collective-permute-start.3 = (bf16[3,128,512]{2,1,0:T(8,128)(2,1)S(1)}, bf16[3,128,512]{2,1,0:T(8,128)(2,1)S(1)}, u32[]{:S(2)}, u32[]{:S(2)}) collective-permute-start(bf16[3,128,512]{2,1,0:T(8,128)(2,1)S(1)} %join.2.refs_0_), channel_id=1, source_target_pairs={{6,14},{7,15},{22,30},{23,31}} | collective-permute-start | bytes 1179656 | tf_op jit(solution)/shard_map/ppermute | solution.py:262
  11.1 14.3 %collective-permute-start.4 = (bf16[3,128,512]{2,1,0:T(8,128)(2,1)S(1)}, bf16[3,128,512]{2,1,0:T(8,128)(2,1)S(1)}, u32[]{:S(2)}, u32[]{:S(2)}) collective-permute-start(bf16[3,128,512]{2,1,0:T(8,128)(2,1)S(1)} %join.2.refs_0_), channel_id=1, source_target_pairs={{2,14},{3,15},{18,30},{19,31}} | collective-permute-start | bytes 1179656 | tf_op jit(solution)/shard_map/ppermute | solution.py:262
  25.5 41.6 %collective-permute-start.5 = (bf16[3,512,512]{2,1,0:T(8,128)(2,1)S(1)}, bf16[3,512,512]{2,1,0:T(8,128)(2,1)S(1)}, u32[]{:S(2)}, u32[]{:S(2)}) collective-permute-start(bf16[3,512,512]{2,1,0:T(8,128)(2,1)S(1)} %join.3.refs_1_), channel_id=1, source_target_pairs={{14,15},{15,14},{30,31},{31,30}} | collective-permute-start | bytes 4718600 | tf_op jit(solution)/shard_map/ppermute | solution.py:262
  28.5 38.6 %collective-permute-start = (bf16[3,384,512]{2,1,0:T(8,128)(2,1)}, bf16[3,384,512]{2,1,0:T(8,128)(2,1)}, u32[]{:S(2)}, u32[]{:S(2)}) collective-permute-start(bf16[3,384,512]{2,1,0:T(8,128)(2,1)} %shard_map.65), channel_id=1, source_target_pairs={{0,15},{1,0},{2,1},{3,2},{4,3},{5,4},{6,5},{7,6},{8,7},{9,8},{10,9... | collective-permute-start | bytes 3538952 | tf_op jit(solution)/shard_map/ppermute | solution.py:262
  30.7 46.9 %collective-permute-start.7 = (bf16[3,384,512]{2,1,0:T(8,128)(2,1)}, bf16[3,384,512]{2,1,0:T(8,128)(2,1)}, u32[]{:S(2)}, u32[]{:S(2)}) collective-permute-start(bf16[3,384,512]{2,1,0:T(8,128)(2,1)} %shard_map.67), channel_id=1, source_target_pairs={{0,14},{1,15},{2,0},{3,1},{4,2},{5,3},{6,4},{7,5},{8,6},{9,7},{10,... | collective-permute-start | bytes 3538952 | tf_op jit(solution)/shard_map/ppermute | solution.py:262
  52.4 50.6 %collective-permute-start.9 = (bf16[3,384,512]{2,1,0:T(8,128)(2,1)}, bf16[3,384,512]{2,1,0:T(8,128)(2,1)}, u32[]{:S(2)}, u32[]{:S(2)}) collective-permute-start(bf16[3,384,512]{2,1,0:T(8,128)(2,1)} %shard_map.69), channel_id=1, source_target_pairs={{0,15},{16,31}} | collective-permute-start | bytes 3538952 | tf_op jit(solution)/shard_map/ppermute | solution.py:262
  54.1 50.3 %collective-permute-start.11 = (bf16[3,384,512]{2,1,0:T(8,128)(2,1)}, bf16[3,384,512]{2,1,0:T(8,128)(2,1)}, u32[]{:S(2)}, u32[]{:S(2)}) collective-permute-start(bf16[3,384,512]{2,1,0:T(8,128)(2,1)} %shard_map.69), channel_id=1, source_target_pairs={{1,14},{2,15},{3,0},{4,1},{5,2},{6,3},{7,4},{8,5},{9,6},{10,7},{11... | collective-permute-start | bytes 3538952 | tf_op jit(solution)/shard_map/ppermute | solution.py:262
  56.1 1.9 %copy-start.2 = (bf16[1,3,1024,512]{3,2,1,0:T(8,128)(2,1)S(1)}, bf16[1,3,1024,512]{3,2,1,0:T(8,128)(2,1)}, u32[]{:S(2)}) copy-start(bf16[1,3,1024,512]{3,2,1,0:T(8,128)(2,1)} %refs_4_.1) | copy-start | bytes 9437188
  75.6 39.8 %collective-permute-start.6 = (bf16[384,512]{1,0:T(8,128)(2,1)S(1)}, bf16[384,512]{1,0:T(8,128)(2,1)}, u32[]{:S(2)}, u32[]{:S(2)}) collective-permute-start(bf16[384,512]{1,0:T(8,128)(2,1)S(1)} %get-tuple-element.14), channel_id=1, source_target_pairs={{0,1},{1,2},{2,3},{3,4},{4,5},{5,6},{6,7},{7,8},{8,9},{9,10},{10,1... | collective-permute-start | bytes 1179656 | tf_op jit(solution)/shard_map/ppermute | solution.py:262
  86.7 1.7 %copy-start = (bf16[3,1024,512]{2,1,0:T(8,128)(2,1)}, bf16[3,1024,512]{2,1,0:T(8,128)(2,1)S(1)}, u32[]{:S(2)}) copy-start(bf16[3,1024,512]{2,1,0:T(8,128)(2,1)S(1)} %get-tuple-element.17.refs_3_) | copy-start | bytes 9437188
  88.4 28.8 %collective-permute-start.8 = (bf16[384,512]{1,0:T(8,128)(2,1)}, bf16[384,512]{1,0:T(8,128)(2,1)}, u32[]{:S(2)}, u32[]{:S(2)}) collective-permute-start(bf16[384,512]{1,0:T(8,128)(2,1)} %get-tuple-element.16), channel_id=1, source_target_pairs={{0,2},{1,3},{2,4},{3,5},{4,6},{5,7},{6,8},{7,9},{8,10},{9,11},{10,... | collective-permute-start | bytes 1179656 | tf_op jit(solution)/shard_map/ppermute | solution.py:262
  103.0 1.9 %copy-start.1 = (bf16[3,1024,512]{2,1,0:T(8,128)(2,1)S(1)}, bf16[3,1024,512]{2,1,0:T(8,128)(2,1)}, u32[]{:S(2)}) copy-start(bf16[3,1024,512]{2,1,0:T(8,128)(2,1)} %copy-done) | copy-start | bytes 9437188
  103.6 15.3 %collective-permute-start.10 = (bf16[384,512]{1,0:T(8,128)(2,1)S(1)}, bf16[384,512]{1,0:T(8,128)(2,1)S(1)}, u32[]{:S(2)}, u32[]{:S(2)}) collective-permute-start(bf16[384,512]{1,0:T(8,128)(2,1)S(1)} %shard_map.70), channel_id=1, source_target_pairs={{15,0},{31,16}} | collective-permute-start | bytes 1179656 | tf_op jit(solution)/shard_map/ppermute | solution.py:262
  113.4 28.0 %collective-permute-start.12 = (bf16[384,512]{1,0:T(8,128)(2,1)S(1)}, bf16[384,512]{1,0:T(8,128)(2,1)S(1)}, u32[]{:S(2)}, u32[]{:S(2)}) collective-permute-start(bf16[384,512]{1,0:T(8,128)(2,1)S(1)} %get-tuple-element.18), channel_id=1, source_target_pairs={{0,3},{1,4},{2,5},{3,6},{4,7},{5,8},{6,9},{7,10},{8,11},{9,12},{10... | collective-permute-start | bytes 1179656 | tf_op jit(solution)/shard_map/ppermute | solution.py:262

commit v5 on v4

--- a/solution.py
+++ b/solution.py
@@ -45,7 +45,9 @@
     )
 
 
-def pack_kernel(tick, k_ref, v_ref, q_ref, r_ref, o_ref, tok, sems):
+def pack_kernel(tick, k_ref, v_ref, q_ref, r_hbm, o_ref, tok, r_ref, sems):
+    rates = pltpu.make_async_copy(r_hbm, r_ref, sems.at[6])
+    rates.start()
     sources = (k_ref, v_ref, q_ref)
     loads = [
         pltpu.make_async_copy(sources[i].at[0, tick], tok.at[i], sems.at[i])
@@ -54,6 +56,7 @@
     stores = [pltpu.make_async_copy(tok.at[i], o_ref.at[i], sems.at[3 + i]) for i in range(3)]
     for i in (1, 0, 2):
         loads[i].start()
+    rates.wait()
     loads[1].wait()
     tok[1] = scaled_values(r_ref[0, tick : tick + 1, :], tok[1])
     stores[1].start()
@@ -68,13 +71,17 @@
     _, _, span, width = keys.shape
     return pl.pallas_call(
         functools.partial(pack_kernel, tick),
-        in_specs=[HBM, HBM, HBM, VMEM],
+        in_specs=[HBM] * 4,
         out_specs=HBM,
         out_shape=jax.ShapeDtypeStruct((3, span, width), bf16),
-        scratch_shapes=[pltpu.VMEM((3, span, width), bf16), pltpu.SemaphoreType.DMA((6,))],
+        scratch_shapes=[
+            pltpu.VMEM((3, span, width), bf16),
+            pltpu.VMEM(steps.shape, bf16),
+            pltpu.SemaphoreType.DMA((7,)),
+        ],
         compiler_params=pltpu.CompilerParams(vmem_limit_bytes=LIMIT),
         cost_estimate=pl.CostEstimate(flops=0, bytes_accessed=0, transcendentals=0),
-    )(*in_hbm(keys, values, queries), steps)
+    )(*in_hbm(keys, values, queries, steps))
 
 
 def join_kernel(*refs):
@@ -298,16 +305,36 @@
 
     state, out = unit(0, flags, args, fast_state, [])
     state, answer1 = unit(1, flags, tokens[:1], state, pieces)
-    (answer_x,) = unit(EXTRA, flags, [tokens_x], None, pieces)
+    (answer_x,) = unit(EXTRA, flags, [tokens_x], None, in_hbm(*pieces))
     back = [shift(answer1, 1)]
     for t in range(2, ticks):
-        state, answer = unit(t, flags, tokens[t - 1 : t], state, pieces)
+        restart = pieces if t < ticks - 1 else []
+        state, answer = unit(t, flags, tokens[t - 1 : t], state, restart)
+        if t == ticks - 2:
+            state = keep(state)
         back.append(shift(answer, t))
     back_x = send(answer_x, [(count - 1, 0)])
     back[-1] = jnp.where(position == 0, back_x, back[-1])
     for t in range(1, ticks):
         out = lax.dynamic_update_slice(out, back[t - 1][None, None], (0, t, 0, 0))
     return out
+
+
+def keep_kernel(state_ref, kept_ref):
+    del state_ref, kept_ref
+
+
+def keep(state):
+    return pl.pallas_call(
+        keep_kernel,
+        in_specs=[VMEM],
+        out_specs=VMEM,
+        out_shape=jax.ShapeDtypeStruct(state.shape, state.dtype),
+        input_output_aliases={0: 0},
+        cost_estimate=pl.CostEstimate(flops=0, bytes_accessed=0, transcendentals=0),
+        compiler_params=pltpu.CompilerParams(vmem_limit_bytes=1 << 20),
+        name="keep",
+    )(state)
 
 
 def solution(mesh):

time: 143 us -> 145 us (1.014)
  the two profiles are of different devices: /device:TPU:4 before, /device:TPU:6 now
where the time goes in v5:
time: 145 us
  starting transfers between devices  55.8 us (38%)
  Pallas kernels  43.5 us (30%)
  waiting for transfers between devices  37.8 us (26%)
  local copies, waits for them, and re-layouts  6.36 us (4%)
    ppermute x13, starting transfers between devices, send(): return lax.ppermute(value, 'seq', pairs)  55.8 us
    ppermute x13, waiting for transfers between devices, send(): return lax.ppermute(value, 'seq', pairs)  37.8 us
    pallas_call x5, Pallas kernels, unit(): pl.pallas_call(functools.partial(unit_kernel, tick, len(pieces), block),...  35.4 us
    pallas_call x3, Pallas kernels, pack(): pl.pallas_call(functools.partial(pack_kernel, tick), in_specs=[HBM] * 4,...  6.77 us
    dynamic_update_slice x2, local copies, waits for them, and re-layouts, body(): out = lax.dynamic_update_slice(out, back[t - 1][None, None], (0, t, 0, 0))  3.54 us
  transfers between devices with their start and end apart: 13, of which 4 were waited for; matrix products, arithmetic and copies ran while one was open for 3% of the time, Pallas kernels for 29%

profile of v5, /device:TPU:6, one launch (start us, length us, event | category | flops | bytes accessed | tf_op | source)
XLA Modules:
  0.0 144.5 jit_solution(15345450428529667558)
XLA Ops:
  0.0 1.3 collective-permute-start.1
  1.3 7.4 %collective-permute-done.1.refs_1_ = bf16[3,64,512]{2,1,0:T(8,128)(2,1)S(1)} collective-permute-done((bf16[3,64,512]{2,1,0:T(8,128)(2,1)}, bf16[3,64,512]{2,1,0:T(8,128)(2,1)S(1)}, u32[]{:S(2)}, u32[]{:S(2)}) %collective-permute-start.1) | collective-permute-done | bytes 196640 | tf_op jit(solution)/shard_map/ppermute | solution.py:269
  8.7 0.0 copy-start.1
  8.7 0.9 copy-done.1
  9.7 0.7 collective-permute-start.2
  10.4 0.7 collective-permute-start.3
  11.1 6.7 %collective-permute-start.4 = (bf16[3,128,512]{2,1,0:T(8,128)(2,1)S(1)}, bf16[3,128,512]{2,1,0:T(8,128)(2,1)S(1)}, u32[]{:S(2)}, u32[]{:S(2)}) collective-permute-start(bf16[3,128,512]{2,1,0:T(8,128)(2,1)S(1)} %join.2.refs_0_), channel_id=1, source_target_pairs={{2,14},{3,15},{18,30},{19,31}} | collective-permute-start | bytes 1179656 | tf_op jit(solution)/shard_map/ppermute | solution.py:269
  17.8 0.0 collective-permute-done.2.refs_1_
  17.8 0.0 collective-permute-done.3.refs_2_
  17.9 7.5 %collective-permute-done.4.refs_3_ = bf16[3,128,512]{2,1,0:T(8,128)(2,1)S(1)} collective-permute-done((bf16[3,128,512]{2,1,0:T(8,128)(2,1)S(1)}, bf16[3,128,512]{2,1,0:T(8,128)(2,1)S(1)}, u32[]{:S(2)}, u32[]{:S(2)}) %collective-permute-start.4) | collective-permute-done | bytes 393248 | tf_op jit(solution)/shard_map/ppermute | solution.py:269
  25.4 1.3 join.3.refs_1_
  26.6 1.8 %collective-permute-start.5 = (bf16[3,512,512]{2,1,0:T(8,128)(2,1)}, bf16[3,512,512]{2,1,0:T(8,128)(2,1)}, u32[]{:S(2)}, u32[]{:S(2)}) collective-permute-start(bf16[3,512,512]{2,1,0:T(8,128)(2,1)} %join.3.refs_1_), channel_id=1, source_target_pairs={{14,15},{15,14},{30,31},{31,30}} | collective-permute-start | bytes 4718600 | tf_op jit(solution)/shard_map/ppermute | solution.py:269
  28.4 2.2 %shard_map.65 = bf16[3,384,512]{2,1,0:T(8,128)(2,1)} custom-call(bf16[1,4,384,512]{3,2,1,0:T(8,128)(2,1)} %k_ref.5, bf16[1,4,384,512]{3,2,1,0:T(8,128)(2,1)} %v_ref.5, bf16[1,4,384,512]{3,2,1,0:T(8,128)(2,1)} %q_ref.5, bf16[1,4,384]{2,1,0:T(4,128)(2,1)} %r_hbm.5), custom_call_target="tpu_custom_call" | custom-call | tf_op jit(solution)/shard_map/pallas_call | solution.py:72
  30.6 0.1 collective-permute-start
  30.7 2.3 %shard_map.67 = bf16[3,384,512]{2,1,0:T(8,128)(2,1)} custom-call(bf16[1,4,384,512]{3,2,1,0:T(8,128)(2,1)} %k_ref.5, bf16[1,4,384,512]{3,2,1,0:T(8,128)(2,1)} %v_ref.5, bf16[1,4,384,512]{3,2,1,0:T(8,128)(2,1)} %q_ref.5, bf16[1,4,384]{2,1,0:T(4,128)(2,1)} %r_hbm.5), custom_call_target="tpu_custom_call" | custom-call | tf_op jit(solution)/shard_map/pallas_call | solution.py:72
  33.0 0.0 copy-start.2
  33.0 18.4 %collective-permute-start.7 = (bf16[3,384,512]{2,1,0:T(8,128)(2,1)}, bf16[3,384,512]{2,1,0:T(8,128)(2,1)}, u32[]{:S(2)}, u32[]{:S(2)}) collective-permute-start(bf16[3,384,512]{2,1,0:T(8,128)(2,1)} %shard_map.67), channel_id=1, source_target_pairs={{0,14},{1,15},{2,0},{3,1},{4,2},{5,3},{6,4},{7,5},{8,6},{9,7},{10,... | collective-permute-start | bytes 3538952 | tf_op jit(solution)/shard_map/ppermute | solution.py:269
  51.5 2.3 %shard_map.69 = bf16[3,384,512]{2,1,0:T(8,128)(2,1)} custom-call(bf16[1,4,384,512]{3,2,1,0:T(8,128)(2,1)} %k_ref.5, bf16[1,4,384,512]{3,2,1,0:T(8,128)(2,1)} %v_ref.5, bf16[1,4,384,512]{3,2,1,0:T(8,128)(2,1)} %q_ref.5, bf16[1,4,384]{2,1,0:T(4,128)(2,1)} %r_hbm.5), custom_call_target="tpu_custom_call" | custom-call | tf_op jit(solution)/shard_map/pallas_call | solution.py:72
  53.7 1.7 %collective-permute-start.9 = (bf16[3,384,512]{2,1,0:T(8,128)(2,1)}, bf16[3,384,512]{2,1,0:T(8,128)(2,1)}, u32[]{:S(2)}, u32[]{:S(2)}) collective-permute-start(bf16[3,384,512]{2,1,0:T(8,128)(2,1)} %shard_map.69), channel_id=1, source_target_pairs={{0,15},{16,31}} | collective-permute-start | bytes 3538952 | tf_op jit(solution)/shard_map/ppermute | solution.py:269
  55.4 1.9 %collective-permute-start.11 = (bf16[3,384,512]{2,1,0:T(8,128)(2,1)}, bf16[3,384,512]{2,1,0:T(8,128)(2,1)}, u32[]{:S(2)}, u32[]{:S(2)}) collective-permute-start(bf16[3,384,512]{2,1,0:T(8,128)(2,1)} %shard_map.69), channel_id=1, source_target_pairs={{1,14},{2,15},{3,0},{4,1},{5,2},{6,3},{7,4},{8,5},{9,6},{10,7},{11... | collective-permute-start | bytes 3538952 | tf_op jit(solution)/shard_map/ppermute | solution.py:269
  57.4 0.1 add_convert_fusion.flags_ref
  57.4 0.0 copy-done.2
  57.5 0.0 copy-start
  57.5 1.9 %copy-done = bf16[1,3,1024,512]{3,2,1,0:T(8,128)(2,1)S(1)} copy-done((bf16[1,3,1024,512]{3,2,1,0:T(8,128)(2,1)S(1)}, bf16[1,3,1024,512]{3,2,1,0:T(8,128)(2,1)}, u32[]{:S(2)}) %copy-start) | copy-done | bytes 3145752
  59.3 9.0 %shard_map.64 = (bf16[3,1024,512]{2,1,0:T(8,128)(2,1)S(1)}, bf16[1,4,384,512]{3,2,1,0:T(8,128)(2,1)}) custom-call(s32[4]{0:T(128)S(1)} %add_convert_fusion.flags_ref, bf16[1,4,384,512]{3,2,1,0:T(8,128)(2,1)} %k_ref.5, bf16[1,4,384,512]{3,2,1,0:T(8,128)(2,1)} %v_ref.5, bf16[1,4,384,512]{3,2,1,0:T(8,128)(2,1)} %q_ref.5, bf16[1,4,384]{2,1,0:T(4,128)(2,1)S(1)} %copy-done.2, ...), custom_call_target="tpu_custom_call" | custom-call | tf_op jit(solution)/shard_map/pallas_call | solution.py:237
  68.3 0.0 collective-permute-done.refs_0_
  68.3 0.0 collective-permute-done.5.refs_2_
  68.3 8.4 %shard_map.66 = (bf16[3,1024,512]{2,1,0:T(8,128)(2,1)S(1)}, bf16[384,512]{1,0:T(8,128)(2,1)S(1)}) custom-call(s32[4]{0:T(128)S(1)} %add_convert_fusion.flags_ref, bf16[3,384,512]{2,1,0:T(8,128)(2,1)} %collective-permute-done.refs_0_, bf16[3,512,512]{2,1,0:T(8,128)(2,1)} %join.3.refs_1_, ...), custom_call_target="tpu_custom_call", output_to_operand_aliasing={{0}: (4, {})} | custom-call | tf_op jit(solution)/shard_map/pallas_call | solution.py:237
  76.8 1.6 %collective-permute-start.6 = (bf16[384,512]{1,0:T(8,128)(2,1)S(1)}, bf16[384,512]{1,0:T(8,128)(2,1)}, u32[]{:S(2)}, u32[]{:S(2)}) collective-permute-start(bf16[384,512]{1,0:T(8,128)(2,1)S(1)} %get-tuple-element.14), channel_id=1, source_target_pairs={{0,1},{1,2},{2,3},{3,4},{4,5},{5,6},{6,7},{7,8},{8,9},{9,10},{10,1... | collective-permute-start | bytes 1179656 | tf_op jit(solution)/shard_map/ppermute | solution.py:269
  78.4 2.1 %collective-permute-done.7.refs_0_ = bf16[3,384,512]{2,1,0:T(8,128)(2,1)} collective-permute-done((bf16[3,384,512]{2,1,0:T(8,128)(2,1)}, bf16[3,384,512]{2,1,0:T(8,128)(2,1)}, u32[]{:S(2)}, u32[]{:S(2)}) %collective-permute-start.7) | collective-permute-done | bytes 1179680 | tf_op jit(solution)/shard_map/ppermute | solution.py:269
  80.5 9.0 %shard_map.68 = (bf16[3,1024,512]{2,1,0:T(8,128)(2,1)S(1)}, bf16[384,512]{1,0:T(8,128)(2,1)}) custom-call(s32[4]{0:T(128)S(1)} %add_convert_fusion.flags_ref, bf16[3,384,512]{2,1,0:T(8,128)(2,1)} %collective-permute-done.7.refs_0_, bf16[3,512,512]{2,1,0:T(8,128)(2,1)} %join.3.refs_1_, ...), custom_call_target="tpu_custom_call", output_to_operand_aliasing={{0}: (4, {})} | custom-call | tf_op jit(solution)/shard_map/pallas_call | solution.py:237
  89.5 18.1 %collective-permute-start.8 = (bf16[384,512]{1,0:T(8,128)(2,1)}, bf16[384,512]{1,0:T(8,128)(2,1)}, u32[]{:S(2)}, u32[]{:S(2)}) collective-permute-start(bf16[384,512]{1,0:T(8,128)(2,1)} %get-tuple-element.16), channel_id=1, source_target_pairs={{0,2},{1,3},{2,4},{3,5},{4,6},{5,7},{6,8},{7,9},{8,10},{9,11},{10,... | collective-permute-start | bytes 1179656 | tf_op jit(solution)/shard_map/ppermute | solution.py:269
  107.6 0.0 collective-permute-done.9.refs_0_
  107.6 0.6 shard_map.70
  108.2 0.9 collective-permute-start.10
  109.1 0.0 collective-permute-done.11.refs_0_
  109.1 8.4 %shard_map.71 = (bf16[3,1024,512]{2,1,0:T(8,128)(2,1)S(1)}, bf16[384,512]{1,0:T(8,128)(2,1)S(1)}) custom-call(s32[4]{0:T(128)S(1)} %add_convert_fusion.flags_ref, bf16[3,384,512]{2,1,0:T(8,128)(2,1)} %collective-permute-done.11.refs_0_, bf16[3,1024,512]{2,1,0:T(8,128)(2,1)S(1)} %keep.1.refs_1_), custom_call_target="tpu_custom_call", output_to_operand_aliasing={{0}: (2, {})} | custom-call | tf_op jit(solution)/shard_map/pallas_call | solution.py:237
  117.5 1.9 %collective-permute-start.12 = (bf16[384,512]{1,0:T(8,128)(2,1)S(1)}, bf16[384,512]{1,0:T(8,128)(2,1)S(1)}, u32[]{:S(2)}, u32[]{:S(2)}) collective-permute-start(bf16[384,512]{1,0:T(8,128)(2,1)S(1)} %get-tuple-element.18), channel_id=1, source_target_pairs={{0,3},{1,4},{2,5},{3,6},{4,7},{5,8},{6,9},{7,10},{8,11},{9,12},{10... | collective-permute-start | bytes 1179656 | tf_op jit(solution)/shard_map/ppermute | solution.py:269
  119.5 0.0 collective-permute-done.6
  119.5 1.8 %bitcast_dynamic-update-slice_fusion.2 = bf16[1,4,384,512]{3,2,1,0:T(8,128)(2,1)} fusion(bf16[1,4,384,512]{3,2,1,0:T(8,128)(2,1)} %get-tuple-element.12, bf16[384,512]{1,0:T(8,128)(2,1)} %collective-permute-done.6), kind=kLoop, calls=%fused_computation.2 | loop fusion | bytes 786432 | tf_op jit(solution)/shard_map/dynamic_update_slice | solution.py:319
  121.2 0.0 collective-permute-done.8
  121.2 1.8 %bitcast_dynamic-update-slice_fusion.1 = bf16[1,4,384,512]{3,2,1,0:T(8,128)(2,1)} fusion(bf16[1,4,384,512]{3,2,1,0:T(8,128)(2,1)} %bitcast_dynamic-update-slice_fusion.2, bf16[384,512]{1,0:T(8,128)(2,1)} %collective-permute-done.8), kind=kLoop, calls=%fused_computation.1 | loop fusion | bytes 786432 | tf_op jit(solution)/shard_map/dynamic_update_slice | solution.py:319
  123.0 0.0 collective-permute-done.10
  123.0 20.7 %collective-permute-done.12 = bf16[384,512]{1,0:T(8,128)(2,1)S(1)} collective-permute-done((bf16[384,512]{1,0:T(8,128)(2,1)S(1)}, bf16[384,512]{1,0:T(8,128)(2,1)S(1)}, u32[]{:S(2)}, u32[]{:S(2)}) %collective-permute-start.12) | collective-permute-done | bytes 393248 | tf_op jit(solution)/shard_map/ppermute | solution.py:269
  143.7 0.8 bitcast_dynamic-update-slice_fusion
  (2 shorter events, 0.0 us)
Async XLA Ops:
  0.0 8.7 %collective-permute-start.1 = (bf16[3,64,512]{2,1,0:T(8,128)(2,1)}, bf16[3,64,512]{2,1,0:T(8,128)(2,1)S(1)}, u32[]{:S(2)}, u32[]{:S(2)}) collective-permute-start(bf16[3,64,512]{2,1,0:T(8,128)(2,1)} %refs_0_.3), channel_id=1, source_target_pairs={{0,2},{1,3},{4,6},{5,7},{8,10},{9,11},{12,14},{13,15},{16,18},{17,... | collective-permute-start | bytes 589832 | tf_op jit(solution)/shard_map/ppermute | solution.py:269
  8.7 0.9 copy-start.1
  9.7 8.1 %collective-permute-start.2 = (bf16[3,128,512]{2,1,0:T(8,128)(2,1)S(1)}, bf16[3,128,512]{2,1,0:T(8,128)(2,1)S(1)}, u32[]{:S(2)}, u32[]{:S(2)}) collective-permute-start(bf16[3,128,512]{2,1,0:T(8,128)(2,1)S(1)} %join.2.refs_0_), channel_id=1, source_target_pairs={{10,14},{11,15},{26,30},{27,31}} | collective-permute-start | bytes 1179656 | tf_op jit(solution)/shard_map/ppermute | solution.py:269
  10.4 7.5 %collective-permute-start.3 = (bf16[3,128,512]{2,1,0:T(8,128)(2,1)S(1)}, bf16[3,128,512]{2,1,0:T(8,128)(2,1)S(1)}, u32[]{:S(2)}, u32[]{:S(2)}) collective-permute-start(bf16[3,128,512]{2,1,0:T(8,128)(2,1)S(1)} %join.2.refs_0_), channel_id=1, source_target_pairs={{6,14},{7,15},{22,30},{23,31}} | collective-permute-start | bytes 1179656 | tf_op jit(solution)/shard_map/ppermute | solution.py:269
  11.1 14.3 %collective-permute-start.4 = (bf16[3,128,512]{2,1,0:T(8,128)(2,1)S(1)}, bf16[3,128,512]{2,1,0:T(8,128)(2,1)S(1)}, u32[]{:S(2)}, u32[]{:S(2)}) collective-permute-start(bf16[3,128,512]{2,1,0:T(8,128)(2,1)S(1)} %join.2.refs_0_), channel_id=1, source_target_pairs={{2,14},{3,15},{18,30},{19,31}} | collective-permute-start | bytes 1179656 | tf_op jit(solution)/shard_map/ppermute | solution.py:269
  26.6 41.7 %collective-permute-start.5 = (bf16[3,512,512]{2,1,0:T(8,128)(2,1)}, bf16[3,512,512]{2,1,0:T(8,128)(2,1)}, u32[]{:S(2)}, u32[]{:S(2)}) collective-permute-start(bf16[3,512,512]{2,1,0:T(8,128)(2,1)} %join.3.refs_1_), channel_id=1, source_target_pairs={{14,15},{15,14},{30,31},{31,30}} | collective-permute-start | bytes 4718600 | tf_op jit(solution)/shard_map/ppermute | solution.py:269
  30.6 37.7 %collective-permute-start = (bf16[3,384,512]{2,1,0:T(8,128)(2,1)}, bf16[3,384,512]{2,1,0:T(8,128)(2,1)}, u32[]{:S(2)}, u32[]{:S(2)}) collective-permute-start(bf16[3,384,512]{2,1,0:T(8,128)(2,1)} %shard_map.65), channel_id=1, source_target_pairs={{0,15},{1,0},{2,1},{3,2},{4,3},{5,4},{6,5},{7,6},{8,7},{9,8},{10,9... | collective-permute-start | bytes 3538952 | tf_op jit(solution)/shard_map/ppermute | solution.py:269
  33.0 24.4 %copy-start.2 = (bf16[1,4,384]{2,1,0:T(4,128)(2,1)S(1)}, bf16[1,4,384]{2,1,0:T(4,128)(2,1)}, u32[]{:S(2)}) copy-start(bf16[1,4,384]{2,1,0:T(4,128)(2,1)} %r_hbm.5) | copy-start | bytes 9220
  33.0 47.4 %collective-permute-start.7 = (bf16[3,384,512]{2,1,0:T(8,128)(2,1)}, bf16[3,384,512]{2,1,0:T(8,128)(2,1)}, u32[]{:S(2)}, u32[]{:S(2)}) collective-permute-start(bf16[3,384,512]{2,1,0:T(8,128)(2,1)} %shard_map.67), channel_id=1, source_target_pairs={{0,14},{1,15},{2,0},{3,1},{4,2},{5,3},{6,4},{7,5},{8,6},{9,7},{10,... | collective-permute-start | bytes 3538952 | tf_op jit(solution)/shard_map/ppermute | solution.py:269
  53.7 53.9 %collective-permute-start.9 = (bf16[3,384,512]{2,1,0:T(8,128)(2,1)}, bf16[3,384,512]{2,1,0:T(8,128)(2,1)}, u32[]{:S(2)}, u32[]{:S(2)}) collective-permute-start(bf16[3,384,512]{2,1,0:T(8,128)(2,1)} %shard_map.69), channel_id=1, source_target_pairs={{0,15},{16,31}} | collective-permute-start | bytes 3538952 | tf_op jit(solution)/shard_map/ppermute | solution.py:269
  55.4 53.7 %collective-permute-start.11 = (bf16[3,384,512]{2,1,0:T(8,128)(2,1)}, bf16[3,384,512]{2,1,0:T(8,128)(2,1)}, u32[]{:S(2)}, u32[]{:S(2)}) collective-permute-start(bf16[3,384,512]{2,1,0:T(8,128)(2,1)} %shard_map.69), channel_id=1, source_target_pairs={{1,14},{2,15},{3,0},{4,1},{5,2},{6,3},{7,4},{8,5},{9,6},{10,7},{11... | collective-permute-start | bytes 3538952 | tf_op jit(solution)/shard_map/ppermute | solution.py:269
  57.5 1.9 %copy-start = (bf16[1,3,1024,512]{3,2,1,0:T(8,128)(2,1)S(1)}, bf16[1,3,1024,512]{3,2,1,0:T(8,128)(2,1)}, u32[]{:S(2)}) copy-start(bf16[1,3,1024,512]{3,2,1,0:T(8,128)(2,1)} %refs_4_.1) | copy-start | bytes 9437188
  76.8 42.7 %collective-permute-start.6 = (bf16[384,512]{1,0:T(8,128)(2,1)S(1)}, bf16[384,512]{1,0:T(8,128)(2,1)}, u32[]{:S(2)}, u32[]{:S(2)}) collective-permute-start(bf16[384,512]{1,0:T(8,128)(2,1)S(1)} %get-tuple-element.14), channel_id=1, source_target_pairs={{0,1},{1,2},{2,3},{3,4},{4,5},{5,6},{6,7},{7,8},{8,9},{9,10},{10,1... | collective-permute-start | bytes 1179656 | tf_op jit(solution)/shard_map/ppermute | solution.py:269
  89.5 31.7 %collective-permute-start.8 = (bf16[384,512]{1,0:T(8,128)(2,1)}, bf16[384,512]{1,0:T(8,128)(2,1)}, u32[]{:S(2)}, u32[]{:S(2)}) collective-permute-start(bf16[384,512]{1,0:T(8,128)(2,1)} %get-tuple-element.16), channel_id=1, source_target_pairs={{0,2},{1,3},{2,4},{3,5},{4,6},{5,7},{6,8},{7,9},{8,10},{9,11},{10,... | collective-permute-start | bytes 1179656 | tf_op jit(solution)/shard_map/ppermute | solution.py:269
  108.2 14.8 %collective-permute-start.10 = (bf16[384,512]{1,0:T(8,128)(2,1)S(1)}, bf16[384,512]{1,0:T(8,128)(2,1)S(1)}, u32[]{:S(2)}, u32[]{:S(2)}) collective-permute-start(bf16[384,512]{1,0:T(8,128)(2,1)S(1)} %shard_map.70), channel_id=1, source_target_pairs={{15,0},{31,16}} | collective-permute-start | bytes 1179656 | tf_op jit(solution)/shard_map/ppermute | solution.py:269
  117.5 26.2 %collective-permute-start.12 = (bf16[384,512]{1,0:T(8,128)(2,1)S(1)}, bf16[384,512]{1,0:T(8,128)(2,1)S(1)}, u32[]{:S(2)}, u32[]{:S(2)}) collective-permute-start(bf16[384,512]{1,0:T(8,128)(2,1)S(1)} %get-tuple-element.18), channel_id=1, source_target_pairs={{0,3},{1,4},{2,5},{3,6},{4,7},{5,8},{6,9},{7,10},{8,11},{9,12},{10... | collective-permute-start | bytes 1179656 | tf_op jit(solution)/shard_map/ppermute | solution.py:269

commit v6 on v5

--- a/solution.py
+++ b/solution.py
@@ -137,7 +137,7 @@
     return nn((c * sigmoid(c) * e).astype(bf16), down)
 
 
-def unit_kernel(tick, n_pieces, block, flags_ref, *refs):
+def unit_kernel(tick, n_pieces, block, direct, flags_ref, *refs):
     refs = list(refs)
     take = lambda n: [refs.pop(0) for _ in range(n)]
     tokens = take(4 if tick == 0 else 1)
@@ -151,6 +151,12 @@
                 tick, block, flags_ref, tokens, pieces, new_ref, new_ref, ans_out, tok,
                 acc, ans, sems,
             )
+    elif direct:
+        state, new_ref, ans_out, tok, acc, sems = refs
+        unit_steps(
+            tick, block, flags_ref, tokens, pieces, state, new_ref, ans_out, tok, acc,
+            ans_out, sems,
+        )
     else:
         unit_steps(tick, block, flags_ref, tokens, pieces, *refs)
 
@@ -213,12 +219,14 @@
     else:
         for j in range(count):
             one(pl.ds(j * block, block), j == 0, j == count - 1)
-    out = pltpu.make_async_copy(ans, ans_out.at[0, 0] if tick == 0 else ans_out, sems.at[3])
-    out.start()
-    out.wait()
-
-
-def unit(tick, flags, tokens, state, pieces, block=512):
+    if ans is not ans_out:
+        target = ans_out.at[0, 0] if tick == 0 else ans_out
+        out = pltpu.make_async_copy(ans, target, sems.at[3])
+        out.start()
+        out.wait()
+
+
+def unit(tick, flags, tokens, state, pieces, block=512, direct=False):
     span, width = tokens[0].shape[-2:]
     if tick == EXTRA:
         hid = sum(piece.shape[1] for piece in pieces)
@@ -235,9 +243,9 @@
         token_specs[3] = VMEM
         tokens = in_hbm(*tokens[:3]) + tokens[3:]
     return pl.pallas_call(
-        functools.partial(unit_kernel, tick, len(pieces), block),
+        functools.partial(unit_kernel, tick, len(pieces), block, direct),
         in_specs=[SMEM] + token_specs + [HBM] * len(pieces) + [VMEM] * len(states),
-        out_specs=[VMEM] * len(states) + [HBM],
+        out_specs=[VMEM] * len(states) + [VMEM if direct else HBM],
         out_shape=state_shapes
         + [jax.ShapeDtypeStruct(tokens[0].shape if tick == 0 else (span, width), bf16)],
         input_output_aliases=aliases,
@@ -245,7 +253,9 @@
         + [
             pltpu.VMEM((3, span, width), bf16),
             pltpu.VMEM((span, width), f32),
-            pltpu.VMEM((span, width), bf16),
+        ]
+        + ([] if direct else [pltpu.VMEM((span, width), bf16)])
+        + [
             pltpu.SemaphoreType.DMA((4 + len(pieces),)),
         ],
         compiler_params=pltpu.CompilerParams(vmem_limit_bytes=LIMIT),
@@ -309,7 +319,9 @@
     back = [shift(answer1, 1)]
     for t in range(2, ticks):
         restart = pieces if t < ticks - 1 else []
-        state, answer = unit(t, flags, tokens[t - 1 : t], state, restart)
+        state, answer = unit(
+            t, flags, tokens[t - 1 : t], state, restart, direct=t == ticks - 1
+        )
         if t == ticks - 2:
             state = keep(state)
         back.append(shift(answer, t))

time: 145 us -> 145 us (level)
  no operation moved by 1% of the time
where the time goes in v6:
time: 145 us; the launch traced here: 144 us
  starting transfers between devices  55.8 us (38%)
  Pallas kernels  43.3 us (30%)
  waiting for transfers between devices  37.8 us (26%)
  local copies, waits for them, and re-layouts  6.36 us (4%)
    ppermute x13, starting transfers between devices, send(): return lax.ppermute(value, 'seq', pairs)  55.8 us
    ppermute x13, waiting for transfers between devices, send(): return lax.ppermute(value, 'seq', pairs)  37.8 us
    pallas_call x5, Pallas kernels, unit(): pl.pallas_call(functools.partial(unit_kernel, tick, len(pieces), block, d...  35.2 us
    pallas_call x3, Pallas kernels, pack(): pl.pallas_call(functools.partial(pack_kernel, tick), in_specs=[HBM] * 4,...  6.77 us
    dynamic_update_slice x2, local copies, waits for them, and re-layouts, body(): out = lax.dynamic_update_slice(out, back[t - 1][None, None], (0, t, 0, 0))  3.54 us
  transfers between devices with their start and end apart: 13, of which 4 were waited for; matrix products, arithmetic and copies ran while one was open for 3% of the time, Pallas kernels for 29%

profile of v6, /device:TPU:6, one launch (start us, length us, event | category | flops | bytes accessed | tf_op | source)
XLA Modules:
  0.0 144.4 jit_solution(2148101556762289491)
XLA Ops:
  0.0 1.3 collective-permute-start.1
  1.3 7.4 %collective-permute-done.1.refs_1_ = bf16[3,64,512]{2,1,0:T(8,128)(2,1)S(1)} collective-permute-done((bf16[3,64,512]{2,1,0:T(8,128)(2,1)}, bf16[3,64,512]{2,1,0:T(8,128)(2,1)S(1)}, u32[]{:S(2)}, u32[]{:S(2)}) %collective-permute-start.1) | collective-permute-done | bytes 196640 | tf_op jit(solution)/shard_map/ppermute | solution.py:279
  8.7 0.0 copy-start.1
  8.7 0.9 copy-done.1
  9.7 0.7 collective-permute-start.2
  10.4 0.7 collective-permute-start.3
  11.1 6.7 %collective-permute-start.4 = (bf16[3,128,512]{2,1,0:T(8,128)(2,1)S(1)}, bf16[3,128,512]{2,1,0:T(8,128)(2,1)S(1)}, u32[]{:S(2)}, u32[]{:S(2)}) collective-permute-start(bf16[3,128,512]{2,1,0:T(8,128)(2,1)S(1)} %join.2.refs_0_), channel_id=1, source_target_pairs={{2,14},{3,15},{18,30},{19,31}} | collective-permute-start | bytes 1179656 | tf_op jit(solution)/shard_map/ppermute | solution.py:279
  17.8 0.0 collective-permute-done.2.refs_1_
  17.8 0.0 collective-permute-done.3.refs_2_
  17.9 7.5 %collective-permute-done.4.refs_3_ = bf16[3,128,512]{2,1,0:T(8,128)(2,1)S(1)} collective-permute-done((bf16[3,128,512]{2,1,0:T(8,128)(2,1)S(1)}, bf16[3,128,512]{2,1,0:T(8,128)(2,1)S(1)}, u32[]{:S(2)}, u32[]{:S(2)}) %collective-permute-start.4) | collective-permute-done | bytes 393248 | tf_op jit(solution)/shard_map/ppermute | solution.py:279
  25.4 1.3 join.3.refs_1_
  26.6 1.8 %collective-permute-start.5 = (bf16[3,512,512]{2,1,0:T(8,128)(2,1)}, bf16[3,512,512]{2,1,0:T(8,128)(2,1)}, u32[]{:S(2)}, u32[]{:S(2)}) collective-permute-start(bf16[3,512,512]{2,1,0:T(8,128)(2,1)} %join.3.refs_1_), channel_id=1, source_target_pairs={{14,15},{15,14},{30,31},{31,30}} | collective-permute-start | bytes 4718600 | tf_op jit(solution)/shard_map/ppermute | solution.py:279
  28.4 2.2 %shard_map.65 = bf16[3,384,512]{2,1,0:T(8,128)(2,1)} custom-call(bf16[1,4,384,512]{3,2,1,0:T(8,128)(2,1)} %k_ref.5, bf16[1,4,384,512]{3,2,1,0:T(8,128)(2,1)} %v_ref.5, bf16[1,4,384,512]{3,2,1,0:T(8,128)(2,1)} %q_ref.5, bf16[1,4,384]{2,1,0:T(4,128)(2,1)} %r_hbm.5), custom_call_target="tpu_custom_call" | custom-call | tf_op jit(solution)/shard_map/pallas_call | solution.py:72
  30.6 0.1 collective-permute-start
  30.7 2.3 %shard_map.67 = bf16[3,384,512]{2,1,0:T(8,128)(2,1)} custom-call(bf16[1,4,384,512]{3,2,1,0:T(8,128)(2,1)} %k_ref.5, bf16[1,4,384,512]{3,2,1,0:T(8,128)(2,1)} %v_ref.5, bf16[1,4,384,512]{3,2,1,0:T(8,128)(2,1)} %q_ref.5, bf16[1,4,384]{2,1,0:T(4,128)(2,1)} %r_hbm.5), custom_call_target="tpu_custom_call" | custom-call | tf_op jit(solution)/shard_map/pallas_call | solution.py:72
  33.0 0.0 copy-start.2
  33.0 18.4 %collective-permute-start.7 = (bf16[3,384,512]{2,1,0:T(8,128)(2,1)}, bf16[3,384,512]{2,1,0:T(8,128)(2,1)}, u32[]{:S(2)}, u32[]{:S(2)}) collective-permute-start(bf16[3,384,512]{2,1,0:T(8,128)(2,1)} %shard_map.67), channel_id=1, source_target_pairs={{0,14},{1,15},{2,0},{3,1},{4,2},{5,3},{6,4},{7,5},{8,6},{9,7},{10,... | collective-permute-start | bytes 3538952 | tf_op jit(solution)/shard_map/ppermute | solution.py:279
  51.5 2.3 %shard_map.69 = bf16[3,384,512]{2,1,0:T(8,128)(2,1)} custom-call(bf16[1,4,384,512]{3,2,1,0:T(8,128)(2,1)} %k_ref.5, bf16[1,4,384,512]{3,2,1,0:T(8,128)(2,1)} %v_ref.5, bf16[1,4,384,512]{3,2,1,0:T(8,128)(2,1)} %q_ref.5, bf16[1,4,384]{2,1,0:T(4,128)(2,1)} %r_hbm.5), custom_call_target="tpu_custom_call" | custom-call | tf_op jit(solution)/shard_map/pallas_call | solution.py:72
  53.7 1.7 %collective-permute-start.9 = (bf16[3,384,512]{2,1,0:T(8,128)(2,1)}, bf16[3,384,512]{2,1,0:T(8,128)(2,1)}, u32[]{:S(2)}, u32[]{:S(2)}) collective-permute-start(bf16[3,384,512]{2,1,0:T(8,128)(2,1)} %shard_map.69), channel_id=1, source_target_pairs={{0,15},{16,31}} | collective-permute-start | bytes 3538952 | tf_op jit(solution)/shard_map/ppermute | solution.py:279
  55.4 1.9 %collective-permute-start.11 = (bf16[3,384,512]{2,1,0:T(8,128)(2,1)}, bf16[3,384,512]{2,1,0:T(8,128)(2,1)}, u32[]{:S(2)}, u32[]{:S(2)}) collective-permute-start(bf16[3,384,512]{2,1,0:T(8,128)(2,1)} %shard_map.69), channel_id=1, source_target_pairs={{1,14},{2,15},{3,0},{4,1},{5,2},{6,3},{7,4},{8,5},{9,6},{10,7},{11... | collective-permute-start | bytes 3538952 | tf_op jit(solution)/shard_map/ppermute | solution.py:279
  57.4 0.1 add_convert_fusion.flags_ref
  57.4 0.0 copy-done.2
  57.5 0.0 copy-start
  57.5 1.9 %copy-done = bf16[1,3,1024,512]{3,2,1,0:T(8,128)(2,1)S(1)} copy-done((bf16[1,3,1024,512]{3,2,1,0:T(8,128)(2,1)S(1)}, bf16[1,3,1024,512]{3,2,1,0:T(8,128)(2,1)}, u32[]{:S(2)}) %copy-start) | copy-done | bytes 3145752
  59.3 9.0 %shard_map.64 = (bf16[3,1024,512]{2,1,0:T(8,128)(2,1)S(1)}, bf16[1,4,384,512]{3,2,1,0:T(8,128)(2,1)}) custom-call(s32[4]{0:T(128)S(1)} %add_convert_fusion.flags_ref, bf16[1,4,384,512]{3,2,1,0:T(8,128)(2,1)} %k_ref.5, bf16[1,4,384,512]{3,2,1,0:T(8,128)(2,1)} %v_ref.5, bf16[1,4,384,512]{3,2,1,0:T(8,128)(2,1)} %q_ref.5, bf16[1,4,384]{2,1,0:T(4,128)(2,1)S(1)} %copy-done.2, ...), custom_call_target="tpu_custom_call" | custom-call | tf_op jit(solution)/shard_map/pallas_call | solution.py:245
  68.3 0.0 collective-permute-done.refs_0_
  68.3 0.0 collective-permute-done.5.refs_2_
  68.3 8.4 %shard_map.66 = (bf16[3,1024,512]{2,1,0:T(8,128)(2,1)S(1)}, bf16[384,512]{1,0:T(8,128)(2,1)S(1)}) custom-call(s32[4]{0:T(128)S(1)} %add_convert_fusion.flags_ref, bf16[3,384,512]{2,1,0:T(8,128)(2,1)} %collective-permute-done.refs_0_, bf16[3,512,512]{2,1,0:T(8,128)(2,1)} %join.3.refs_1_, ...), custom_call_target="tpu_custom_call", output_to_operand_aliasing={{0}: (4, {})} | custom-call | tf_op jit(solution)/shard_map/pallas_call | solution.py:245
  76.8 1.6 %collective-permute-start.6 = (bf16[384,512]{1,0:T(8,128)(2,1)S(1)}, bf16[384,512]{1,0:T(8,128)(2,1)}, u32[]{:S(2)}, u32[]{:S(2)}) collective-permute-start(bf16[384,512]{1,0:T(8,128)(2,1)S(1)} %get-tuple-element.14), channel_id=1, source_target_pairs={{0,1},{1,2},{2,3},{3,4},{4,5},{5,6},{6,7},{7,8},{8,9},{9,10},{10,1... | collective-permute-start | bytes 1179656 | tf_op jit(solution)/shard_map/ppermute | solution.py:279
  78.4 2.1 %collective-permute-done.7.refs_0_ = bf16[3,384,512]{2,1,0:T(8,128)(2,1)} collective-permute-done((bf16[3,384,512]{2,1,0:T(8,128)(2,1)}, bf16[3,384,512]{2,1,0:T(8,128)(2,1)}, u32[]{:S(2)}, u32[]{:S(2)}) %collective-permute-start.7) | collective-permute-done | bytes 1179680 | tf_op jit(solution)/shard_map/ppermute | solution.py:279
  80.5 9.0 %shard_map.68 = (bf16[3,1024,512]{2,1,0:T(8,128)(2,1)S(1)}, bf16[384,512]{1,0:T(8,128)(2,1)}) custom-call(s32[4]{0:T(128)S(1)} %add_convert_fusion.flags_ref, bf16[3,384,512]{2,1,0:T(8,128)(2,1)} %collective-permute-done.7.refs_0_, bf16[3,512,512]{2,1,0:T(8,128)(2,1)} %join.3.refs_1_, ...), custom_call_target="tpu_custom_call", output_to_operand_aliasing={{0}: (4, {})} | custom-call | tf_op jit(solution)/shard_map/pallas_call | solution.py:245
  89.5 18.1 %collective-permute-start.8 = (bf16[384,512]{1,0:T(8,128)(2,1)}, bf16[384,512]{1,0:T(8,128)(2,1)}, u32[]{:S(2)}, u32[]{:S(2)}) collective-permute-start(bf16[384,512]{1,0:T(8,128)(2,1)} %get-tuple-element.16), channel_id=1, source_target_pairs={{0,2},{1,3},{2,4},{3,5},{4,6},{5,7},{6,8},{7,9},{8,10},{9,11},{10,... | collective-permute-start | bytes 1179656 | tf_op jit(solution)/shard_map/ppermute | solution.py:279
  107.6 0.0 collective-permute-done.9.refs_0_
  107.6 0.6 shard_map.70
  108.2 0.9 collective-permute-start.10
  109.1 0.0 collective-permute-done.11.refs_0_
  109.1 8.2 %shard_map.71 = (bf16[3,1024,512]{2,1,0:T(8,128)(2,1)S(1)}, bf16[384,512]{1,0:T(8,128)(2,1)S(1)}) custom-call(s32[4]{0:T(128)S(1)} %add_convert_fusion.flags_ref, bf16[3,384,512]{2,1,0:T(8,128)(2,1)} %collective-permute-done.11.refs_0_, bf16[3,1024,512]{2,1,0:T(8,128)(2,1)S(1)} %keep.1.refs_1_), custom_call_target="tpu_custom_call", output_to_operand_aliasing={{0}: (2, {})} | custom-call | tf_op jit(solution)/shard_map/pallas_call | solution.py:245
  117.3 1.9 %collective-permute-start.12 = (bf16[384,512]{1,0:T(8,128)(2,1)S(1)}, bf16[384,512]{1,0:T(8,128)(2,1)S(1)}, u32[]{:S(2)}, u32[]{:S(2)}) collective-permute-start(bf16[384,512]{1,0:T(8,128)(2,1)S(1)} %get-tuple-element.18), channel_id=1, source_target_pairs={{0,3},{1,4},{2,5},{3,6},{4,7},{5,8},{6,9},{7,10},{8,11},{9,12},{10... | collective-permute-start | bytes 1179656 | tf_op jit(solution)/shard_map/ppermute | solution.py:279
  119.3 0.0 collective-permute-done.6
  119.3 1.8 %bitcast_dynamic-update-slice_fusion.2 = bf16[1,4,384,512]{3,2,1,0:T(8,128)(2,1)} fusion(bf16[1,4,384,512]{3,2,1,0:T(8,128)(2,1)} %get-tuple-element.12, bf16[384,512]{1,0:T(8,128)(2,1)} %collective-permute-done.6), kind=kLoop, calls=%fused_computation.2 | loop fusion | bytes 786432 | tf_op jit(solution)/shard_map/dynamic_update_slice | solution.py:331
  121.1 0.0 collective-permute-done.8
  121.1 1.8 %bitcast_dynamic-update-slice_fusion.1 = bf16[1,4,384,512]{3,2,1,0:T(8,128)(2,1)} fusion(bf16[1,4,384,512]{3,2,1,0:T(8,128)(2,1)} %bitcast_dynamic-update-slice_fusion.2, bf16[384,512]{1,0:T(8,128)(2,1)} %collective-permute-done.8), kind=kLoop, calls=%fused_computation.1 | loop fusion | bytes 786432 | tf_op jit(solution)/shard_map/dynamic_update_slice | solution.py:331
  122.8 0.0 collective-permute-done.10
  122.8 20.7 %collective-permute-done.12 = bf16[384,512]{1,0:T(8,128)(2,1)S(1)} collective-permute-done((bf16[384,512]{1,0:T(8,128)(2,1)S(1)}, bf16[384,512]{1,0:T(8,128)(2,1)S(1)}, u32[]{:S(2)}, u32[]{:S(2)}) %collective-permute-start.12) | collective-permute-done | bytes 393248 | tf_op jit(solution)/shard_map/ppermute | solution.py:279
  143.5 0.8 bitcast_dynamic-update-slice_fusion
  (2 shorter events, 0.0 us)
Async XLA Ops:
  0.0 8.7 %collective-permute-start.1 = (bf16[3,64,512]{2,1,0:T(8,128)(2,1)}, bf16[3,64,512]{2,1,0:T(8,128)(2,1)S(1)}, u32[]{:S(2)}, u32[]{:S(2)}) collective-permute-start(bf16[3,64,512]{2,1,0:T(8,128)(2,1)} %refs_0_.3), channel_id=1, source_target_pairs={{0,2},{1,3},{4,6},{5,7},{8,10},{9,11},{12,14},{13,15},{16,18},{17,... | collective-permute-start | bytes 589832 | tf_op jit(solution)/shard_map/ppermute | solution.py:279
  8.7 0.9 copy-start.1
  9.7 8.1 %collective-permute-start.2 = (bf16[3,128,512]{2,1,0:T(8,128)(2,1)S(1)}, bf16[3,128,512]{2,1,0:T(8,128)(2,1)S(1)}, u32[]{:S(2)}, u32[]{:S(2)}) collective-permute-start(bf16[3,128,512]{2,1,0:T(8,128)(2,1)S(1)} %join.2.refs_0_), channel_id=1, source_target_pairs={{10,14},{11,15},{26,30},{27,31}} | collective-permute-start | bytes 1179656 | tf_op jit(solution)/shard_map/ppermute | solution.py:279
  10.4 7.5 %collective-permute-start.3 = (bf16[3,128,512]{2,1,0:T(8,128)(2,1)S(1)}, bf16[3,128,512]{2,1,0:T(8,128)(2,1)S(1)}, u32[]{:S(2)}, u32[]{:S(2)}) collective-permute-start(bf16[3,128,512]{2,1,0:T(8,128)(2,1)S(1)} %join.2.refs_0_), channel_id=1, source_target_pairs={{6,14},{7,15},{22,30},{23,31}} | collective-permute-start | bytes 1179656 | tf_op jit(solution)/shard_map/ppermute | solution.py:279
  11.1 14.3 %collective-permute-start.4 = (bf16[3,128,512]{2,1,0:T(8,128)(2,1)S(1)}, bf16[3,128,512]{2,1,0:T(8,128)(2,1)S(1)}, u32[]{:S(2)}, u32[]{:S(2)}) collective-permute-start(bf16[3,128,512]{2,1,0:T(8,128)(2,1)S(1)} %join.2.refs_0_), channel_id=1, source_target_pairs={{2,14},{3,15},{18,30},{19,31}} | collective-permute-start | bytes 1179656 | tf_op jit(solution)/shard_map/ppermute | solution.py:279
  26.6 41.7 %collective-permute-start.5 = (bf16[3,512,512]{2,1,0:T(8,128)(2,1)}, bf16[3,512,512]{2,1,0:T(8,128)(2,1)}, u32[]{:S(2)}, u32[]{:S(2)}) collective-permute-start(bf16[3,512,512]{2,1,0:T(8,128)(2,1)} %join.3.refs_1_), channel_id=1, source_target_pairs={{14,15},{15,14},{30,31},{31,30}} | collective-permute-start | bytes 4718600 | tf_op jit(solution)/shard_map/ppermute | solution.py:279
  30.6 37.7 %collective-permute-start = (bf16[3,384,512]{2,1,0:T(8,128)(2,1)}, bf16[3,384,512]{2,1,0:T(8,128)(2,1)}, u32[]{:S(2)}, u32[]{:S(2)}) collective-permute-start(bf16[3,384,512]{2,1,0:T(8,128)(2,1)} %shard_map.65), channel_id=1, source_target_pairs={{0,15},{1,0},{2,1},{3,2},{4,3},{5,4},{6,5},{7,6},{8,7},{9,8},{10,9... | collective-permute-start | bytes 3538952 | tf_op jit(solution)/shard_map/ppermute | solution.py:279
  33.0 24.4 %copy-start.2 = (bf16[1,4,384]{2,1,0:T(4,128)(2,1)S(1)}, bf16[1,4,384]{2,1,0:T(4,128)(2,1)}, u32[]{:S(2)}) copy-start(bf16[1,4,384]{2,1,0:T(4,128)(2,1)} %r_hbm.5) | copy-start | bytes 9220
  33.0 47.4 %collective-permute-start.7 = (bf16[3,384,512]{2,1,0:T(8,128)(2,1)}, bf16[3,384,512]{2,1,0:T(8,128)(2,1)}, u32[]{:S(2)}, u32[]{:S(2)}) collective-permute-start(bf16[3,384,512]{2,1,0:T(8,128)(2,1)} %shard_map.67), channel_id=1, source_target_pairs={{0,14},{1,15},{2,0},{3,1},{4,2},{5,3},{6,4},{7,5},{8,6},{9,7},{10,... | collective-permute-start | bytes 3538952 | tf_op jit(solution)/shard_map/ppermute | solution.py:279
  53.7 53.9 %collective-permute-start.9 = (bf16[3,384,512]{2,1,0:T(8,128)(2,1)}, bf16[3,384,512]{2,1,0:T(8,128)(2,1)}, u32[]{:S(2)}, u32[]{:S(2)}) collective-permute-start(bf16[3,384,512]{2,1,0:T(8,128)(2,1)} %shard_map.69), channel_id=1, source_target_pairs={{0,15},{16,31}} | collective-permute-start | bytes 3538952 | tf_op jit(solution)/shard_map/ppermute | solution.py:279
  55.4 53.7 %collective-permute-start.11 = (bf16[3,384,512]{2,1,0:T(8,128)(2,1)}, bf16[3,384,512]{2,1,0:T(8,128)(2,1)}, u32[]{:S(2)}, u32[]{:S(2)}) collective-permute-start(bf16[3,384,512]{2,1,0:T(8,128)(2,1)} %shard_map.69), channel_id=1, source_target_pairs={{1,14},{2,15},{3,0},{4,1},{5,2},{6,3},{7,4},{8,5},{9,6},{10,7},{11... | collective-permute-start | bytes 3538952 | tf_op jit(solution)/shard_map/ppermute | solution.py:279
  57.5 1.9 %copy-start = (bf16[1,3,1024,512]{3,2,1,0:T(8,128)(2,1)S(1)}, bf16[1,3,1024,512]{3,2,1,0:T(8,128)(2,1)}, u32[]{:S(2)}) copy-start(bf16[1,3,1024,512]{3,2,1,0:T(8,128)(2,1)} %refs_4_.1) | copy-start | bytes 9437188
  76.8 42.5 %collective-permute-start.6 = (bf16[384,512]{1,0:T(8,128)(2,1)S(1)}, bf16[384,512]{1,0:T(8,128)(2,1)}, u32[]{:S(2)}, u32[]{:S(2)}) collective-permute-start(bf16[384,512]{1,0:T(8,128)(2,1)S(1)} %get-tuple-element.14), channel_id=1, source_target_pairs={{0,1},{1,2},{2,3},{3,4},{4,5},{5,6},{6,7},{7,8},{8,9},{9,10},{10,1... | collective-permute-start | bytes 1179656 | tf_op jit(solution)/shard_map/ppermute | solution.py:279
  89.5 31.6 %collective-permute-start.8 = (bf16[384,512]{1,0:T(8,128)(2,1)}, bf16[384,512]{1,0:T(8,128)(2,1)}, u32[]{:S(2)}, u32[]{:S(2)}) collective-permute-start(bf16[384,512]{1,0:T(8,128)(2,1)} %get-tuple-element.16), channel_id=1, source_target_pairs={{0,2},{1,3},{2,4},{3,5},{4,6},{5,7},{6,8},{7,9},{8,10},{9,11},{10,... | collective-permute-start | bytes 1179656 | tf_op jit(solution)/shard_map/ppermute | solution.py:279
  108.2 14.6 %collective-permute-start.10 = (bf16[384,512]{1,0:T(8,128)(2,1)S(1)}, bf16[384,512]{1,0:T(8,128)(2,1)S(1)}, u32[]{:S(2)}, u32[]{:S(2)}) collective-permute-start(bf16[384,512]{1,0:T(8,128)(2,1)S(1)} %shard_map.70), channel_id=1, source_target_pairs={{15,0},{31,16}} | collective-permute-start | bytes 1179656 | tf_op jit(solution)/shard_map/ppermute | solution.py:279
  117.3 26.2 %collective-permute-start.12 = (bf16[384,512]{1,0:T(8,128)(2,1)S(1)}, bf16[384,512]{1,0:T(8,128)(2,1)S(1)}, u32[]{:S(2)}, u32[]{:S(2)}) collective-permute-start(bf16[384,512]{1,0:T(8,128)(2,1)S(1)} %get-tuple-element.18), channel_id=1, source_target_pairs={{0,3},{1,4},{2,5},{3,6},{4,7},{5,8},{6,9},{7,10},{8,11},{9,12},{10... | collective-permute-start | bytes 1179656 | tf_op jit(solution)/shard_map/ppermute | solution.py:279

commit v7 on v5

--- a/solution.py
+++ b/solution.py
@@ -45,7 +45,9 @@
     )
 
 
-def pack_kernel(tick, k_ref, v_ref, q_ref, r_hbm, o_ref, tok, r_ref, sems):
+def pack_kernel(tick, split, k_ref, v_ref, q_ref, r_hbm, *refs):
+    o_ref = refs[0]
+    tok, r_ref, sems = refs[-3:]
     rates = pltpu.make_async_copy(r_hbm, r_ref, sems.at[6])
     rates.start()
     sources = (k_ref, v_ref, q_ref)
@@ -53,31 +55,43 @@
         pltpu.make_async_copy(sources[i].at[0, tick], tok.at[i], sems.at[i])
         for i in range(3)
     ]
-    stores = [pltpu.make_async_copy(tok.at[i], o_ref.at[i], sems.at[3 + i]) for i in range(3)]
+    stores = [
+        [pltpu.make_async_copy(tok.at[i], o_ref.at[i], sems.at[3 + i])] for i in range(3)
+    ]
+    if split:
+        parts = (refs[1].at[0], refs[1].at[1], refs[2])
+        for i in range(3):
+            stores[i].append(pltpu.make_async_copy(tok.at[i], parts[i], sems.at[7 + i]))
     for i in (1, 0, 2):
         loads[i].start()
     rates.wait()
     loads[1].wait()
     tok[1] = scaled_values(r_ref[0, tick : tick + 1, :], tok[1])
-    stores[1].start()
-    for i in (0, 2):
-        loads[i].wait()
-        stores[i].start()
-    for store in stores:
-        store.wait()
+    for i in (1, 0, 2):
+        if i != 1:
+            loads[i].wait()
+        for store in reversed(stores[i]):
+            store.start()
+    for group in stores:
+        for store in group:
+            store.wait()
 
 
 def pack(tick, keys, values, queries, steps):
-    _, _, span, width = keys.shape
-    return pl.pallas_call(
-        functools.partial(pack_kernel, tick),
+    _, ticks, span, width = keys.shape
+    split = tick == ticks - 1
+    shapes = [(3, span, width)]
+    if split:
+        shapes += [(2, span, width), (span, width)]
+    return pl.pallas_call(
+        functools.partial(pack_kernel, tick, split),
         in_specs=[HBM] * 4,
-        out_specs=HBM,
-        out_shape=jax.ShapeDtypeStruct((3, span, width), bf16),
+        out_specs=[HBM] * len(shapes),
+        out_shape=[jax.ShapeDtypeStruct(shape, bf16) for shape in shapes],
         scratch_shapes=[
             pltpu.VMEM((3, span, width), bf16),
             pltpu.VMEM(steps.shape, bf16),
-            pltpu.SemaphoreType.DMA((7,)),
+            pltpu.SemaphoreType.DMA((10,)),
         ],
         compiler_params=pltpu.CompilerParams(vmem_limit_bytes=LIMIT),
         cost_estimate=pl.CostEstimate(flops=0, bytes_accessed=0, transcendentals=0),
@@ -280,8 +294,11 @@
     held = initial_fast
     args = [token_keys, token_values, queries, step_sizes]
     packs = [pack(t, *args) for t in range(1, ticks)]
-    tokens = [shift(packs[t - 1], -t) for t in range(1, ticks)]
-    tokens_x = send(packs[-1], [(0, count - 1)])
+    tokens = [shift(packs[t - 1][0], -t) for t in range(1, ticks - 1)]
+    whole_last, learn_last, ask_last = packs[-1]
+    learn_last = shift(learn_last, 1 - ticks)
+    ask_last = shift(ask_last, 1 - ticks)
+    tokens_x = send(whole_last, [(0, count - 1)])
     width = quads
     while width > 1:
         held = join([held] + got)
@@ -307,17 +324,84 @@
     state, answer1 = unit(1, flags, tokens[:1], state, pieces)
     (answer_x,) = unit(EXTRA, flags, [tokens_x], None, in_hbm(*pieces))
     back = [shift(answer1, 1)]
-    for t in range(2, ticks):
-        restart = pieces if t < ticks - 1 else []
-        state, answer = unit(t, flags, tokens[t - 1 : t], state, restart)
+    for t in range(2, ticks - 1):
+        state, answer = unit(t, flags, tokens[t - 1 : t], state, pieces)
         if t == ticks - 2:
             state = keep(state)
         back.append(shift(answer, t))
+    state = advance_only(learn_last, state)
+    back.append(shift(serve_only(ask_last, state), ticks - 1))
     back_x = send(answer_x, [(count - 1, 0)])
     back[-1] = jnp.where(position == 0, back_x, back[-1])
     for t in range(1, ticks):
         out = lax.dynamic_update_slice(out, back[t - 1][None, None], (0, t, 0, 0))
     return out
+
+
+def advance_kernel(block, tokens_ref, state_ref, new_ref, tok, sems):
+    del state_ref
+    loads = [
+        pltpu.make_async_copy(tokens_ref.at[i], tok.at[i], sems.at[i]) for i in range(2)
+    ]
+    for load in loads:
+        load.start()
+    for load in loads:
+        load.wait()
+    for j in range(new_ref.shape[1] // block):
+        rows = pl.ds(j * block, block)
+        new = advance_rows(
+            tok[0], tok[1], new_ref[0, rows], new_ref[1, rows], new_ref[2, rows]
+        )
+        for i in range(3):
+            new_ref[i, rows] = new[i]
+
+
+def advance_only(tokens, state, block=512):
+    return pl.pallas_call(
+        functools.partial(advance_kernel, block),
+        in_specs=[HBM, VMEM],
+        out_specs=VMEM,
+        out_shape=jax.ShapeDtypeStruct(state.shape, bf16),
+        input_output_aliases={1: 0},
+        scratch_shapes=[pltpu.VMEM(tokens.shape, bf16), pltpu.SemaphoreType.DMA((2,))],
+        compiler_params=pltpu.CompilerParams(vmem_limit_bytes=LIMIT),
+        cost_estimate=pl.CostEstimate(flops=0, bytes_accessed=0, transcendentals=0),
+        name="advance",
+    )(tokens, state)
+
+
+def serve_kernel(block, queries_ref, state_ref, ans_ref, asked, acc, sem):
+    load = pltpu.make_async_copy(queries_ref, asked, sem)
+    load.start()
+    load.wait()
+    count = state_ref.shape[1] // block
+    for j in range(count):
+        rows = pl.ds(j * block, block)
+        part = serve_rows(
+            asked[...], state_ref[0, rows], state_ref[1, rows], state_ref[2, rows]
+        )
+        total = part if j == 0 else acc[...] + part
+        if j == count - 1:
+            ans_ref[...] = total.astype(bf16)
+        else:
+            acc[...] = total
+
+
+def serve_only(queries, state, block=512):
+    return pl.pallas_call(
+        functools.partial(serve_kernel, block),
+        in_specs=[HBM, VMEM],
+        out_specs=VMEM,
+        out_shape=jax.ShapeDtypeStruct(queries.shape, bf16),
+        scratch_shapes=[
+            pltpu.VMEM(queries.shape, bf16),
+            pltpu.VMEM(queries.shape, f32),
+            pltpu.SemaphoreType.DMA,
+        ],
+        compiler_params=pltpu.CompilerParams(vmem_limit_bytes=LIMIT),
+        cost_estimate=pl.CostEstimate(flops=0, bytes_accessed=0, transcendentals=0),
+        name="serve",
+    )(queries, state)
 
 
 def keep_kernel(state_ref, kept_ref):

time: 145 us -> 144 us (level)
  starting transfers between devices: 55.8 us -> 52.8 us
  waiting for transfers between devices: 37.8 us -> 39.7 us
    pallas_call x3 -> x5, Pallas kernels: 6.77 us -> 14.9 us  [the longest x3 7.15 us: pack(): pl.pallas_call(functools.partial(pack_kernel, tick, split), in_specs=[HBM...]
    pallas_call x5 -> x4, Pallas kernels: 35.4 us -> 27.5 us  [unit(): pl.pallas_call(functools.partial(unit_kernel, tick, len(pieces), block),...]
    ppermute x13 -> x14, starting transfers between devices: 55.8 us -> 52.8 us  [send(): return lax.ppermute(value, 'seq', pairs)]
    ppermute x13 -> x14, waiting for transfers between devices: 37.8 us -> 39.7 us  [send(): return lax.ppermute(value, 'seq', pairs)]
  transfers between devices with their start and end apart: 13 -> 14, of which waited for: 4 -> 3; matrix products, arithmetic and copies ran while one was open for 3% -> 3% of each run, Pallas kernels for 29% -> 29%
where the time goes in v7:
time: 144 us
  starting transfers between devices  52.8 us (37%)
  Pallas kernels  43.7 us (30%)
  waiting for transfers between devices  39.7 us (28%)
  local copies, waits for them, and re-layouts  6.36 us (4%)
    ppermute x14, starting transfers between devices, send(): return lax.ppermute(value, 'seq', pairs)  52.8 us
    ppermute x14, waiting for transfers between devices, send(): return lax.ppermute(value, 'seq', pairs)  39.7 us
    pallas_call x4, Pallas kernels, unit(): pl.pallas_call(functools.partial(unit_kernel, tick, len(pieces), block),...  27.5 us
    pallas_call x3, Pallas kernels, pack(): pl.pallas_call(functools.partial(pack_kernel, tick, split), in_specs=[HBM...  7.15 us
    pallas_call x1, Pallas kernels, advance_only(): pl.pallas_call(functools.partial(advance_kernel, block), in_specs=[HBM, V...  6 us
    dynamic_update_slice x2, local copies, waits for them, and re-layouts, body(): out = lax.dynamic_update_slice(out, back[t - 1][None, None], (0, t, 0, 0))  3.54 us
  transfers between devices with their start and end apart: 14, of which 3 were waited for; matrix products, arithmetic and copies ran while one was open for 3% of the time, Pallas kernels for 29%

profile of v7, /device:TPU:6, one launch (start us, length us, event | category | flops | bytes accessed | tf_op | source)
XLA Modules:
  0.0 143.7 jit_solution(10263649828136764365)
XLA Ops:
  0.0 1.3 collective-permute-start.1
  1.3 7.4 %collective-permute-done.1.refs_1_ = bf16[3,64,512]{2,1,0:T(8,128)(2,1)S(1)} collective-permute-done((bf16[3,64,512]{2,1,0:T(8,128)(2,1)}, bf16[3,64,512]{2,1,0:T(8,128)(2,1)S(1)}, u32[]{:S(2)}, u32[]{:S(2)}) %collective-permute-start.1) | collective-permute-done | bytes 196640 | tf_op jit(solution)/shard_map/ppermute | solution.py:283
  8.7 0.0 copy-start.1
  8.7 0.9 copy-done.1
  9.7 0.7 collective-permute-start.2
  10.4 0.7 collective-permute-start.3
  11.1 6.7 %collective-permute-start.4 = (bf16[3,128,512]{2,1,0:T(8,128)(2,1)S(1)}, bf16[3,128,512]{2,1,0:T(8,128)(2,1)S(1)}, u32[]{:S(2)}, u32[]{:S(2)}) collective-permute-start(bf16[3,128,512]{2,1,0:T(8,128)(2,1)S(1)} %join.2.refs_0_), channel_id=1, source_target_pairs={{2,14},{3,15},{18,30},{19,31}} | collective-permute-start | bytes 1179656 | tf_op jit(solution)/shard_map/ppermute | solution.py:283
  17.8 0.0 collective-permute-done.2.refs_1_
  17.8 0.0 collective-permute-done.3.refs_2_
  17.9 7.5 %collective-permute-done.4.refs_3_ = bf16[3,128,512]{2,1,0:T(8,128)(2,1)S(1)} collective-permute-done((bf16[3,128,512]{2,1,0:T(8,128)(2,1)S(1)}, bf16[3,128,512]{2,1,0:T(8,128)(2,1)S(1)}, u32[]{:S(2)}, u32[]{:S(2)}) %collective-permute-start.4) | collective-permute-done | bytes 393248 | tf_op jit(solution)/shard_map/ppermute | solution.py:283
  25.4 1.3 join.3.refs_1_
  26.6 1.8 %collective-permute-start.5 = (bf16[3,512,512]{2,1,0:T(8,128)(2,1)}, bf16[3,512,512]{2,1,0:T(8,128)(2,1)}, u32[]{:S(2)}, u32[]{:S(2)}) collective-permute-start(bf16[3,512,512]{2,1,0:T(8,128)(2,1)} %join.3.refs_1_), channel_id=1, source_target_pairs={{14,15},{15,14},{30,31},{31,30}} | collective-permute-start | bytes 4718600 | tf_op jit(solution)/shard_map/ppermute | solution.py:283
  28.4 2.2 %shard_map.65 = bf16[3,384,512]{2,1,0:T(8,128)(2,1)} custom-call(bf16[1,4,384,512]{3,2,1,0:T(8,128)(2,1)} %k_ref.5, bf16[1,4,384,512]{3,2,1,0:T(8,128)(2,1)} %v_ref.5, bf16[1,4,384,512]{3,2,1,0:T(8,128)(2,1)} %q_ref.5, bf16[1,4,384]{2,1,0:T(4,128)(2,1)} %r_hbm.5), custom_call_target="tpu_custom_call" | custom-call | tf_op jit(solution)/shard_map/pallas_call | solution.py:86
  30.7 0.1 collective-permute-start
  30.7 2.3 %shard_map.67 = bf16[3,384,512]{2,1,0:T(8,128)(2,1)} custom-call(bf16[1,4,384,512]{3,2,1,0:T(8,128)(2,1)} %k_ref.5, bf16[1,4,384,512]{3,2,1,0:T(8,128)(2,1)} %v_ref.5, bf16[1,4,384,512]{3,2,1,0:T(8,128)(2,1)} %q_ref.5, bf16[1,4,384]{2,1,0:T(4,128)(2,1)} %r_hbm.5), custom_call_target="tpu_custom_call" | custom-call | tf_op jit(solution)/shard_map/pallas_call | solution.py:86
  33.0 0.0 copy-start.2
  33.0 18.4 %collective-permute-start.7 = (bf16[3,384,512]{2,1,0:T(8,128)(2,1)}, bf16[3,384,512]{2,1,0:T(8,128)(2,1)}, u32[]{:S(2)}, u32[]{:S(2)}) collective-permute-start(bf16[3,384,512]{2,1,0:T(8,128)(2,1)} %shard_map.67), channel_id=1, source_target_pairs={{0,14},{1,15},{2,0},{3,1},{4,2},{5,3},{6,4},{7,5},{8,6},{9,7},{10,... | collective-permute-start | bytes 3538952 | tf_op jit(solution)/shard_map/ppermute | solution.py:283
  51.5 2.6 %shard_map.69 = (bf16[3,384,512]{2,1,0:T(8,128)(2,1)}, bf16[2,384,512]{2,1,0:T(8,128)(2,1)}, bf16[384,512]{1,0:T(8,128)(2,1)}) custom-call(bf16[1,4,384,512]{3,2,1,0:T(8,128)(2,1)} %k_ref.5, bf16[1,4,384,512]{3,2,1,0:T(8,128)(2,1)} %v_ref.5, bf16[1,4,384,512]{3,2,1,0:T(8,128)(2,1)} %q_ref.5, bf16[1,4,384]{2,1,0:T(4,128)(2,1)} %r_hbm.5), custom_call_target="tpu_custom_call" | custom-call | tf_op jit(solution)/shard_map/pallas_call | solution.py:86
  54.1 1.7 %collective-permute-start.9 = (bf16[3,384,512]{2,1,0:T(8,128)(2,1)}, bf16[3,384,512]{2,1,0:T(8,128)(2,1)}, u32[]{:S(2)}, u32[]{:S(2)}) collective-permute-start(bf16[3,384,512]{2,1,0:T(8,128)(2,1)} %get-tuple-element.19), channel_id=1, source_target_pairs={{0,15},{16,31}} | collective-permute-start | bytes 3538952 | tf_op jit(solution)/shard_map/ppermute | solution.py:283
  55.8 1.9 %collective-permute-start.12 = (bf16[2,384,512]{2,1,0:T(8,128)(2,1)}, bf16[2,384,512]{2,1,0:T(8,128)(2,1)}, u32[]{:S(2)}, u32[]{:S(2)}) collective-permute-start(bf16[2,384,512]{2,1,0:T(8,128)(2,1)} %get-tuple-element.21), channel_id=1, source_target_pairs={{1,14},{2,15},{3,0},{4,1},{5,2},{6,3},{7,4},{8,5},{9,6},{10,7},{11... | collective-permute-start | bytes 2359304 | tf_op jit(solution)/shard_map/ppermute | solution.py:283
  57.8 0.1 add_convert_fusion.flags_ref
  57.8 0.0 copy-done.2
  57.9 0.0 copy-start
  57.9 1.9 %copy-done = bf16[1,3,1024,512]{3,2,1,0:T(8,128)(2,1)S(1)} copy-done((bf16[1,3,1024,512]{3,2,1,0:T(8,128)(2,1)S(1)}, bf16[1,3,1024,512]{3,2,1,0:T(8,128)(2,1)}, u32[]{:S(2)}) %copy-start) | copy-done | bytes 3145752
  59.7 9.0 %shard_map.64 = (bf16[3,1024,512]{2,1,0:T(8,128)(2,1)S(1)}, bf16[1,4,384,512]{3,2,1,0:T(8,128)(2,1)}) custom-call(s32[4]{0:T(128)S(1)} %add_convert_fusion.flags_ref, bf16[1,4,384,512]{3,2,1,0:T(8,128)(2,1)} %k_ref.5, bf16[1,4,384,512]{3,2,1,0:T(8,128)(2,1)} %v_ref.5, bf16[1,4,384,512]{3,2,1,0:T(8,128)(2,1)} %q_ref.5, bf16[1,4,384]{2,1,0:T(4,128)(2,1)S(1)} %copy-done.2, ...), custom_call_target="tpu_custom_call" | custom-call | tf_op jit(solution)/shard_map/pallas_call | solution.py:251
  68.7 0.0 collective-permute-done.refs_0_
  68.7 10.5 %collective-permute-start.11 = (bf16[384,512]{1,0:T(8,128)(2,1)}, bf16[384,512]{1,0:T(8,128)(2,1)S(1)}, u32[]{:S(2)}, u32[]{:S(2)}) collective-permute-start(bf16[384,512]{1,0:T(8,128)(2,1)} %get-tuple-element.20), channel_id=1, source_target_pairs={{1,14},{2,15},{3,0},{4,1},{5,2},{6,3},{7,4},{8,5},{9,6},{10,7},{11... | collective-permute-start | bytes 1179656 | tf_op jit(solution)/shard_map/ppermute | solution.py:283
  79.2 0.0 collective-permute-done.5.refs_2_
  79.2 9.0 %shard_map.66 = (bf16[3,1024,512]{2,1,0:T(8,128)(2,1)S(1)}, bf16[384,512]{1,0:T(8,128)(2,1)}) custom-call(s32[4]{0:T(128)S(1)} %add_convert_fusion.flags_ref, bf16[3,384,512]{2,1,0:T(8,128)(2,1)} %collective-permute-done.refs_0_, bf16[3,512,512]{2,1,0:T(8,128)(2,1)} %join.3.refs_1_, ...), custom_call_target="tpu_custom_call", output_to_operand_aliasing={{0}: (4, {})} | custom-call | tf_op jit(solution)/shard_map/pallas_call | solution.py:251
  88.2 0.1 collective-permute-start.6
  88.3 0.0 collective-permute-done.7.refs_0_
  88.3 9.0 %shard_map.68 = (bf16[3,1024,512]{2,1,0:T(8,128)(2,1)S(1)}, bf16[384,512]{1,0:T(8,128)(2,1)}) custom-call(s32[4]{0:T(128)S(1)} %add_convert_fusion.flags_ref, bf16[3,384,512]{2,1,0:T(8,128)(2,1)} %collective-permute-done.7.refs_0_, bf16[3,512,512]{2,1,0:T(8,128)(2,1)} %join.3.refs_1_, ...), custom_call_target="tpu_custom_call", output_to_operand_aliasing={{0}: (4, {})} | custom-call | tf_op jit(solution)/shard_map/pallas_call | solution.py:251
  97.3 6.3 %collective-permute-start.8 = (bf16[384,512]{1,0:T(8,128)(2,1)}, bf16[384,512]{1,0:T(8,128)(2,1)}, u32[]{:S(2)}, u32[]{:S(2)}) collective-permute-start(bf16[384,512]{1,0:T(8,128)(2,1)} %get-tuple-element.18), channel_id=1, source_target_pairs={{0,2},{1,3},{2,4},{3,5},{4,6},{5,7},{6,8},{7,9},{8,10},{9,11},{10,... | collective-permute-start | bytes 1179656 | tf_op jit(solution)/shard_map/ppermute | solution.py:283
  103.6 0.0 collective-permute-done.9.refs_0_
  103.6 0.6 shard_map.70
  104.2 0.7 collective-permute-start.10
  104.9 0.0 collective-permute-done.12.tokens_ref
  104.9 6.0 %advance.1.state_ref = bf16[3,1024,512]{2,1,0:T(8,128)(2,1)S(1)} custom-call(bf16[2,384,512]{2,1,0:T(8,128)(2,1)} %collective-permute-done.12.tokens_ref, bf16[3,1024,512]{2,1,0:T(8,128)(2,1)S(1)} %keep.1.state_ref), custom_call_target="tpu_custom_call", output_to_operand_aliasing={{}: (1, {})} | custom-call | tf_op jit(solution)/shard_map/advance/pallas_call | solution.py:360
  110.9 0.0 collective-permute-done.11.queries_ref
  110.9 1.7 %serve.1 = bf16[384,512]{1,0:T(8,128)(2,1)S(1)} custom-call(bf16[384,512]{1,0:T(8,128)(2,1)S(1)} %collective-permute-done.11.queries_ref, bf16[3,1024,512]{2,1,0:T(8,128)(2,1)S(1)} %advance.1.state_ref), custom_call_target="tpu_custom_call" | custom-call | tf_op jit(solution)/shard_map/serve/pallas_call | solution.py:391
  112.7 1.9 %collective-permute-start.13 = (bf16[384,512]{1,0:T(8,128)(2,1)S(1)}, bf16[384,512]{1,0:T(8,128)(2,1)S(1)}, u32[]{:S(2)}, u32[]{:S(2)}) collective-permute-start(bf16[384,512]{1,0:T(8,128)(2,1)S(1)} %serve.1), channel_id=1, source_target_pairs={{0,3},{1,4},{2,5},{3,6},{4,7},{5,8},{6,9},{7,10},{8,11},{9,12},{10... | collective-permute-start | bytes 1179656 | tf_op jit(solution)/shard_map/ppermute | solution.py:283
  114.6 0.0 collective-permute-done.6
  114.6 1.8 %bitcast_dynamic-update-slice_fusion.2 = bf16[1,4,384,512]{3,2,1,0:T(8,128)(2,1)} fusion(bf16[1,4,384,512]{3,2,1,0:T(8,128)(2,1)} %get-tuple-element.14, bf16[384,512]{1,0:T(8,128)(2,1)} %collective-permute-done.6), kind=kLoop, calls=%fused_computation.2 | loop fusion | bytes 786432 | tf_op jit(solution)/shard_map/dynamic_update_slice | solution.py:337
  116.4 0.0 collective-permute-done.8
  116.4 1.8 %bitcast_dynamic-update-slice_fusion.1 = bf16[1,4,384,512]{3,2,1,0:T(8,128)(2,1)} fusion(bf16[1,4,384,512]{3,2,1,0:T(8,128)(2,1)} %bitcast_dynamic-update-slice_fusion.2, bf16[384,512]{1,0:T(8,128)(2,1)} %collective-permute-done.8), kind=kLoop, calls=%fused_computation.1 | loop fusion | bytes 786432 | tf_op jit(solution)/shard_map/dynamic_update_slice | solution.py:337
  118.1 0.0 collective-permute-done.10
  118.1 24.7 %collective-permute-done.13 = bf16[384,512]{1,0:T(8,128)(2,1)S(1)} collective-permute-done((bf16[384,512]{1,0:T(8,128)(2,1)S(1)}, bf16[384,512]{1,0:T(8,128)(2,1)S(1)}, u32[]{:S(2)}, u32[]{:S(2)}) %collective-permute-start.13) | collective-permute-done | bytes 393248 | tf_op jit(solution)/shard_map/ppermute | solution.py:283
  142.9 0.8 bitcast_dynamic-update-slice_fusion
  (2 shorter events, 0.0 us)
Async XLA Ops:
  0.0 8.7 %collective-permute-start.1 = (bf16[3,64,512]{2,1,0:T(8,128)(2,1)}, bf16[3,64,512]{2,1,0:T(8,128)(2,1)S(1)}, u32[]{:S(2)}, u32[]{:S(2)}) collective-permute-start(bf16[3,64,512]{2,1,0:T(8,128)(2,1)} %refs_0_.3), channel_id=1, source_target_pairs={{0,2},{1,3},{4,6},{5,7},{8,10},{9,11},{12,14},{13,15},{16,18},{17,... | collective-permute-start | bytes 589832 | tf_op jit(solution)/shard_map/ppermute | solution.py:283
  8.7 0.9 copy-start.1
  9.7 8.1 %collective-permute-start.2 = (bf16[3,128,512]{2,1,0:T(8,128)(2,1)S(1)}, bf16[3,128,512]{2,1,0:T(8,128)(2,1)S(1)}, u32[]{:S(2)}, u32[]{:S(2)}) collective-permute-start(bf16[3,128,512]{2,1,0:T(8,128)(2,1)S(1)} %join.2.refs_0_), channel_id=1, source_target_pairs={{10,14},{11,15},{26,30},{27,31}} | collective-permute-start | bytes 1179656 | tf_op jit(solution)/shard_map/ppermute | solution.py:283
  10.4 7.5 %collective-permute-start.3 = (bf16[3,128,512]{2,1,0:T(8,128)(2,1)S(1)}, bf16[3,128,512]{2,1,0:T(8,128)(2,1)S(1)}, u32[]{:S(2)}, u32[]{:S(2)}) collective-permute-start(bf16[3,128,512]{2,1,0:T(8,128)(2,1)S(1)} %join.2.refs_0_), channel_id=1, source_target_pairs={{6,14},{7,15},{22,30},{23,31}} | collective-permute-start | bytes 1179656 | tf_op jit(solution)/shard_map/ppermute | solution.py:283
  11.1 14.3 %collective-permute-start.4 = (bf16[3,128,512]{2,1,0:T(8,128)(2,1)S(1)}, bf16[3,128,512]{2,1,0:T(8,128)(2,1)S(1)}, u32[]{:S(2)}, u32[]{:S(2)}) collective-permute-start(bf16[3,128,512]{2,1,0:T(8,128)(2,1)S(1)} %join.2.refs_0_), channel_id=1, source_target_pairs={{2,14},{3,15},{18,30},{19,31}} | collective-permute-start | bytes 1179656 | tf_op jit(solution)/shard_map/ppermute | solution.py:283
  26.6 52.6 %collective-permute-start.5 = (bf16[3,512,512]{2,1,0:T(8,128)(2,1)}, bf16[3,512,512]{2,1,0:T(8,128)(2,1)}, u32[]{:S(2)}, u32[]{:S(2)}) collective-permute-start(bf16[3,512,512]{2,1,0:T(8,128)(2,1)} %join.3.refs_1_), channel_id=1, source_target_pairs={{14,15},{15,14},{30,31},{31,30}} | collective-permute-start | bytes 4718600 | tf_op jit(solution)/shard_map/ppermute | solution.py:283
  30.7 38.1 %collective-permute-start = (bf16[3,384,512]{2,1,0:T(8,128)(2,1)}, bf16[3,384,512]{2,1,0:T(8,128)(2,1)}, u32[]{:S(2)}, u32[]{:S(2)}) collective-permute-start(bf16[3,384,512]{2,1,0:T(8,128)(2,1)} %shard_map.65), channel_id=1, source_target_pairs={{0,15},{1,0},{2,1},{3,2},{4,3},{5,4},{6,5},{7,6},{8,7},{9,8},{10,9... | collective-permute-start | bytes 3538952 | tf_op jit(solution)/shard_map/ppermute | solution.py:283
  33.0 24.8 %copy-start.2 = (bf16[1,4,384]{2,1,0:T(4,128)(2,1)S(1)}, bf16[1,4,384]{2,1,0:T(4,128)(2,1)}, u32[]{:S(2)}) copy-start(bf16[1,4,384]{2,1,0:T(4,128)(2,1)} %r_hbm.5) | copy-start | bytes 9220
  33.0 55.3 %collective-permute-start.7 = (bf16[3,384,512]{2,1,0:T(8,128)(2,1)}, bf16[3,384,512]{2,1,0:T(8,128)(2,1)}, u32[]{:S(2)}, u32[]{:S(2)}) collective-permute-start(bf16[3,384,512]{2,1,0:T(8,128)(2,1)} %shard_map.67), channel_id=1, source_target_pairs={{0,14},{1,15},{2,0},{3,1},{4,2},{5,3},{6,4},{7,5},{8,6},{9,7},{10,... | collective-permute-start | bytes 3538952 | tf_op jit(solution)/shard_map/ppermute | solution.py:283
  54.1 49.5 %collective-permute-start.9 = (bf16[3,384,512]{2,1,0:T(8,128)(2,1)}, bf16[3,384,512]{2,1,0:T(8,128)(2,1)}, u32[]{:S(2)}, u32[]{:S(2)}) collective-permute-start(bf16[3,384,512]{2,1,0:T(8,128)(2,1)} %get-tuple-element.19), channel_id=1, source_target_pairs={{0,15},{16,31}} | collective-permute-start | bytes 3538952 | tf_op jit(solution)/shard_map/ppermute | solution.py:283
  55.8 49.1 %collective-permute-start.12 = (bf16[2,384,512]{2,1,0:T(8,128)(2,1)}, bf16[2,384,512]{2,1,0:T(8,128)(2,1)}, u32[]{:S(2)}, u32[]{:S(2)}) collective-permute-start(bf16[2,384,512]{2,1,0:T(8,128)(2,1)} %get-tuple-element.21), channel_id=1, source_target_pairs={{1,14},{2,15},{3,0},{4,1},{5,2},{6,3},{7,4},{8,5},{9,6},{10,7},{11... | collective-permute-start | bytes 2359304 | tf_op jit(solution)/shard_map/ppermute | solution.py:283
  57.9 1.9 %copy-start = (bf16[1,3,1024,512]{3,2,1,0:T(8,128)(2,1)S(1)}, bf16[1,3,1024,512]{3,2,1,0:T(8,128)(2,1)}, u32[]{:S(2)}) copy-start(bf16[1,3,1024,512]{3,2,1,0:T(8,128)(2,1)} %refs_4_.1) | copy-start | bytes 9437188
  68.7 42.2 %collective-permute-start.11 = (bf16[384,512]{1,0:T(8,128)(2,1)}, bf16[384,512]{1,0:T(8,128)(2,1)S(1)}, u32[]{:S(2)}, u32[]{:S(2)}) collective-permute-start(bf16[384,512]{1,0:T(8,128)(2,1)} %get-tuple-element.20), channel_id=1, source_target_pairs={{1,14},{2,15},{3,0},{4,1},{5,2},{6,3},{7,4},{8,5},{9,6},{10,7},{11... | collective-permute-start | bytes 1179656 | tf_op jit(solution)/shard_map/ppermute | solution.py:283
  88.2 26.4 %collective-permute-start.6 = (bf16[384,512]{1,0:T(8,128)(2,1)}, bf16[384,512]{1,0:T(8,128)(2,1)}, u32[]{:S(2)}, u32[]{:S(2)}) collective-permute-start(bf16[384,512]{1,0:T(8,128)(2,1)} %get-tuple-element.16), channel_id=1, source_target_pairs={{0,1},{1,2},{2,3},{3,4},{4,5},{5,6},{6,7},{7,8},{8,9},{9,10},{10,1... | collective-permute-start | bytes 1179656 | tf_op jit(solution)/shard_map/ppermute | solution.py:283
  97.3 19.1 %collective-permute-start.8 = (bf16[384,512]{1,0:T(8,128)(2,1)}, bf16[384,512]{1,0:T(8,128)(2,1)}, u32[]{:S(2)}, u32[]{:S(2)}) collective-permute-start(bf16[384,512]{1,0:T(8,128)(2,1)} %get-tuple-element.18), channel_id=1, source_target_pairs={{0,2},{1,3},{2,4},{3,5},{4,6},{5,7},{6,8},{7,9},{8,10},{9,11},{10,... | collective-permute-start | bytes 1179656 | tf_op jit(solution)/shard_map/ppermute | solution.py:283
  104.2 14.0 %collective-permute-start.10 = (bf16[384,512]{1,0:T(8,128)(2,1)S(1)}, bf16[384,512]{1,0:T(8,128)(2,1)S(1)}, u32[]{:S(2)}, u32[]{:S(2)}) collective-permute-start(bf16[384,512]{1,0:T(8,128)(2,1)S(1)} %shard_map.70), channel_id=1, source_target_pairs={{15,0},{31,16}} | collective-permute-start | bytes 1179656 | tf_op jit(solution)/shard_map/ppermute | solution.py:283
  112.7 30.2 %collective-permute-start.13 = (bf16[384,512]{1,0:T(8,128)(2,1)S(1)}, bf16[384,512]{1,0:T(8,128)(2,1)S(1)}, u32[]{:S(2)}, u32[]{:S(2)}) collective-permute-start(bf16[384,512]{1,0:T(8,128)(2,1)S(1)} %serve.1), channel_id=1, source_target_pairs={{0,3},{1,4},{2,5},{3,6},{4,7},{5,8},{6,9},{7,10},{8,11},{9,12},{10... | collective-permute-start | bytes 1179656 | tf_op jit(solution)/shard_map/ppermute | solution.py:283

commit v8 on v7

--- a/solution.py
+++ b/solution.py
@@ -215,18 +215,8 @@
         else:
             acc[...] = total
 
-    if tick == EXTRA:
-        loads[2].wait()
-        acc[...] = jnp.zeros_like(acc)
-
-        @pl.loop(0, count)
-        def _(j):
-            one(pl.ds(pl.multiple_of(j * block, block), block), False, False)
-
-        ans[...] = acc[...].astype(bf16)
-    else:
-        for j in range(count):
-            one(pl.ds(j * block, block), j == 0, j == count - 1)
+    for j in range(count):
+        one(pl.ds(j * block, block), j == 0, j == count - 1)
     out = pltpu.make_async_copy(ans, ans_out.at[0, 0] if tick == 0 else ans_out, sems.at[3])
     out.start()
     out.wait()

time: 144 us -> 145 us (level)
  the two profiles are of different devices: /device:TPU:6 before, /device:TPU:4 now
where the time goes in v8:
time: 145 us; the launch traced here: 144 us
  starting transfers between devices  53.1 us (37%)
  Pallas kernels  43.7 us (30%)
  waiting for transfers between devices  39.8 us (27%)
  local copies, waits for them, and re-layouts  6.36 us (4%)
    ppermute x14, starting transfers between devices, send(): return lax.ppermute(value, 'seq', pairs)  53.1 us
    ppermute x14, waiting for transfers between devices, send(): return lax.ppermute(value, 'seq', pairs)  39.8 us
    pallas_call x4, Pallas kernels, unit(): pl.pallas_call(functools.partial(unit_kernel, tick, len(pieces), block),...  27.5 us
    pallas_call x3, Pallas kernels, pack(): pl.pallas_call(functools.partial(pack_kernel, tick, split), in_specs=[HBM...  7.15 us
    pallas_call x1, Pallas kernels, advance_only(): pl.pallas_call(functools.partial(advance_kernel, block), in_specs=[HBM, V...  6 us
    dynamic_update_slice x2, local copies, waits for them, and re-layouts, body(): out = lax.dynamic_update_slice(out, back[t - 1][None, None], (0, t, 0, 0))  3.54 us
  transfers between devices with their start and end apart: 14, of which 3 were waited for; matrix products, arithmetic and copies ran while one was open for 3% of the time, Pallas kernels for 29%

profile of v8, /device:TPU:4, one launch (start us, length us, event | category | flops | bytes accessed | tf_op | source)
XLA Modules:
  0.0 144.1 jit_solution(17198997086530575501)
XLA Ops:
  0.0 1.3 collective-permute-start.1
  1.3 7.4 %collective-permute-done.1.refs_1_ = bf16[3,64,512]{2,1,0:T(8,128)(2,1)S(1)} collective-permute-done((bf16[3,64,512]{2,1,0:T(8,128)(2,1)}, bf16[3,64,512]{2,1,0:T(8,128)(2,1)S(1)}, u32[]{:S(2)}, u32[]{:S(2)}) %collective-permute-start.1) | collective-permute-done | bytes 196640 | tf_op jit(solution)/shard_map/ppermute | solution.py:273
  8.7 0.0 copy-start.1
  8.7 0.9 copy-done.1
  9.7 0.7 collective-permute-start.2
  10.4 0.7 collective-permute-start.3
  11.1 6.7 %collective-permute-start.4 = (bf16[3,128,512]{2,1,0:T(8,128)(2,1)S(1)}, bf16[3,128,512]{2,1,0:T(8,128)(2,1)S(1)}, u32[]{:S(2)}, u32[]{:S(2)}) collective-permute-start(bf16[3,128,512]{2,1,0:T(8,128)(2,1)S(1)} %join.2.refs_0_), channel_id=1, source_target_pairs={{2,14},{3,15},{18,30},{19,31}} | collective-permute-start | bytes 1179656 | tf_op jit(solution)/shard_map/ppermute | solution.py:273
  17.8 0.0 collective-permute-done.2.refs_1_
  17.8 0.0 collective-permute-done.3.refs_2_
  17.9 7.5 %collective-permute-done.4.refs_3_ = bf16[3,128,512]{2,1,0:T(8,128)(2,1)S(1)} collective-permute-done((bf16[3,128,512]{2,1,0:T(8,128)(2,1)S(1)}, bf16[3,128,512]{2,1,0:T(8,128)(2,1)S(1)}, u32[]{:S(2)}, u32[]{:S(2)}) %collective-permute-start.4) | collective-permute-done | bytes 393248 | tf_op jit(solution)/shard_map/ppermute | solution.py:273
  25.4 1.3 join.3.refs_1_
  26.6 1.8 %collective-permute-start.5 = (bf16[3,512,512]{2,1,0:T(8,128)(2,1)}, bf16[3,512,512]{2,1,0:T(8,128)(2,1)}, u32[]{:S(2)}, u32[]{:S(2)}) collective-permute-start(bf16[3,512,512]{2,1,0:T(8,128)(2,1)} %join.3.refs_1_), channel_id=1, source_target_pairs={{14,15},{15,14},{30,31},{31,30}} | collective-permute-start | bytes 4718600 | tf_op jit(solution)/shard_map/ppermute | solution.py:273
  28.4 2.2 %shard_map.65 = bf16[3,384,512]{2,1,0:T(8,128)(2,1)} custom-call(bf16[1,4,384,512]{3,2,1,0:T(8,128)(2,1)} %k_ref.5, bf16[1,4,384,512]{3,2,1,0:T(8,128)(2,1)} %v_ref.5, bf16[1,4,384,512]{3,2,1,0:T(8,128)(2,1)} %q_ref.5, bf16[1,4,384]{2,1,0:T(4,128)(2,1)} %r_hbm.5), custom_call_target="tpu_custom_call" | custom-call | tf_op jit(solution)/shard_map/pallas_call | solution.py:86
  30.7 0.1 collective-permute-start
  30.7 2.3 %shard_map.67 = bf16[3,384,512]{2,1,0:T(8,128)(2,1)} custom-call(bf16[1,4,384,512]{3,2,1,0:T(8,128)(2,1)} %k_ref.5, bf16[1,4,384,512]{3,2,1,0:T(8,128)(2,1)} %v_ref.5, bf16[1,4,384,512]{3,2,1,0:T(8,128)(2,1)} %q_ref.5, bf16[1,4,384]{2,1,0:T(4,128)(2,1)} %r_hbm.5), custom_call_target="tpu_custom_call" | custom-call | tf_op jit(solution)/shard_map/pallas_call | solution.py:86
  33.0 0.0 copy-start.2
  33.0 18.4 %collective-permute-start.7 = (bf16[3,384,512]{2,1,0:T(8,128)(2,1)}, bf16[3,384,512]{2,1,0:T(8,128)(2,1)}, u32[]{:S(2)}, u32[]{:S(2)}) collective-permute-start(bf16[3,384,512]{2,1,0:T(8,128)(2,1)} %shard_map.67), channel_id=1, source_target_pairs={{0,14},{1,15},{2,0},{3,1},{4,2},{5,3},{6,4},{7,5},{8,6},{9,7},{10,... | collective-permute-start | bytes 3538952 | tf_op jit(solution)/shard_map/ppermute | solution.py:273
  51.5 2.6 %shard_map.69 = (bf16[3,384,512]{2,1,0:T(8,128)(2,1)}, bf16[2,384,512]{2,1,0:T(8,128)(2,1)}, bf16[384,512]{1,0:T(8,128)(2,1)}) custom-call(bf16[1,4,384,512]{3,2,1,0:T(8,128)(2,1)} %k_ref.5, bf16[1,4,384,512]{3,2,1,0:T(8,128)(2,1)} %v_ref.5, bf16[1,4,384,512]{3,2,1,0:T(8,128)(2,1)} %q_ref.5, bf16[1,4,384]{2,1,0:T(4,128)(2,1)} %r_hbm.5), custom_call_target="tpu_custom_call" | custom-call | tf_op jit(solution)/shard_map/pallas_call | solution.py:86
  54.1 1.7 %collective-permute-start.9 = (bf16[3,384,512]{2,1,0:T(8,128)(2,1)}, bf16[3,384,512]{2,1,0:T(8,128)(2,1)}, u32[]{:S(2)}, u32[]{:S(2)}) collective-permute-start(bf16[3,384,512]{2,1,0:T(8,128)(2,1)} %get-tuple-element.19), channel_id=1, source_target_pairs={{0,15},{16,31}} | collective-permute-start | bytes 3538952 | tf_op jit(solution)/shard_map/ppermute | solution.py:273
  55.8 1.9 %collective-permute-start.12 = (bf16[2,384,512]{2,1,0:T(8,128)(2,1)}, bf16[2,384,512]{2,1,0:T(8,128)(2,1)}, u32[]{:S(2)}, u32[]{:S(2)}) collective-permute-start(bf16[2,384,512]{2,1,0:T(8,128)(2,1)} %get-tuple-element.21), channel_id=1, source_target_pairs={{1,14},{2,15},{3,0},{4,1},{5,2},{6,3},{7,4},{8,5},{9,6},{10,7},{11... | collective-permute-start | bytes 2359304 | tf_op jit(solution)/shard_map/ppermute | solution.py:273
  57.8 0.1 add_convert_fusion.flags_ref
  57.8 0.0 copy-done.2
  57.9 0.0 copy-start
  57.9 1.9 %copy-done = bf16[1,3,1024,512]{3,2,1,0:T(8,128)(2,1)S(1)} copy-done((bf16[1,3,1024,512]{3,2,1,0:T(8,128)(2,1)S(1)}, bf16[1,3,1024,512]{3,2,1,0:T(8,128)(2,1)}, u32[]{:S(2)}) %copy-start) | copy-done | bytes 3145752
  59.7 9.0 %shard_map.64 = (bf16[3,1024,512]{2,1,0:T(8,128)(2,1)S(1)}, bf16[1,4,384,512]{3,2,1,0:T(8,128)(2,1)}) custom-call(s32[4]{0:T(128)S(1)} %add_convert_fusion.flags_ref, bf16[1,4,384,512]{3,2,1,0:T(8,128)(2,1)} %k_ref.5, bf16[1,4,384,512]{3,2,1,0:T(8,128)(2,1)} %v_ref.5, bf16[1,4,384,512]{3,2,1,0:T(8,128)(2,1)} %q_ref.5, bf16[1,4,384]{2,1,0:T(4,128)(2,1)S(1)} %copy-done.2, ...), custom_call_target="tpu_custom_call" | custom-call | tf_op jit(solution)/shard_map/pallas_call | solution.py:241
  68.7 0.0 collective-permute-done.refs_0_
  68.7 10.5 %collective-permute-start.11 = (bf16[384,512]{1,0:T(8,128)(2,1)}, bf16[384,512]{1,0:T(8,128)(2,1)S(1)}, u32[]{:S(2)}, u32[]{:S(2)}) collective-permute-start(bf16[384,512]{1,0:T(8,128)(2,1)} %get-tuple-element.20), channel_id=1, source_target_pairs={{1,14},{2,15},{3,0},{4,1},{5,2},{6,3},{7,4},{8,5},{9,6},{10,7},{11... | collective-permute-start | bytes 1179656 | tf_op jit(solution)/shard_map/ppermute | solution.py:273
  79.2 0.0 collective-permute-done.5.refs_2_
  79.2 9.0 %shard_map.66 = (bf16[3,1024,512]{2,1,0:T(8,128)(2,1)S(1)}, bf16[384,512]{1,0:T(8,128)(2,1)}) custom-call(s32[4]{0:T(128)S(1)} %add_convert_fusion.flags_ref, bf16[3,384,512]{2,1,0:T(8,128)(2,1)} %collective-permute-done.refs_0_, bf16[3,512,512]{2,1,0:T(8,128)(2,1)} %join.3.refs_1_, ...), custom_call_target="tpu_custom_call", output_to_operand_aliasing={{0}: (4, {})} | custom-call | tf_op jit(solution)/shard_map/pallas_call | solution.py:241
  88.2 0.1 collective-permute-start.6
  88.3 0.0 collective-permute-done.7.refs_0_
  88.3 8.9 %shard_map.68 = (bf16[3,1024,512]{2,1,0:T(8,128)(2,1)S(1)}, bf16[384,512]{1,0:T(8,128)(2,1)}) custom-call(s32[4]{0:T(128)S(1)} %add_convert_fusion.flags_ref, bf16[3,384,512]{2,1,0:T(8,128)(2,1)} %collective-permute-done.7.refs_0_, bf16[3,512,512]{2,1,0:T(8,128)(2,1)} %join.3.refs_1_, ...), custom_call_target="tpu_custom_call", output_to_operand_aliasing={{0}: (4, {})} | custom-call | tf_op jit(solution)/shard_map/pallas_call | solution.py:241
  97.3 6.3 %collective-permute-start.8 = (bf16[384,512]{1,0:T(8,128)(2,1)}, bf16[384,512]{1,0:T(8,128)(2,1)}, u32[]{:S(2)}, u32[]{:S(2)}) collective-permute-start(bf16[384,512]{1,0:T(8,128)(2,1)} %get-tuple-element.18), channel_id=1, source_target_pairs={{0,2},{1,3},{2,4},{3,5},{4,6},{5,7},{6,8},{7,9},{8,10},{9,11},{10,... | collective-permute-start | bytes 1179656 | tf_op jit(solution)/shard_map/ppermute | solution.py:273
  103.6 0.0 collective-permute-done.9.refs_0_
  103.6 0.6 shard_map.70
  104.2 0.9 collective-permute-start.10
  105.2 0.0 collective-permute-done.12.tokens_ref
  105.2 6.0 %advance.1.state_ref = bf16[3,1024,512]{2,1,0:T(8,128)(2,1)S(1)} custom-call(bf16[2,384,512]{2,1,0:T(8,128)(2,1)} %collective-permute-done.12.tokens_ref, bf16[3,1024,512]{2,1,0:T(8,128)(2,1)S(1)} %keep.1.state_ref), custom_call_target="tpu_custom_call", output_to_operand_aliasing={{}: (1, {})} | custom-call | tf_op jit(solution)/shard_map/advance/pallas_call | solution.py:350
  111.2 0.0 collective-permute-done.11.queries_ref
  111.2 1.7 %serve.1 = bf16[384,512]{1,0:T(8,128)(2,1)S(1)} custom-call(bf16[384,512]{1,0:T(8,128)(2,1)S(1)} %collective-permute-done.11.queries_ref, bf16[3,1024,512]{2,1,0:T(8,128)(2,1)S(1)} %advance.1.state_ref), custom_call_target="tpu_custom_call" | custom-call | tf_op jit(solution)/shard_map/serve/pallas_call | solution.py:381
  112.9 1.9 %collective-permute-start.13 = (bf16[384,512]{1,0:T(8,128)(2,1)S(1)}, bf16[384,512]{1,0:T(8,128)(2,1)S(1)}, u32[]{:S(2)}, u32[]{:S(2)}) collective-permute-start(bf16[384,512]{1,0:T(8,128)(2,1)S(1)} %serve.1), channel_id=1, source_target_pairs={{0,3},{1,4},{2,5},{3,6},{4,7},{5,8},{6,9},{7,10},{8,11},{9,12},{10... | collective-permute-start | bytes 1179656 | tf_op jit(solution)/shard_map/ppermute | solution.py:273
  114.9 0.0 collective-permute-done.6
  114.9 1.8 %bitcast_dynamic-update-slice_fusion.2 = bf16[1,4,384,512]{3,2,1,0:T(8,128)(2,1)} fusion(bf16[1,4,384,512]{3,2,1,0:T(8,128)(2,1)} %get-tuple-element.14, bf16[384,512]{1,0:T(8,128)(2,1)} %collective-permute-done.6), kind=kLoop, calls=%fused_computation.2 | loop fusion | bytes 786432 | tf_op jit(solution)/shard_map/dynamic_update_slice | solution.py:327
  116.6 0.0 collective-permute-done.8
  116.6 1.8 %bitcast_dynamic-update-slice_fusion.1 = bf16[1,4,384,512]{3,2,1,0:T(8,128)(2,1)} fusion(bf16[1,4,384,512]{3,2,1,0:T(8,128)(2,1)} %bitcast_dynamic-update-slice_fusion.2, bf16[384,512]{1,0:T(8,128)(2,1)} %collective-permute-done.8), kind=kLoop, calls=%fused_computation.1 | loop fusion | bytes 786432 | tf_op jit(solution)/shard_map/dynamic_update_slice | solution.py:327
  118.4 0.0 collective-permute-done.10
  118.4 24.8 %collective-permute-done.13 = bf16[384,512]{1,0:T(8,128)(2,1)S(1)} collective-permute-done((bf16[384,512]{1,0:T(8,128)(2,1)S(1)}, bf16[384,512]{1,0:T(8,128)(2,1)S(1)}, u32[]{:S(2)}, u32[]{:S(2)}) %collective-permute-start.13) | collective-permute-done | bytes 393248 | tf_op jit(solution)/shard_map/ppermute | solution.py:273
  143.3 0.8 bitcast_dynamic-update-slice_fusion
  (2 shorter events, 0.0 us)
Async XLA Ops:
  0.0 8.7 %collective-permute-start.1 = (bf16[3,64,512]{2,1,0:T(8,128)(2,1)}, bf16[3,64,512]{2,1,0:T(8,128)(2,1)S(1)}, u32[]{:S(2)}, u32[]{:S(2)}) collective-permute-start(bf16[3,64,512]{2,1,0:T(8,128)(2,1)} %refs_0_.3), channel_id=1, source_target_pairs={{0,2},{1,3},{4,6},{5,7},{8,10},{9,11},{12,14},{13,15},{16,18},{17,... | collective-permute-start | bytes 589832 | tf_op jit(solution)/shard_map/ppermute | solution.py:273
  8.7 0.9 copy-start.1
  9.7 8.1 %collective-permute-start.2 = (bf16[3,128,512]{2,1,0:T(8,128)(2,1)S(1)}, bf16[3,128,512]{2,1,0:T(8,128)(2,1)S(1)}, u32[]{:S(2)}, u32[]{:S(2)}) collective-permute-start(bf16[3,128,512]{2,1,0:T(8,128)(2,1)S(1)} %join.2.refs_0_), channel_id=1, source_target_pairs={{10,14},{11,15},{26,30},{27,31}} | collective-permute-start | bytes 1179656 | tf_op jit(solution)/shard_map/ppermute | solution.py:273
  10.4 7.5 %collective-permute-start.3 = (bf16[3,128,512]{2,1,0:T(8,128)(2,1)S(1)}, bf16[3,128,512]{2,1,0:T(8,128)(2,1)S(1)}, u32[]{:S(2)}, u32[]{:S(2)}) collective-permute-start(bf16[3,128,512]{2,1,0:T(8,128)(2,1)S(1)} %join.2.refs_0_), channel_id=1, source_target_pairs={{6,14},{7,15},{22,30},{23,31}} | collective-permute-start | bytes 1179656 | tf_op jit(solution)/shard_map/ppermute | solution.py:273
  11.1 14.3 %collective-permute-start.4 = (bf16[3,128,512]{2,1,0:T(8,128)(2,1)S(1)}, bf16[3,128,512]{2,1,0:T(8,128)(2,1)S(1)}, u32[]{:S(2)}, u32[]{:S(2)}) collective-permute-start(bf16[3,128,512]{2,1,0:T(8,128)(2,1)S(1)} %join.2.refs_0_), channel_id=1, source_target_pairs={{2,14},{3,15},{18,30},{19,31}} | collective-permute-start | bytes 1179656 | tf_op jit(solution)/shard_map/ppermute | solution.py:273
  26.6 52.6 %collective-permute-start.5 = (bf16[3,512,512]{2,1,0:T(8,128)(2,1)}, bf16[3,512,512]{2,1,0:T(8,128)(2,1)}, u32[]{:S(2)}, u32[]{:S(2)}) collective-permute-start(bf16[3,512,512]{2,1,0:T(8,128)(2,1)} %join.3.refs_1_), channel_id=1, source_target_pairs={{14,15},{15,14},{30,31},{31,30}} | collective-permute-start | bytes 4718600 | tf_op jit(solution)/shard_map/ppermute | solution.py:273
  30.7 38.0 %collective-permute-start = (bf16[3,384,512]{2,1,0:T(8,128)(2,1)}, bf16[3,384,512]{2,1,0:T(8,128)(2,1)}, u32[]{:S(2)}, u32[]{:S(2)}) collective-permute-start(bf16[3,384,512]{2,1,0:T(8,128)(2,1)} %shard_map.65), channel_id=1, source_target_pairs={{0,15},{1,0},{2,1},{3,2},{4,3},{5,4},{6,5},{7,6},{8,7},{9,8},{10,9... | collective-permute-start | bytes 3538952 | tf_op jit(solution)/shard_map/ppermute | solution.py:273
  33.0 24.8 %copy-start.2 = (bf16[1,4,384]{2,1,0:T(4,128)(2,1)S(1)}, bf16[1,4,384]{2,1,0:T(4,128)(2,1)}, u32[]{:S(2)}) copy-start(bf16[1,4,384]{2,1,0:T(4,128)(2,1)} %r_hbm.5) | copy-start | bytes 9220
  33.0 55.3 %collective-permute-start.7 = (bf16[3,384,512]{2,1,0:T(8,128)(2,1)}, bf16[3,384,512]{2,1,0:T(8,128)(2,1)}, u32[]{:S(2)}, u32[]{:S(2)}) collective-permute-start(bf16[3,384,512]{2,1,0:T(8,128)(2,1)} %shard_map.67), channel_id=1, source_target_pairs={{0,14},{1,15},{2,0},{3,1},{4,2},{5,3},{6,4},{7,5},{8,6},{9,7},{10,... | collective-permute-start | bytes 3538952 | tf_op jit(solution)/shard_map/ppermute | solution.py:273
  54.1 49.5 %collective-permute-start.9 = (bf16[3,384,512]{2,1,0:T(8,128)(2,1)}, bf16[3,384,512]{2,1,0:T(8,128)(2,1)}, u32[]{:S(2)}, u32[]{:S(2)}) collective-permute-start(bf16[3,384,512]{2,1,0:T(8,128)(2,1)} %get-tuple-element.19), channel_id=1, source_target_pairs={{0,15},{16,31}} | collective-permute-start | bytes 3538952 | tf_op jit(solution)/shard_map/ppermute | solution.py:273
  55.8 49.3 %collective-permute-start.12 = (bf16[2,384,512]{2,1,0:T(8,128)(2,1)}, bf16[2,384,512]{2,1,0:T(8,128)(2,1)}, u32[]{:S(2)}, u32[]{:S(2)}) collective-permute-start(bf16[2,384,512]{2,1,0:T(8,128)(2,1)} %get-tuple-element.21), channel_id=1, source_target_pairs={{1,14},{2,15},{3,0},{4,1},{5,2},{6,3},{7,4},{8,5},{9,6},{10,7},{11... | collective-permute-start | bytes 2359304 | tf_op jit(solution)/shard_map/ppermute | solution.py:273
  57.9 1.9 %copy-start = (bf16[1,3,1024,512]{3,2,1,0:T(8,128)(2,1)S(1)}, bf16[1,3,1024,512]{3,2,1,0:T(8,128)(2,1)}, u32[]{:S(2)}) copy-start(bf16[1,3,1024,512]{3,2,1,0:T(8,128)(2,1)} %refs_4_.1) | copy-start | bytes 9437188
  68.7 42.5 %collective-permute-start.11 = (bf16[384,512]{1,0:T(8,128)(2,1)}, bf16[384,512]{1,0:T(8,128)(2,1)S(1)}, u32[]{:S(2)}, u32[]{:S(2)}) collective-permute-start(bf16[384,512]{1,0:T(8,128)(2,1)} %get-tuple-element.20), channel_id=1, source_target_pairs={{1,14},{2,15},{3,0},{4,1},{5,2},{6,3},{7,4},{8,5},{9,6},{10,7},{11... | collective-permute-start | bytes 1179656 | tf_op jit(solution)/shard_map/ppermute | solution.py:273
  88.2 26.6 %collective-permute-start.6 = (bf16[384,512]{1,0:T(8,128)(2,1)}, bf16[384,512]{1,0:T(8,128)(2,1)}, u32[]{:S(2)}, u32[]{:S(2)}) collective-permute-start(bf16[384,512]{1,0:T(8,128)(2,1)} %get-tuple-element.16), channel_id=1, source_target_pairs={{0,1},{1,2},{2,3},{3,4},{4,5},{5,6},{6,7},{7,8},{8,9},{9,10},{10,1... | collective-permute-start | bytes 1179656 | tf_op jit(solution)/shard_map/ppermute | solution.py:273
  97.3 19.4 %collective-permute-start.8 = (bf16[384,512]{1,0:T(8,128)(2,1)}, bf16[384,512]{1,0:T(8,128)(2,1)}, u32[]{:S(2)}, u32[]{:S(2)}) collective-permute-start(bf16[384,512]{1,0:T(8,128)(2,1)} %get-tuple-element.18), channel_id=1, source_target_pairs={{0,2},{1,3},{2,4},{3,5},{4,6},{5,7},{6,8},{7,9},{8,10},{9,11},{10,... | collective-permute-start | bytes 1179656 | tf_op jit(solution)/shard_map/ppermute | solution.py:273
  104.2 14.2 %collective-permute-start.10 = (bf16[384,512]{1,0:T(8,128)(2,1)S(1)}, bf16[384,512]{1,0:T(8,128)(2,1)S(1)}, u32[]{:S(2)}, u32[]{:S(2)}) collective-permute-start(bf16[384,512]{1,0:T(8,128)(2,1)S(1)} %shard_map.70), channel_id=1, source_target_pairs={{15,0},{31,16}} | collective-permute-start | bytes 1179656 | tf_op jit(solution)/shard_map/ppermute | solution.py:273
  112.9 30.3 %collective-permute-start.13 = (bf16[384,512]{1,0:T(8,128)(2,1)S(1)}, bf16[384,512]{1,0:T(8,128)(2,1)S(1)}, u32[]{:S(2)}, u32[]{:S(2)}) collective-permute-start(bf16[384,512]{1,0:T(8,128)(2,1)S(1)} %serve.1), channel_id=1, source_target_pairs={{0,3},{1,4},{2,5},{3,6},{4,7},{5,8},{6,9},{7,10},{8,11},{9,12},{10... | collective-permute-start | bytes 1179656 | tf_op jit(solution)/shard_map/ppermute | solution.py:273

commit v9 on v7

--- a/solution.py
+++ b/solution.py
@@ -274,9 +274,9 @@
     flags = jnp.stack(
         [(position == count - 1).astype(jnp.int32)]
         + [
-            ((position + t == count) & (t < ticks - 1)).astype(jnp.int32)
-            for t in range(1, ticks)
+            (position + t == count).astype(jnp.int32) for t in range(1, ticks - 1)
         ]
+        + [(position + ticks > count + 1).astype(jnp.int32)]
     )
 
     def send(value, pairs):
@@ -296,8 +296,11 @@
     packs = [pack(t, *args) for t in range(1, ticks)]
     tokens = [shift(packs[t - 1][0], -t) for t in range(1, ticks - 1)]
     whole_last, learn_last, ask_last = packs[-1]
-    learn_last = shift(learn_last, 1 - ticks)
-    ask_last = shift(ask_last, 1 - ticks)
+    far = ticks - 1
+    straight = [(s, s - far) for s in range(far, count)]
+    learn_last = send(learn_last, straight)
+    ask_last = send(ask_last, straight)
+    wrapped = send(whole_last, [(s, s - far + count) for s in range(1, far)])
     tokens_x = send(whole_last, [(0, count - 1)])
     width = quads
     while width > 1:
@@ -329,8 +332,9 @@
         if t == ticks - 2:
             state = keep(state)
         back.append(shift(answer, t))
-    state = advance_only(learn_last, state)
-    back.append(shift(serve_only(ask_last, state), ticks - 1))
+    state = advance_only(far, flags, learn_last, wrapped, state)
+    answer = serve_only(far, flags, ask_last, wrapped, state)
+    back.append(shift(answer, far))
     back_x = send(answer_x, [(count - 1, 0)])
     back[-1] = jnp.where(position == 0, back_x, back[-1])
     for t in range(1, ticks):
@@ -338,13 +342,25 @@
     return out
 
 
-def advance_kernel(block, tokens_ref, state_ref, new_ref, tok, sems):
+def pick(wrapped, usual, other):
+    @pl.when(wrapped != 0)
+    def _():
+        for load in other:
+            load.start()
+
+    @pl.when(wrapped == 0)
+    def _():
+        for load in usual:
+            load.start()
+
+
+def advance_kernel(slot, block, flags_ref, tokens_ref, wrap_ref, state_ref, new_ref, tok, sems):
     del state_ref
-    loads = [
-        pltpu.make_async_copy(tokens_ref.at[i], tok.at[i], sems.at[i]) for i in range(2)
+    loads, other = [
+        [pltpu.make_async_copy(ref.at[i], tok.at[i], sems.at[i]) for i in range(2)]
+        for ref in (tokens_ref, wrap_ref)
     ]
-    for load in loads:
-        load.start()
+    pick(flags_ref[slot], loads, other)
     for load in loads:
         load.wait()
     for j in range(new_ref.shape[1] // block):
@@ -356,23 +372,26 @@
             new_ref[i, rows] = new[i]
 
 
-def advance_only(tokens, state, block=512):
-    return pl.pallas_call(
-        functools.partial(advance_kernel, block),
-        in_specs=[HBM, VMEM],
+def advance_only(slot, flags, tokens, wrapped, state, block=512):
+    return pl.pallas_call(
+        functools.partial(advance_kernel, slot, block),
+        in_specs=[SMEM, HBM, HBM, VMEM],
         out_specs=VMEM,
         out_shape=jax.ShapeDtypeStruct(state.shape, bf16),
-        input_output_aliases={1: 0},
+        input_output_aliases={3: 0},
         scratch_shapes=[pltpu.VMEM(tokens.shape, bf16), pltpu.SemaphoreType.DMA((2,))],
         compiler_params=pltpu.CompilerParams(vmem_limit_bytes=LIMIT),
         cost_estimate=pl.CostEstimate(flops=0, bytes_accessed=0, transcendentals=0),
         name="advance",
-    )(tokens, state)
-
-
-def serve_kernel(block, queries_ref, state_ref, ans_ref, asked, acc, sem):
+    )(flags, tokens, wrapped, state)
+
+
+def serve_kernel(
+    slot, block, flags_ref, queries_ref, wrap_ref, state_ref, ans_ref, asked, acc, sem
+):
     load = pltpu.make_async_copy(queries_ref, asked, sem)
-    load.start()
+    other = pltpu.make_async_copy(wrap_ref.at[2], asked, sem)
+    pick(flags_ref[slot], [load], [other])
     load.wait()
     count = state_ref.shape[1] // block
     for j in range(count):
@@ -387,10 +406,10 @@
             acc[...] = total
 
 
-def serve_only(queries, state, block=512):
-    return pl.pallas_call(
-        functools.partial(serve_kernel, block),
-        in_specs=[HBM, VMEM],
+def serve_only(slot, flags, queries, wrapped, state, block=512):
+    return pl.pallas_call(
+        functools.partial(serve_kernel, slot, block),
+        in_specs=[SMEM, HBM, HBM, VMEM],
         out_specs=VMEM,
         out_shape=jax.ShapeDtypeStruct(queries.shape, bf16),
         scratch_shapes=[
@@ -401,7 +420,7 @@
         compiler_params=pltpu.CompilerParams(vmem_limit_bytes=LIMIT),
         cost_estimate=pl.CostEstimate(flops=0, bytes_accessed=0, transcendentals=0),
         name="serve",
-    )(queries, state)
+    )(flags, queries, wrapped, state)
 
 
 def keep_kernel(state_ref, kept_ref):

time: 144 us -> 133 us (0.924)
  the two profiles are of different devices: /device:TPU:6 before, /device:TPU:4 now
where the time goes in v9:
time: 133 us
  starting transfers between devices  45.2 us (34%)
  Pallas kernels  43.8 us (33%)
  waiting for transfers between devices  35.1 us (26%)
  local copies, waits for them, and re-layouts  7.37 us (6%)
    ppermute x15, starting transfers between devices, send(): return lax.ppermute(value, 'seq', pairs)  45.2 us
    ppermute x15, waiting for transfers between devices, send(): return lax.ppermute(value, 'seq', pairs)  35.1 us
    pallas_call x4, Pallas kernels, unit(): pl.pallas_call(functools.partial(unit_kernel, tick, len(pieces), block),...  26.9 us
    pallas_call x3, Pallas kernels, pack(): pl.pallas_call(functools.partial(pack_kernel, tick, split), in_specs=[HBM...  6.78 us
    pallas_call x1, Pallas kernels, advance_only(): pl.pallas_call(functools.partial(advance_kernel, slot, block), in_specs=[...  6.54 us
    unnamed x10, local copies, waits for them, and re-layouts  3.83 us
    dynamic_update_slice x2, local copies, waits for them, and re-layouts, body(): out = lax.dynamic_update_slice(out, back[t - 1][None, None], (0, t, 0, 0))  3.54 us
  transfers between devices with their start and end apart: 15, of which 3 were waited for; matrix products, arithmetic and copies ran while one was open for 3% of the time, Pallas kernels for 33%

profile of v9, /device:TPU:4, one launch (start us, length us, event | category | flops | bytes accessed | tf_op | source)
XLA Modules:
  0.0 132.8 jit_solution(4601161032249641845)
XLA Ops:
  0.0 1.3 collective-permute-start.1
  1.3 7.4 %collective-permute-done.1.refs_1_ = bf16[3,64,512]{2,1,0:T(8,128)(2,1)S(1)} collective-permute-done((bf16[3,64,512]{2,1,0:T(8,128)(2,1)}, bf16[3,64,512]{2,1,0:T(8,128)(2,1)S(1)}, u32[]{:S(2)}, u32[]{:S(2)}) %collective-permute-start.1) | collective-permute-done | bytes 196640 | tf_op jit(solution)/shard_map/ppermute | solution.py:283
  8.7 0.0 copy-start.3
  8.7 0.9 copy-done.3
  9.7 0.7 collective-permute-start.2
  10.4 0.7 collective-permute-start.3
  11.1 6.7 %collective-permute-start.4 = (bf16[3,128,512]{2,1,0:T(8,128)(2,1)S(1)}, bf16[3,128,512]{2,1,0:T(8,128)(2,1)S(1)}, u32[]{:S(2)}, u32[]{:S(2)}) collective-permute-start(bf16[3,128,512]{2,1,0:T(8,128)(2,1)S(1)} %join.2.refs_0_), channel_id=1, source_target_pairs={{2,14},{3,15},{18,30},{19,31}} | collective-permute-start | bytes 1179656 | tf_op jit(solution)/shard_map/ppermute | solution.py:283
  17.8 1.8 %shard_map.65 = bf16[3,384,512]{2,1,0:T(8,128)(2,1)S(1)} custom-call(bf16[1,4,384,512]{3,2,1,0:T(8,128)(2,1)} %k_ref.5, bf16[1,4,384,512]{3,2,1,0:T(8,128)(2,1)} %v_ref.5, bf16[1,4,384,512]{3,2,1,0:T(8,128)(2,1)} %q_ref.5, bf16[1,4,384]{2,1,0:T(4,128)(2,1)} %r_hbm.5), custom_call_target="tpu_custom_call" | custom-call | tf_op jit(solution)/shard_map/pallas_call | solution.py:86
  19.6 0.1 collective-permute-start
  19.7 0.0 collective-permute-done.2.refs_1_
  19.7 0.0 collective-permute-done.3.refs_2_
  19.7 5.6 %collective-permute-done.4.refs_3_ = bf16[3,128,512]{2,1,0:T(8,128)(2,1)S(1)} collective-permute-done((bf16[3,128,512]{2,1,0:T(8,128)(2,1)S(1)}, bf16[3,128,512]{2,1,0:T(8,128)(2,1)S(1)}, u32[]{:S(2)}, u32[]{:S(2)}) %collective-permute-start.4) | collective-permute-done | bytes 393248 | tf_op jit(solution)/shard_map/ppermute | solution.py:283
  25.4 1.3 join.3.refs_1_
  26.6 1.8 %collective-permute-start.5 = (bf16[3,512,512]{2,1,0:T(8,128)(2,1)}, bf16[3,512,512]{2,1,0:T(8,128)(2,1)}, u32[]{:S(2)}, u32[]{:S(2)}) collective-permute-start(bf16[3,512,512]{2,1,0:T(8,128)(2,1)} %join.3.refs_1_), channel_id=1, source_target_pairs={{14,15},{15,14},{30,31},{31,30}} | collective-permute-start | bytes 4718600 | tf_op jit(solution)/shard_map/ppermute | solution.py:283
  28.4 2.3 %shard_map.67 = bf16[3,384,512]{2,1,0:T(8,128)(2,1)} custom-call(bf16[1,4,384,512]{3,2,1,0:T(8,128)(2,1)} %k_ref.5, bf16[1,4,384,512]{3,2,1,0:T(8,128)(2,1)} %v_ref.5, bf16[1,4,384,512]{3,2,1,0:T(8,128)(2,1)} %q_ref.5, bf16[1,4,384]{2,1,0:T(4,128)(2,1)} %r_hbm.5), custom_call_target="tpu_custom_call" | custom-call | tf_op jit(solution)/shard_map/pallas_call | solution.py:86
  30.7 0.0 copy-start.4
  30.8 0.1 collective-permute-start.7
  30.8 2.6 %shard_map.69 = (bf16[3,384,512]{2,1,0:T(8,128)(2,1)}, bf16[2,384,512]{2,1,0:T(8,128)(2,1)}, bf16[384,512]{1,0:T(8,128)(2,1)}) custom-call(bf16[1,4,384,512]{3,2,1,0:T(8,128)(2,1)} %k_ref.5, bf16[1,4,384,512]{3,2,1,0:T(8,128)(2,1)} %v_ref.5, bf16[1,4,384,512]{3,2,1,0:T(8,128)(2,1)} %q_ref.5, bf16[1,4,384]{2,1,0:T(4,128)(2,1)} %r_hbm.5), custom_call_target="tpu_custom_call" | custom-call | tf_op jit(solution)/shard_map/pallas_call | solution.py:86
  33.5 1.7 %collective-permute-start.9 = (bf16[3,384,512]{2,1,0:T(8,128)(2,1)}, bf16[3,384,512]{2,1,0:T(8,128)(2,1)}, u32[]{:S(2)}, u32[]{:S(2)}) collective-permute-start(bf16[3,384,512]{2,1,0:T(8,128)(2,1)} %get-tuple-element.19), channel_id=1, source_target_pairs={{0,15},{16,31}} | collective-permute-start | bytes 3538952 | tf_op jit(solution)/shard_map/ppermute | solution.py:283
  35.2 19.5 %collective-permute-start.12 = (bf16[3,384,512]{2,1,0:T(8,128)(2,1)}, bf16[3,384,512]{2,1,0:T(8,128)(2,1)}, u32[]{:S(2)}, u32[]{:S(2)}) collective-permute-start(bf16[3,384,512]{2,1,0:T(8,128)(2,1)} %get-tuple-element.19), channel_id=1, source_target_pairs={{1,14},{2,15},{17,30},{18,31}} | collective-permute-start | bytes 3538952 | tf_op jit(solution)/shard_map/ppermute | solution.py:283
  54.7 0.0 collective-permute-done.refs_0_
  54.7 0.0 copy-start.1
  54.7 1.0 copy-done.1
  55.7 1.3 collective-permute-start.13
  57.0 0.1 add_convert_fusion.flags_ref
  57.1 0.0 copy-done.4
  57.1 0.0 copy-start
  57.1 1.9 %copy-done = bf16[1,3,1024,512]{3,2,1,0:T(8,128)(2,1)S(1)} copy-done((bf16[1,3,1024,512]{3,2,1,0:T(8,128)(2,1)S(1)}, bf16[1,3,1024,512]{3,2,1,0:T(8,128)(2,1)}, u32[]{:S(2)}) %copy-start) | copy-done | bytes 3145752
  59.0 0.0 copy-start.2
  59.0 9.0 %shard_map.64 = (bf16[3,1024,512]{2,1,0:T(8,128)(2,1)S(1)}, bf16[1,4,384,512]{3,2,1,0:T(8,128)(2,1)}) custom-call(s32[4]{0:T(128)S(1)} %add_convert_fusion.flags_ref, bf16[1,4,384,512]{3,2,1,0:T(8,128)(2,1)} %k_ref.5, bf16[1,4,384,512]{3,2,1,0:T(8,128)(2,1)} %v_ref.5, bf16[1,4,384,512]{3,2,1,0:T(8,128)(2,1)} %q_ref.5, bf16[1,4,384]{2,1,0:T(4,128)(2,1)S(1)} %copy-done.4, ...), custom_call_target="tpu_custom_call" | custom-call | tf_op jit(solution)/shard_map/pallas_call | solution.py:251
  67.9 0.0 collective-permute-done.5.refs_2_
  67.9 1.5 %collective-permute-start.11 = (bf16[384,512]{1,0:T(8,128)(2,1)}, bf16[384,512]{1,0:T(8,128)(2,1)S(1)}, u32[]{:S(2)}, u32[]{:S(2)}) collective-permute-start(bf16[384,512]{1,0:T(8,128)(2,1)} %get-tuple-element.20), channel_id=1, source_target_pairs={{3,0},{4,1},{5,2},{6,3},{7,4},{8,5},{9,6},{10,7},{11,8},{12,9},{13... | collective-permute-start | bytes 1179656 | tf_op jit(solution)/shard_map/ppermute | solution.py:283
  69.4 0.0 copy-done.2
  69.4 8.4 %shard_map.66 = (bf16[3,1024,512]{2,1,0:T(8,128)(2,1)S(1)}, bf16[384,512]{1,0:T(8,128)(2,1)}) custom-call(s32[4]{0:T(128)S(1)} %add_convert_fusion.flags_ref, bf16[3,384,512]{2,1,0:T(8,128)(2,1)S(1)} %copy-done.2, bf16[3,512,512]{2,1,0:T(8,128)(2,1)} %join.3.refs_1_, ...), custom_call_target="tpu_custom_call", output_to_operand_aliasing={{0}: (4, {})} | custom-call | tf_op jit(solution)/shard_map/pallas_call | solution.py:251
  77.9 0.0 collective-permute-done.7.refs_0_
  77.9 3.5 %collective-permute-start.6 = (bf16[384,512]{1,0:T(8,128)(2,1)}, bf16[384,512]{1,0:T(8,128)(2,1)}, u32[]{:S(2)}, u32[]{:S(2)}) collective-permute-start(bf16[384,512]{1,0:T(8,128)(2,1)} %get-tuple-element.16), channel_id=1, source_target_pairs={{0,1},{1,2},{2,3},{3,4},{4,5},{5,6},{6,7},{7,8},{8,9},{9,10},{10,1... | collective-permute-start | bytes 1179656 | tf_op jit(solution)/shard_map/ppermute | solution.py:283
  81.3 8.9 %shard_map.68 = (bf16[3,1024,512]{2,1,0:T(8,128)(2,1)S(1)}, bf16[384,512]{1,0:T(8,128)(2,1)}) custom-call(s32[4]{0:T(128)S(1)} %add_convert_fusion.flags_ref, bf16[3,384,512]{2,1,0:T(8,128)(2,1)} %collective-permute-done.7.refs_0_, bf16[3,512,512]{2,1,0:T(8,128)(2,1)} %join.3.refs_1_, ...), custom_call_target="tpu_custom_call", output_to_operand_aliasing={{0}: (4, {})} | custom-call | tf_op jit(solution)/shard_map/pallas_call | solution.py:251
  90.3 0.0 collective-permute-done.9.refs_0_
  90.3 1.1 collective-permute-start.8
  91.5 0.6 shard_map.70
  92.1 0.0 collective-permute-done.13.tokens_ref
  92.1 0.9 collective-permute-start.10
  93.0 0.0 collective-permute-done.12.wrap_ref
  93.0 6.5 %advance.1.state_ref = bf16[3,1024,512]{2,1,0:T(8,128)(2,1)S(1)} custom-call(s32[4]{0:T(128)S(1)} %add_convert_fusion.flags_ref, bf16[2,384,512]{2,1,0:T(8,128)(2,1)} %collective-permute-done.13.tokens_ref, bf16[3,384,512]{2,1,0:T(8,128)(2,1)} %collective-permute-done.12.wrap_ref, ...), custom_call_target="tpu_custom_call", output_to_operand_aliasing={{}: (3, {})} | custom-call | tf_op jit(solution)/shard_map/advance/pallas_call | solution.py:376
  99.6 0.0 collective-permute-done.11.queries_ref
  99.6 2.3 %serve.1 = bf16[384,512]{1,0:T(8,128)(2,1)S(1)} custom-call(s32[4]{0:T(128)S(1)} %add_convert_fusion.flags_ref, bf16[384,512]{1,0:T(8,128)(2,1)S(1)} %collective-permute-done.11.queries_ref, bf16[3,384,512]{2,1,0:T(8,128)(2,1)} %collective-permute-done.12.wrap_ref, bf16[3,1024,512]{2,1,0:T(8,128)(2,1)S(1)} %advance.1.state_ref), custom_call_target="tpu_custom_call" | custom-call | tf_op jit(solution)/shard_map/serve/pallas_call | solution.py:410
  101.9 4.4 %collective-permute-start.14 = (bf16[384,512]{1,0:T(8,128)(2,1)S(1)}, bf16[384,512]{1,0:T(8,128)(2,1)S(1)}, u32[]{:S(2)}, u32[]{:S(2)}) collective-permute-start(bf16[384,512]{1,0:T(8,128)(2,1)S(1)} %serve.1), channel_id=1, source_target_pairs={{0,3},{1,4},{2,5},{3,6},{4,7},{5,8},{6,9},{7,10},{8,11},{9,12},{10... | collective-permute-start | bytes 1179656 | tf_op jit(solution)/shard_map/ppermute | solution.py:283
  106.3 0.0 collective-permute-done.6
  106.3 1.8 %bitcast_dynamic-update-slice_fusion.2 = bf16[1,4,384,512]{3,2,1,0:T(8,128)(2,1)} fusion(bf16[1,4,384,512]{3,2,1,0:T(8,128)(2,1)} %get-tuple-element.14, bf16[384,512]{1,0:T(8,128)(2,1)} %collective-permute-done.6), kind=kLoop, calls=%fused_computation.2 | loop fusion | bytes 786432 | tf_op jit(solution)/shard_map/dynamic_update_slice | solution.py:341
  108.1 0.0 collective-permute-done.8
  108.1 1.8 %bitcast_dynamic-update-slice_fusion.1 = bf16[1,4,384,512]{3,2,1,0:T(8,128)(2,1)} fusion(bf16[1,4,384,512]{3,2,1,0:T(8,128)(2,1)} %bitcast_dynamic-update-slice_fusion.2, bf16[384,512]{1,0:T(8,128)(2,1)} %collective-permute-done.8), kind=kLoop, calls=%fused_computation.1 | loop fusion | bytes 786432 | tf_op jit(solution)/shard_map/dynamic_update_slice | solution.py:341
  109.9 0.0 collective-permute-done.10
  109.9 22.0 %collective-permute-done.14 = bf16[384,512]{1,0:T(8,128)(2,1)S(1)} collective-permute-done((bf16[384,512]{1,0:T(8,128)(2,1)S(1)}, bf16[384,512]{1,0:T(8,128)(2,1)S(1)}, u32[]{:S(2)}, u32[]{:S(2)}) %collective-permute-start.14) | collective-permute-done | bytes 393248 | tf_op jit(solution)/shard_map/ppermute | solution.py:283
  131.9 0.8 bitcast_dynamic-update-slice_fusion
  (2 shorter events, 0.0 us)
Async XLA Ops:
  0.0 8.7 %collective-permute-start.1 = (bf16[3,64,512]{2,1,0:T(8,128)(2,1)}, bf16[3,64,512]{2,1,0:T(8,128)(2,1)S(1)}, u32[]{:S(2)}, u32[]{:S(2)}) collective-permute-start(bf16[3,64,512]{2,1,0:T(8,128)(2,1)} %refs_0_.3), channel_id=1, source_target_pairs={{0,2},{1,3},{4,6},{5,7},{8,10},{9,11},{12,14},{13,15},{16,18},{17,... | collective-permute-start | bytes 589832 | tf_op jit(solution)/shard_map/ppermute | solution.py:283
  8.7 0.9 copy-start.3
  9.7 10.0 %collective-permute-start.2 = (bf16[3,128,512]{2,1,0:T(8,128)(2,1)S(1)}, bf16[3,128,512]{2,1,0:T(8,128)(2,1)S(1)}, u32[]{:S(2)}, u32[]{:S(2)}) collective-permute-start(bf16[3,128,512]{2,1,0:T(8,128)(2,1)S(1)} %join.2.refs_0_), channel_id=1, source_target_pairs={{10,14},{11,15},{26,30},{27,31}} | collective-permute-start | bytes 1179656 | tf_op jit(solution)/shard_map/ppermute | solution.py:283
  10.4 9.3 %collective-permute-start.3 = (bf16[3,128,512]{2,1,0:T(8,128)(2,1)S(1)}, bf16[3,128,512]{2,1,0:T(8,128)(2,1)S(1)}, u32[]{:S(2)}, u32[]{:S(2)}) collective-permute-start(bf16[3,128,512]{2,1,0:T(8,128)(2,1)S(1)} %join.2.refs_0_), channel_id=1, source_target_pairs={{6,14},{7,15},{22,30},{23,31}} | collective-permute-start | bytes 1179656 | tf_op jit(solution)/shard_map/ppermute | solution.py:283
  11.1 14.3 %collective-permute-start.4 = (bf16[3,128,512]{2,1,0:T(8,128)(2,1)S(1)}, bf16[3,128,512]{2,1,0:T(8,128)(2,1)S(1)}, u32[]{:S(2)}, u32[]{:S(2)}) collective-permute-start(bf16[3,128,512]{2,1,0:T(8,128)(2,1)S(1)} %join.2.refs_0_), channel_id=1, source_target_pairs={{2,14},{3,15},{18,30},{19,31}} | collective-permute-start | bytes 1179656 | tf_op jit(solution)/shard_map/ppermute | solution.py:283
  19.6 35.0 %collective-permute-start = (bf16[3,384,512]{2,1,0:T(8,128)(2,1)S(1)}, bf16[3,384,512]{2,1,0:T(8,128)(2,1)S(1)}, u32[]{:S(2)}, u32[]{:S(2)}) collective-permute-start(bf16[3,384,512]{2,1,0:T(8,128)(2,1)S(1)} %shard_map.65), channel_id=1, source_target_pairs={{0,15},{1,0},{2,1},{3,2},{4,3},{5,4},{6,5},{7,6},{8,7},{9,8},{10,9... | collective-permute-start | bytes 3538952 | tf_op jit(solution)/shard_map/ppermute | solution.py:283
  26.6 41.3 %collective-permute-start.5 = (bf16[3,512,512]{2,1,0:T(8,128)(2,1)}, bf16[3,512,512]{2,1,0:T(8,128)(2,1)}, u32[]{:S(2)}, u32[]{:S(2)}) collective-permute-start(bf16[3,512,512]{2,1,0:T(8,128)(2,1)} %join.3.refs_1_), channel_id=1, source_target_pairs={{14,15},{15,14},{30,31},{31,30}} | collective-permute-start | bytes 4718600 | tf_op jit(solution)/shard_map/ppermute | solution.py:283
  30.7 26.3 %copy-start.4 = (bf16[1,4,384]{2,1,0:T(4,128)(2,1)S(1)}, bf16[1,4,384]{2,1,0:T(4,128)(2,1)}, u32[]{:S(2)}) copy-start(bf16[1,4,384]{2,1,0:T(4,128)(2,1)} %r_hbm.5) | copy-start | bytes 9220
  30.8 47.1 %collective-permute-start.7 = (bf16[3,384,512]{2,1,0:T(8,128)(2,1)}, bf16[3,384,512]{2,1,0:T(8,128)(2,1)}, u32[]{:S(2)}, u32[]{:S(2)}) collective-permute-start(bf16[3,384,512]{2,1,0:T(8,128)(2,1)} %shard_map.67), channel_id=1, source_target_pairs={{0,14},{1,15},{2,0},{3,1},{4,2},{5,3},{6,4},{7,5},{8,6},{9,7},{10,... | collective-permute-start | bytes 3538952 | tf_op jit(solution)/shard_map/ppermute | solution.py:283
  33.5 56.8 %collective-permute-start.9 = (bf16[3,384,512]{2,1,0:T(8,128)(2,1)}, bf16[3,384,512]{2,1,0:T(8,128)(2,1)}, u32[]{:S(2)}, u32[]{:S(2)}) collective-permute-start(bf16[3,384,512]{2,1,0:T(8,128)(2,1)} %get-tuple-element.19), channel_id=1, source_target_pairs={{0,15},{16,31}} | collective-permute-start | bytes 3538952 | tf_op jit(solution)/shard_map/ppermute | solution.py:283
  35.2 57.9 %collective-permute-start.12 = (bf16[3,384,512]{2,1,0:T(8,128)(2,1)}, bf16[3,384,512]{2,1,0:T(8,128)(2,1)}, u32[]{:S(2)}, u32[]{:S(2)}) collective-permute-start(bf16[3,384,512]{2,1,0:T(8,128)(2,1)} %get-tuple-element.19), channel_id=1, source_target_pairs={{1,14},{2,15},{17,30},{18,31}} | collective-permute-start | bytes 3538952 | tf_op jit(solution)/shard_map/ppermute | solution.py:283
  54.7 1.0 copy-start.1
  55.7 36.4 %collective-permute-start.13 = (bf16[2,384,512]{2,1,0:T(8,128)(2,1)}, bf16[2,384,512]{2,1,0:T(8,128)(2,1)}, u32[]{:S(2)}, u32[]{:S(2)}) collective-permute-start(bf16[2,384,512]{2,1,0:T(8,128)(2,1)} %get-tuple-element.21), channel_id=1, source_target_pairs={{3,0},{4,1},{5,2},{6,3},{7,4},{8,5},{9,6},{10,7},{11,8},{12,9},{13... | collective-permute-start | bytes 2359304 | tf_op jit(solution)/shard_map/ppermute | solution.py:283
  57.1 1.9 %copy-start = (bf16[1,3,1024,512]{3,2,1,0:T(8,128)(2,1)S(1)}, bf16[1,3,1024,512]{3,2,1,0:T(8,128)(2,1)}, u32[]{:S(2)}) copy-start(bf16[1,3,1024,512]{3,2,1,0:T(8,128)(2,1)} %refs_4_.1) | copy-start | bytes 9437188
  59.0 10.5 %copy-start.2 = (bf16[3,384,512]{2,1,0:T(8,128)(2,1)S(1)}, bf16[3,384,512]{2,1,0:T(8,128)(2,1)}, u32[]{:S(2)}) copy-start(bf16[3,384,512]{2,1,0:T(8,128)(2,1)} %copy-done.1) | copy-start | bytes 3538948
  67.9 31.6 %collective-permute-start.11 = (bf16[384,512]{1,0:T(8,128)(2,1)}, bf16[384,512]{1,0:T(8,128)(2,1)S(1)}, u32[]{:S(2)}, u32[]{:S(2)}) collective-permute-start(bf16[384,512]{1,0:T(8,128)(2,1)} %get-tuple-element.20), channel_id=1, source_target_pairs={{3,0},{4,1},{5,2},{6,3},{7,4},{8,5},{9,6},{10,7},{11,8},{12,9},{13... | collective-permute-start | bytes 1179656 | tf_op jit(solution)/shard_map/ppermute | solution.py:283
  77.9 28.5 %collective-permute-start.6 = (bf16[384,512]{1,0:T(8,128)(2,1)}, bf16[384,512]{1,0:T(8,128)(2,1)}, u32[]{:S(2)}, u32[]{:S(2)}) collective-permute-start(bf16[384,512]{1,0:T(8,128)(2,1)} %get-tuple-element.16), channel_id=1, source_target_pairs={{0,1},{1,2},{2,3},{3,4},{4,5},{5,6},{6,7},{7,8},{8,9},{9,10},{10,1... | collective-permute-start | bytes 1179656 | tf_op jit(solution)/shard_map/ppermute | solution.py:283
  90.3 17.8 %collective-permute-start.8 = (bf16[384,512]{1,0:T(8,128)(2,1)}, bf16[384,512]{1,0:T(8,128)(2,1)}, u32[]{:S(2)}, u32[]{:S(2)}) collective-permute-start(bf16[384,512]{1,0:T(8,128)(2,1)} %get-tuple-element.18), channel_id=1, source_target_pairs={{0,2},{1,3},{2,4},{3,5},{4,6},{5,7},{6,8},{7,9},{8,10},{9,11},{10,... | collective-permute-start | bytes 1179656 | tf_op jit(solution)/shard_map/ppermute | solution.py:283
  92.1 17.8 %collective-permute-start.10 = (bf16[384,512]{1,0:T(8,128)(2,1)S(1)}, bf16[384,512]{1,0:T(8,128)(2,1)S(1)}, u32[]{:S(2)}, u32[]{:S(2)}) collective-permute-start(bf16[384,512]{1,0:T(8,128)(2,1)S(1)} %shard_map.70), channel_id=1, source_target_pairs={{15,0},{31,16}} | collective-permute-start | bytes 1179656 | tf_op jit(solution)/shard_map/ppermute | solution.py:283
  101.9 30.0 %collective-permute-start.14 = (bf16[384,512]{1,0:T(8,128)(2,1)S(1)}, bf16[384,512]{1,0:T(8,128)(2,1)S(1)}, u32[]{:S(2)}, u32[]{:S(2)}) collective-permute-start(bf16[384,512]{1,0:T(8,128)(2,1)S(1)} %serve.1), channel_id=1, source_target_pairs={{0,3},{1,4},{2,5},{3,6},{4,7},{5,8},{6,9},{7,10},{8,11},{9,12},{10... | collective-permute-start | bytes 1179656 | tf_op jit(solution)/shard_map/ppermute | solution.py:283

commit v10 on v8

--- a/solution.py
+++ b/solution.py
@@ -157,13 +157,13 @@
     tokens = take(4 if tick == 0 else 1)
     pieces = take(n_pieces)
     if tick == EXTRA:
-        ans_out, new_ref, tok, acc, ans, sems = refs
+        ans_out, new_ref, tok, acc, _, sems = refs
 
         @pl.when(flags_ref[0] != 0)
         def _():
             unit_steps(
                 tick, block, flags_ref, tokens, pieces, new_ref, new_ref, ans_out, tok,
-                acc, ans, sems,
+                acc, ans_out, sems,
             )
     else:
         unit_steps(tick, block, flags_ref, tokens, pieces, *refs)
@@ -181,20 +181,20 @@
     loads = [pltpu.make_async_copy(sources[i], tok.at[i], sems.at[i]) for i in range(3)]
     for load in loads:
         load.start()
+    brought = []
     if pieces:
+        rows = 0
+        for n, piece in enumerate(pieces):
+            height = piece.shape[1]
+            part = new_ref.at[:, pl.ds(rows, height)]
+            copy = pltpu.make_async_copy(piece, part, sems.at[4 + n])
+            brought.append((rows // block, copy))
+            rows += height
+
         @pl.when(flags_ref[max(tick, 0)] != 0)
         def _():
-            rows = 0
-            copies = []
-            for n, piece in enumerate(pieces):
-                height = piece.shape[1]
-                part = new_ref.at[:, pl.ds(rows, height)]
-                copies.append(pltpu.make_async_copy(piece, part, sems.at[4 + n]))
-                rows += height
-            for copy in copies:
+            for _, copy in brought:
                 copy.start()
-            for copy in copies:
-                copy.wait()
 
     loads[0].wait()
     loads[1].wait()
@@ -202,21 +202,28 @@
         tok[1] = scaled_values(tokens[3][0, 0:1, :], tok[1])
     count = new_ref.shape[1] // block
 
-    def one(rows, first, last):
+    for j in range(count):
+        rows = pl.ds(j * block, block)
+        due = [copy for at, copy in brought if at == j]
+        if due:
+            @pl.when(flags_ref[max(tick, 0)] != 0)
+            def _():
+                for copy in due:
+                    copy.wait()
+
         new = advance_rows(tok[0], tok[1], state[0, rows], state[1, rows], state[2, rows])
         for i in range(3):
             new_ref[i, rows] = new[i]
-        if first:
+        if j == 0:
             loads[2].wait()
         part = serve_rows(tok[2], new_ref[0, rows], new_ref[1, rows], new_ref[2, rows])
-        total = part if first else acc[...] + part
-        if last:
+        total = part if j == 0 else acc[...] + part
+        if j == count - 1:
             ans[...] = total.astype(bf16)
         else:
             acc[...] = total
-
-    for j in range(count):
-        one(pl.ds(j * block, block), j == 0, j == count - 1)
+    if tick == EXTRA:
+        return
     out = pltpu.make_async_copy(ans, ans_out.at[0, 0] if tick == 0 else ans_out, sems.at[3])
     out.start()
     out.wait()
@@ -241,7 +248,7 @@
     return pl.pallas_call(
         functools.partial(unit_kernel, tick, len(pieces), block),
         in_specs=[SMEM] + token_specs + [HBM] * len(pieces) + [VMEM] * len(states),
-        out_specs=[VMEM] * len(states) + [HBM],
+        out_specs=[VMEM] * len(states) + [VMEM if tick == EXTRA else HBM],
         out_shape=state_shapes
         + [jax.ShapeDtypeStruct(tokens[0].shape if tick == 0 else (span, width), bf16)],
         input_output_aliases=aliases,

time: 145 us -> 144 us (level)
  the two profiles are of different devices: /device:TPU:4 before, /device:TPU:6 now
where the time goes in v10:
time: 144 us
  starting transfers between devices  52.7 us (37%)
  Pallas kernels  44.3 us (31%)
  waiting for transfers between devices  39.4 us (27%)
  local copies, waits for them, and re-layouts  6.36 us (4%)
    ppermute x14, starting transfers between devices, send(): return lax.ppermute(value, 'seq', pairs)  52.7 us
    ppermute x14, waiting for transfers between devices, send(): return lax.ppermute(value, 'seq', pairs)  39.4 us
    pallas_call x4, Pallas kernels, unit(): pl.pallas_call(functools.partial(unit_kernel, tick, len(pieces), block),...  28.1 us
    pallas_call x3, Pallas kernels, pack(): pl.pallas_call(functools.partial(pack_kernel, tick, split), in_specs=[HBM...  7.15 us
    pallas_call x1, Pallas kernels, advance_only(): pl.pallas_call(functools.partial(advance_kernel, block), in_specs=[HBM, V...  6 us
    dynamic_update_slice x2, local copies, waits for them, and re-layouts, body(): out = lax.dynamic_update_slice(out, back[t - 1][None, None], (0, t, 0, 0))  3.54 us
  transfers between devices with their start and end apart: 14, of which 3 were waited for; matrix products, arithmetic and copies ran while one was open for 3% of the time, Pallas kernels for 30%

profile of v10, /device:TPU:6, one launch (start us, length us, event | category | flops | bytes accessed | tf_op | source)
XLA Modules:
  0.0 143.9 jit_solution(13004913094141688177)
XLA Ops:
  0.0 1.3 collective-permute-start.1
  1.3 7.4 %collective-permute-done.1.refs_1_ = bf16[3,64,512]{2,1,0:T(8,128)(2,1)S(1)} collective-permute-done((bf16[3,64,512]{2,1,0:T(8,128)(2,1)}, bf16[3,64,512]{2,1,0:T(8,128)(2,1)S(1)}, u32[]{:S(2)}, u32[]{:S(2)}) %collective-permute-start.1) | collective-permute-done | bytes 196640 | tf_op jit(solution)/shard_map/ppermute | solution.py:280
  8.7 0.0 copy-start.1
  8.7 0.9 copy-done.1
  9.7 0.7 collective-permute-start.2
  10.4 0.7 collective-permute-start.3
  11.1 6.7 %collective-permute-start.4 = (bf16[3,128,512]{2,1,0:T(8,128)(2,1)S(1)}, bf16[3,128,512]{2,1,0:T(8,128)(2,1)S(1)}, u32[]{:S(2)}, u32[]{:S(2)}) collective-permute-start(bf16[3,128,512]{2,1,0:T(8,128)(2,1)S(1)} %join.2.refs_0_), channel_id=1, source_target_pairs={{2,14},{3,15},{18,30},{19,31}} | collective-permute-start | bytes 1179656 | tf_op jit(solution)/shard_map/ppermute | solution.py:280
  17.8 0.0 collective-permute-done.2.refs_1_
  17.8 0.0 collective-permute-done.3.refs_2_
  17.9 7.5 %collective-permute-done.4.refs_3_ = bf16[3,128,512]{2,1,0:T(8,128)(2,1)S(1)} collective-permute-done((bf16[3,128,512]{2,1,0:T(8,128)(2,1)S(1)}, bf16[3,128,512]{2,1,0:T(8,128)(2,1)S(1)}, u32[]{:S(2)}, u32[]{:S(2)}) %collective-permute-start.4) | collective-permute-done | bytes 393248 | tf_op jit(solution)/shard_map/ppermute | solution.py:280
  25.4 1.3 join.3.refs_1_
  26.6 1.8 %collective-permute-start.5 = (bf16[3,512,512]{2,1,0:T(8,128)(2,1)}, bf16[3,512,512]{2,1,0:T(8,128)(2,1)}, u32[]{:S(2)}, u32[]{:S(2)}) collective-permute-start(bf16[3,512,512]{2,1,0:T(8,128)(2,1)} %join.3.refs_1_), channel_id=1, source_target_pairs={{14,15},{15,14},{30,31},{31,30}} | collective-permute-start | bytes 4718600 | tf_op jit(solution)/shard_map/ppermute | solution.py:280
  28.4 2.2 %shard_map.65 = bf16[3,384,512]{2,1,0:T(8,128)(2,1)} custom-call(bf16[1,4,384,512]{3,2,1,0:T(8,128)(2,1)} %k_ref.5, bf16[1,4,384,512]{3,2,1,0:T(8,128)(2,1)} %v_ref.5, bf16[1,4,384,512]{3,2,1,0:T(8,128)(2,1)} %q_ref.5, bf16[1,4,384]{2,1,0:T(4,128)(2,1)} %r_hbm.5), custom_call_target="tpu_custom_call" | custom-call | tf_op jit(solution)/shard_map/pallas_call | solution.py:86
  30.7 0.1 collective-permute-start
  30.7 2.3 %shard_map.67 = bf16[3,384,512]{2,1,0:T(8,128)(2,1)} custom-call(bf16[1,4,384,512]{3,2,1,0:T(8,128)(2,1)} %k_ref.5, bf16[1,4,384,512]{3,2,1,0:T(8,128)(2,1)} %v_ref.5, bf16[1,4,384,512]{3,2,1,0:T(8,128)(2,1)} %q_ref.5, bf16[1,4,384]{2,1,0:T(4,128)(2,1)} %r_hbm.5), custom_call_target="tpu_custom_call" | custom-call | tf_op jit(solution)/shard_map/pallas_call | solution.py:86
  33.0 0.0 copy-start.2
  33.0 18.4 %collective-permute-start.7 = (bf16[3,384,512]{2,1,0:T(8,128)(2,1)}, bf16[3,384,512]{2,1,0:T(8,128)(2,1)}, u32[]{:S(2)}, u32[]{:S(2)}) collective-permute-start(bf16[3,384,512]{2,1,0:T(8,128)(2,1)} %shard_map.67), channel_id=1, source_target_pairs={{0,14},{1,15},{2,0},{3,1},{4,2},{5,3},{6,4},{7,5},{8,6},{9,7},{10,... | collective-permute-start | bytes 3538952 | tf_op jit(solution)/shard_map/ppermute | solution.py:280
  51.5 2.6 %shard_map.69 = (bf16[3,384,512]{2,1,0:T(8,128)(2,1)}, bf16[2,384,512]{2,1,0:T(8,128)(2,1)}, bf16[384,512]{1,0:T(8,128)(2,1)}) custom-call(bf16[1,4,384,512]{3,2,1,0:T(8,128)(2,1)} %k_ref.5, bf16[1,4,384,512]{3,2,1,0:T(8,128)(2,1)} %v_ref.5, bf16[1,4,384,512]{3,2,1,0:T(8,128)(2,1)} %q_ref.5, bf16[1,4,384]{2,1,0:T(4,128)(2,1)} %r_hbm.5), custom_call_target="tpu_custom_call" | custom-call | tf_op jit(solution)/shard_map/pallas_call | solution.py:86
  54.1 1.7 %collective-permute-start.9 = (bf16[3,384,512]{2,1,0:T(8,128)(2,1)}, bf16[3,384,512]{2,1,0:T(8,128)(2,1)}, u32[]{:S(2)}, u32[]{:S(2)}) collective-permute-start(bf16[3,384,512]{2,1,0:T(8,128)(2,1)} %get-tuple-element.19), channel_id=1, source_target_pairs={{0,15},{16,31}} | collective-permute-start | bytes 3538952 | tf_op jit(solution)/shard_map/ppermute | solution.py:280
  55.8 1.9 %collective-permute-start.12 = (bf16[2,384,512]{2,1,0:T(8,128)(2,1)}, bf16[2,384,512]{2,1,0:T(8,128)(2,1)}, u32[]{:S(2)}, u32[]{:S(2)}) collective-permute-start(bf16[2,384,512]{2,1,0:T(8,128)(2,1)} %get-tuple-element.21), channel_id=1, source_target_pairs={{1,14},{2,15},{3,0},{4,1},{5,2},{6,3},{7,4},{8,5},{9,6},{10,7},{11... | collective-permute-start | bytes 2359304 | tf_op jit(solution)/shard_map/ppermute | solution.py:280
  57.8 0.1 add_convert_fusion.flags_ref
  57.8 0.0 copy-done.2
  57.9 0.0 copy-start
  57.9 1.9 %copy-done = bf16[1,3,1024,512]{3,2,1,0:T(8,128)(2,1)S(1)} copy-done((bf16[1,3,1024,512]{3,2,1,0:T(8,128)(2,1)S(1)}, bf16[1,3,1024,512]{3,2,1,0:T(8,128)(2,1)}, u32[]{:S(2)}) %copy-start) | copy-done | bytes 3145752
  59.7 9.0 %shard_map.64 = (bf16[3,1024,512]{2,1,0:T(8,128)(2,1)S(1)}, bf16[1,4,384,512]{3,2,1,0:T(8,128)(2,1)}) custom-call(s32[4]{0:T(128)S(1)} %add_convert_fusion.flags_ref, bf16[1,4,384,512]{3,2,1,0:T(8,128)(2,1)} %k_ref.5, bf16[1,4,384,512]{3,2,1,0:T(8,128)(2,1)} %v_ref.5, bf16[1,4,384,512]{3,2,1,0:T(8,128)(2,1)} %q_ref.5, bf16[1,4,384]{2,1,0:T(4,128)(2,1)S(1)} %copy-done.2, ...), custom_call_target="tpu_custom_call" | custom-call | tf_op jit(solution)/shard_map/pallas_call | solution.py:248
  68.7 0.0 collective-permute-done.refs_0_
  68.7 10.5 %collective-permute-start.11 = (bf16[384,512]{1,0:T(8,128)(2,1)}, bf16[384,512]{1,0:T(8,128)(2,1)S(1)}, u32[]{:S(2)}, u32[]{:S(2)}) collective-permute-start(bf16[384,512]{1,0:T(8,128)(2,1)} %get-tuple-element.20), channel_id=1, source_target_pairs={{1,14},{2,15},{3,0},{4,1},{5,2},{6,3},{7,4},{8,5},{9,6},{10,7},{11... | collective-permute-start | bytes 1179656 | tf_op jit(solution)/shard_map/ppermute | solution.py:280
  79.2 0.0 collective-permute-done.5.refs_2_
  79.2 9.2 %shard_map.66 = (bf16[3,1024,512]{2,1,0:T(8,128)(2,1)S(1)}, bf16[384,512]{1,0:T(8,128)(2,1)}) custom-call(s32[4]{0:T(128)S(1)} %add_convert_fusion.flags_ref, bf16[3,384,512]{2,1,0:T(8,128)(2,1)} %collective-permute-done.refs_0_, bf16[3,512,512]{2,1,0:T(8,128)(2,1)} %join.3.refs_1_, ...), custom_call_target="tpu_custom_call", output_to_operand_aliasing={{0}: (4, {})} | custom-call | tf_op jit(solution)/shard_map/pallas_call | solution.py:248
  88.4 0.3 collective-permute-start.6
  88.7 0.0 collective-permute-done.7.refs_0_
  88.7 9.1 %shard_map.68 = (bf16[3,1024,512]{2,1,0:T(8,128)(2,1)S(1)}, bf16[384,512]{1,0:T(8,128)(2,1)}) custom-call(s32[4]{0:T(128)S(1)} %add_convert_fusion.flags_ref, bf16[3,384,512]{2,1,0:T(8,128)(2,1)} %collective-permute-done.7.refs_0_, bf16[3,512,512]{2,1,0:T(8,128)(2,1)} %join.3.refs_1_, ...), custom_call_target="tpu_custom_call", output_to_operand_aliasing={{0}: (4, {})} | custom-call | tf_op jit(solution)/shard_map/pallas_call | solution.py:248
  97.9 5.7 %collective-permute-start.8 = (bf16[384,512]{1,0:T(8,128)(2,1)}, bf16[384,512]{1,0:T(8,128)(2,1)}, u32[]{:S(2)}, u32[]{:S(2)}) collective-permute-start(bf16[384,512]{1,0:T(8,128)(2,1)} %get-tuple-element.18), channel_id=1, source_target_pairs={{0,2},{1,3},{2,4},{3,5},{4,6},{5,7},{6,8},{7,9},{8,10},{9,11},{10,... | collective-permute-start | bytes 1179656 | tf_op jit(solution)/shard_map/ppermute | solution.py:280
  103.5 0.0 collective-permute-done.9.refs_0_
  103.6 0.9 shard_map.70
  104.4 1.0 collective-permute-start.10
  105.4 0.0 collective-permute-done.12.tokens_ref
  105.4 6.0 %advance.1.state_ref = bf16[3,1024,512]{2,1,0:T(8,128)(2,1)S(1)} custom-call(bf16[2,384,512]{2,1,0:T(8,128)(2,1)} %collective-permute-done.12.tokens_ref, bf16[3,1024,512]{2,1,0:T(8,128)(2,1)S(1)} %keep.1.state_ref), custom_call_target="tpu_custom_call", output_to_operand_aliasing={{}: (1, {})} | custom-call | tf_op jit(solution)/shard_map/advance/pallas_call | solution.py:357
  111.4 0.0 collective-permute-done.11.queries_ref
  111.5 1.7 %serve.1 = bf16[384,512]{1,0:T(8,128)(2,1)S(1)} custom-call(bf16[384,512]{1,0:T(8,128)(2,1)S(1)} %collective-permute-done.11.queries_ref, bf16[3,1024,512]{2,1,0:T(8,128)(2,1)S(1)} %advance.1.state_ref), custom_call_target="tpu_custom_call" | custom-call | tf_op jit(solution)/shard_map/serve/pallas_call | solution.py:388
  113.2 1.9 %collective-permute-start.13 = (bf16[384,512]{1,0:T(8,128)(2,1)S(1)}, bf16[384,512]{1,0:T(8,128)(2,1)S(1)}, u32[]{:S(2)}, u32[]{:S(2)}) collective-permute-start(bf16[384,512]{1,0:T(8,128)(2,1)S(1)} %serve.1), channel_id=1, source_target_pairs={{0,3},{1,4},{2,5},{3,6},{4,7},{5,8},{6,9},{7,10},{8,11},{9,12},{10... | collective-permute-start | bytes 1179656 | tf_op jit(solution)/shard_map/ppermute | solution.py:280
  115.1 0.0 collective-permute-done.6
  115.1 1.8 %bitcast_dynamic-update-slice_fusion.2 = bf16[1,4,384,512]{3,2,1,0:T(8,128)(2,1)} fusion(bf16[1,4,384,512]{3,2,1,0:T(8,128)(2,1)} %get-tuple-element.14, bf16[384,512]{1,0:T(8,128)(2,1)} %collective-permute-done.6), kind=kLoop, calls=%fused_computation.2 | loop fusion | bytes 786432 | tf_op jit(solution)/shard_map/dynamic_update_slice | solution.py:334
  116.9 0.0 collective-permute-done.8
  116.9 1.8 %bitcast_dynamic-update-slice_fusion.1 = bf16[1,4,384,512]{3,2,1,0:T(8,128)(2,1)} fusion(bf16[1,4,384,512]{3,2,1,0:T(8,128)(2,1)} %bitcast_dynamic-update-slice_fusion.2, bf16[384,512]{1,0:T(8,128)(2,1)} %collective-permute-done.8), kind=kLoop, calls=%fused_computation.1 | loop fusion | bytes 786432 | tf_op jit(solution)/shard_map/dynamic_update_slice | solution.py:334
  118.7 0.0 collective-permute-done.10
  118.7 24.4 %collective-permute-done.13 = bf16[384,512]{1,0:T(8,128)(2,1)S(1)} collective-permute-done((bf16[384,512]{1,0:T(8,128)(2,1)S(1)}, bf16[384,512]{1,0:T(8,128)(2,1)S(1)}, u32[]{:S(2)}, u32[]{:S(2)}) %collective-permute-start.13) | collective-permute-done | bytes 393248 | tf_op jit(solution)/shard_map/ppermute | solution.py:280
  143.1 0.8 bitcast_dynamic-update-slice_fusion
  (2 shorter events, 0.0 us)
Async XLA Ops:
  0.0 8.7 %collective-permute-start.1 = (bf16[3,64,512]{2,1,0:T(8,128)(2,1)}, bf16[3,64,512]{2,1,0:T(8,128)(2,1)S(1)}, u32[]{:S(2)}, u32[]{:S(2)}) collective-permute-start(bf16[3,64,512]{2,1,0:T(8,128)(2,1)} %refs_0_.3), channel_id=1, source_target_pairs={{0,2},{1,3},{4,6},{5,7},{8,10},{9,11},{12,14},{13,15},{16,18},{17,... | collective-permute-start | bytes 589832 | tf_op jit(solution)/shard_map/ppermute | solution.py:280
  8.7 0.9 copy-start.1
  9.7 8.1 %collective-permute-start.2 = (bf16[3,128,512]{2,1,0:T(8,128)(2,1)S(1)}, bf16[3,128,512]{2,1,0:T(8,128)(2,1)S(1)}, u32[]{:S(2)}, u32[]{:S(2)}) collective-permute-start(bf16[3,128,512]{2,1,0:T(8,128)(2,1)S(1)} %join.2.refs_0_), channel_id=1, source_target_pairs={{10,14},{11,15},{26,30},{27,31}} | collective-permute-start | bytes 1179656 | tf_op jit(solution)/shard_map/ppermute | solution.py:280
  10.4 7.5 %collective-permute-start.3 = (bf16[3,128,512]{2,1,0:T(8,128)(2,1)S(1)}, bf16[3,128,512]{2,1,0:T(8,128)(2,1)S(1)}, u32[]{:S(2)}, u32[]{:S(2)}) collective-permute-start(bf16[3,128,512]{2,1,0:T(8,128)(2,1)S(1)} %join.2.refs_0_), channel_id=1, source_target_pairs={{6,14},{7,15},{22,30},{23,31}} | collective-permute-start | bytes 1179656 | tf_op jit(solution)/shard_map/ppermute | solution.py:280
  11.1 14.3 %collective-permute-start.4 = (bf16[3,128,512]{2,1,0:T(8,128)(2,1)S(1)}, bf16[3,128,512]{2,1,0:T(8,128)(2,1)S(1)}, u32[]{:S(2)}, u32[]{:S(2)}) collective-permute-start(bf16[3,128,512]{2,1,0:T(8,128)(2,1)S(1)} %join.2.refs_0_), channel_id=1, source_target_pairs={{2,14},{3,15},{18,30},{19,31}} | collective-permute-start | bytes 1179656 | tf_op jit(solution)/shard_map/ppermute | solution.py:280
  26.6 52.6 %collective-permute-start.5 = (bf16[3,512,512]{2,1,0:T(8,128)(2,1)}, bf16[3,512,512]{2,1,0:T(8,128)(2,1)}, u32[]{:S(2)}, u32[]{:S(2)}) collective-permute-start(bf16[3,512,512]{2,1,0:T(8,128)(2,1)} %join.3.refs_1_), channel_id=1, source_target_pairs={{14,15},{15,14},{30,31},{31,30}} | collective-permute-start | bytes 4718600 | tf_op jit(solution)/shard_map/ppermute | solution.py:280
  30.7 38.1 %collective-permute-start = (bf16[3,384,512]{2,1,0:T(8,128)(2,1)}, bf16[3,384,512]{2,1,0:T(8,128)(2,1)}, u32[]{:S(2)}, u32[]{:S(2)}) collective-permute-start(bf16[3,384,512]{2,1,0:T(8,128)(2,1)} %shard_map.65), channel_id=1, source_target_pairs={{0,15},{1,0},{2,1},{3,2},{4,3},{5,4},{6,5},{7,6},{8,7},{9,8},{10,9... | collective-permute-start | bytes 3538952 | tf_op jit(solution)/shard_map/ppermute | solution.py:280
  33.0 24.8 %copy-start.2 = (bf16[1,4,384]{2,1,0:T(4,128)(2,1)S(1)}, bf16[1,4,384]{2,1,0:T(4,128)(2,1)}, u32[]{:S(2)}) copy-start(bf16[1,4,384]{2,1,0:T(4,128)(2,1)} %r_hbm.5) | copy-start | bytes 9220
  33.0 55.7 %collective-permute-start.7 = (bf16[3,384,512]{2,1,0:T(8,128)(2,1)}, bf16[3,384,512]{2,1,0:T(8,128)(2,1)}, u32[]{:S(2)}, u32[]{:S(2)}) collective-permute-start(bf16[3,384,512]{2,1,0:T(8,128)(2,1)} %shard_map.67), channel_id=1, source_target_pairs={{0,14},{1,15},{2,0},{3,1},{4,2},{5,3},{6,4},{7,5},{8,6},{9,7},{10,... | collective-permute-start | bytes 3538952 | tf_op jit(solution)/shard_map/ppermute | solution.py:280
  54.1 49.4 %collective-permute-start.9 = (bf16[3,384,512]{2,1,0:T(8,128)(2,1)}, bf16[3,384,512]{2,1,0:T(8,128)(2,1)}, u32[]{:S(2)}, u32[]{:S(2)}) collective-permute-start(bf16[3,384,512]{2,1,0:T(8,128)(2,1)} %get-tuple-element.19), channel_id=1, source_target_pairs={{0,15},{16,31}} | collective-permute-start | bytes 3538952 | tf_op jit(solution)/shard_map/ppermute | solution.py:280
  55.8 49.6 %collective-permute-start.12 = (bf16[2,384,512]{2,1,0:T(8,128)(2,1)}, bf16[2,384,512]{2,1,0:T(8,128)(2,1)}, u32[]{:S(2)}, u32[]{:S(2)}) collective-permute-start(bf16[2,384,512]{2,1,0:T(8,128)(2,1)} %get-tuple-element.21), channel_id=1, source_target_pairs={{1,14},{2,15},{3,0},{4,1},{5,2},{6,3},{7,4},{8,5},{9,6},{10,7},{11... | collective-permute-start | bytes 2359304 | tf_op jit(solution)/shard_map/ppermute | solution.py:280
  57.9 1.9 %copy-start = (bf16[1,3,1024,512]{3,2,1,0:T(8,128)(2,1)S(1)}, bf16[1,3,1024,512]{3,2,1,0:T(8,128)(2,1)}, u32[]{:S(2)}) copy-start(bf16[1,3,1024,512]{3,2,1,0:T(8,128)(2,1)} %refs_4_.1) | copy-start | bytes 9437188
  68.7 42.7 %collective-permute-start.11 = (bf16[384,512]{1,0:T(8,128)(2,1)}, bf16[384,512]{1,0:T(8,128)(2,1)S(1)}, u32[]{:S(2)}, u32[]{:S(2)}) collective-permute-start(bf16[384,512]{1,0:T(8,128)(2,1)} %get-tuple-element.20), channel_id=1, source_target_pairs={{1,14},{2,15},{3,0},{4,1},{5,2},{6,3},{7,4},{8,5},{9,6},{10,7},{11... | collective-permute-start | bytes 1179656 | tf_op jit(solution)/shard_map/ppermute | solution.py:280
  88.4 26.7 %collective-permute-start.6 = (bf16[384,512]{1,0:T(8,128)(2,1)}, bf16[384,512]{1,0:T(8,128)(2,1)}, u32[]{:S(2)}, u32[]{:S(2)}) collective-permute-start(bf16[384,512]{1,0:T(8,128)(2,1)} %get-tuple-element.16), channel_id=1, source_target_pairs={{0,1},{1,2},{2,3},{3,4},{4,5},{5,6},{6,7},{7,8},{8,9},{9,10},{10,1... | collective-permute-start | bytes 1179656 | tf_op jit(solution)/shard_map/ppermute | solution.py:280
  97.9 19.1 %collective-permute-start.8 = (bf16[384,512]{1,0:T(8,128)(2,1)}, bf16[384,512]{1,0:T(8,128)(2,1)}, u32[]{:S(2)}, u32[]{:S(2)}) collective-permute-start(bf16[384,512]{1,0:T(8,128)(2,1)} %get-tuple-element.18), channel_id=1, source_target_pairs={{0,2},{1,3},{2,4},{3,5},{4,6},{5,7},{6,8},{7,9},{8,10},{9,11},{10,... | collective-permute-start | bytes 1179656 | tf_op jit(solution)/shard_map/ppermute | solution.py:280
  104.4 14.3 %collective-permute-start.10 = (bf16[384,512]{1,0:T(8,128)(2,1)S(1)}, bf16[384,512]{1,0:T(8,128)(2,1)S(1)}, u32[]{:S(2)}, u32[]{:S(2)}) collective-permute-start(bf16[384,512]{1,0:T(8,128)(2,1)S(1)} %shard_map.70), channel_id=1, source_target_pairs={{15,0},{31,16}} | collective-permute-start | bytes 1179656 | tf_op jit(solution)/shard_map/ppermute | solution.py:280
  113.2 29.9 %collective-permute-start.13 = (bf16[384,512]{1,0:T(8,128)(2,1)S(1)}, bf16[384,512]{1,0:T(8,128)(2,1)S(1)}, u32[]{:S(2)}, u32[]{:S(2)}) collective-permute-start(bf16[384,512]{1,0:T(8,128)(2,1)S(1)} %serve.1), channel_id=1, source_target_pairs={{0,3},{1,4},{2,5},{3,6},{4,7},{5,8},{6,9},{7,10},{8,11},{9,12},{10... | collective-permute-start | bytes 1179656 | tf_op jit(solution)/shard_map/ppermute | solution.py:280
